TPU v7x, 128 devices: a whole 4x4x4 slice. The times are simulated.
128 devices in a mesh: fsdp: 4 (over y_lo, core), ctx: 32 (over z, y_hi, x).
Axes of the slice: x: 4, y: 4 (y_hi: 2, y_lo: 2; y = y_hi * 2 + y_lo), z: 4, core: 2. Of those that a mesh axis runs over, the one named last changes fastest.
Arguments:
- query_proj: bfloat16 [4, 4096, 4096], P('fsdp', 'ctx'), may hold values from -10 to 10
- key_proj: bfloat16 [4, 4096, 4096], P('fsdp', 'ctx'), may hold values from -10 to 10
- value_proj: bfloat16 [4, 4096, 4096], P('fsdp', 'ctx'), may hold values from -12 to 12
- modality: int32 [4, 4096], P('fsdp', 'ctx'), may hold values from 0 to 1, as said below
- out_weight: bfloat16 [2, 4096, 2048], P(None, ('fsdp', 'ctx')), may hold values from -0.09375 to 0.09375
- grad_projected: bfloat16 [4, 4096, 2048], P('fsdp', 'ctx'), may hold values from -6 to 6
Outputs:
- projected: bfloat16 [4, 4096, 2048], P('fsdp', 'ctx')
- grad_query: bfloat16 [4, 4096, 4096], P('fsdp', 'ctx')
- grad_key: bfloat16 [4, 4096, 4096], P('fsdp', 'ctx')
- grad_value: bfloat16 [4, 4096, 4096], P('fsdp', 'ctx')
Inputs may be any that keep to these rules, and one draw needn't show every extreme that they name: `modality`: each sequence holds exactly two image spans of 1024 positions each, one starting within the first half and lying in the first half, the other lying in the second half; all other positions are text, so exactly half of each sequence's positions are image.
All inputs are finite; a program needn't handle non-finite values.
Results may differ from a plain program's by a relative error of at most 0.012.
The roundings to bfloat16 on the way count: a program that leaves them out, or rounds other values in their place, can miss the bound.
Values may be sent and summed in bfloat16 or wider, within the bound.
No kernel may reach another device: no remote copies, remote signals or barrier semaphores. Data moves between devices by JAX's collectives and lax.ppermute only.
A program may use at most 320 MiB of HBM per device.

v0:
```python
import jax
import jax.numpy as jnp
from jax import lax
from jax.sharding import PartitionSpec as P

HEAD_SIZE = 128


def cut_along(array, dim, length):
    before, after = (array.shape[:dim], array.shape[dim + 1 :])
    return jnp.moveaxis(array.reshape(*before, length, -1, *after), dim, 0)


def edges_of(length, count):
    unit = 8 if length >= 8 * count else 1
    return [length // unit * k // count * unit for k in range(1, count)]


def in_order(blocks, dim):
    dims = list(blocks.shape[1:])
    dims[dim] *= blocks.shape[0]
    return jnp.moveaxis(blocks, 0, dim).reshape(dims)


def exchange_in_pieces(array, axis, pieces, split_dim, concat_dim):
    blocks = cut_along(array, split_dim, lax.axis_size(axis))
    widest = max(range(1, max(2, blocks.ndim - 1)), key=lambda d: blocks.shape[d])
    done = []
    for share in jnp.split(blocks, edges_of(blocks.shape[widest], pieces), axis=widest):
        if share.size:
            done.append(lax.all_to_all(share, axis, split_axis=0, concat_axis=0, tiled=True))
    return in_order(jnp.concatenate(done, axis=widest), concat_dim)


def sent_together(arrays, axis, split_dim, concat_dim, along):
    widths = [a.shape[along] for a in arrays]
    both = jnp.concatenate(arrays, axis=along)
    filled = lax.all_to_all(both, axis, split_axis=split_dim, concat_axis=concat_dim, tiled=True)
    return tuple(jnp.split(filled, [sum(widths[:k]) for k in range(1, len(widths))], axis=along))


def block_count(length):
    return max(1, min(8, length // 512))


def probabilities(query_block, key_prefix, offset):
    scaling = query_block.shape[-1] ** (-0.5)
    scores = (
        jnp.einsum("hqd,hkd->hqk", query_block, key_prefix, preferred_element_type=jnp.float32)
        * scaling
    )
    query_places = offset + jnp.arange(query_block.shape[1])
    key_places = jnp.arange(key_prefix.shape[1])
    scores = jnp.where(key_places[None, None, :] <= query_places[None, :, None], scores, -jnp.inf)
    highest = jnp.max(scores, axis=-1, keepdims=True)
    raised = jnp.exp(scores - highest)
    return raised / jnp.sum(raised, axis=-1, keepdims=True)


def attend_forward(queries, keys_all, values_all):
    length = queries.shape[1]
    block_rows = length // block_count(length)
    pieces = []
    for block_index in range(length // block_rows):
        offset = block_index * block_rows
        finish = offset + block_rows
        weights = probabilities(queries[:, offset:finish], keys_all[:, :finish], offset).astype(
            jnp.bfloat16
        )
        output = jnp.einsum(
            "hqk,hkd->hqd", weights, values_all[:, :finish], preferred_element_type=jnp.float32
        )
        pieces.append(output.astype(jnp.bfloat16))
    return jnp.concatenate(pieces, axis=1)


def attend_backward(queries, keys_all, values_all, attention, grad_attention):
    length = queries.shape[1]
    block_rows = length // block_count(length)
    scaling = queries.shape[-1] ** (-0.5)
    grad_keys = jnp.zeros(queries.shape, jnp.float32)
    grad_values = jnp.zeros(queries.shape, jnp.float32)
    query_pieces = []
    for block_index in range(length // block_rows):
        offset = block_index * block_rows
        finish = offset + block_rows
        query_block = queries[:, offset:finish]
        weights = probabilities(query_block, keys_all[:, :finish], offset)
        grad_block = grad_attention[:, offset:finish]
        attn_block = attention[:, offset:finish]
        grad_values = grad_values.at[:, :finish].add(
            jnp.einsum(
                "hqk,hqd->hkd",
                weights.astype(jnp.bfloat16),
                grad_block,
                preferred_element_type=jnp.float32,
            )
        )
        grad_weights = jnp.einsum(
            "hqd,hkd->hqk", grad_block, values_all[:, :finish], preferred_element_type=jnp.float32
        )
        row_delta = jnp.sum(
            grad_block.astype(jnp.float32) * attn_block.astype(jnp.float32), axis=-1, keepdims=True
        )
        grad_scores = (weights * (grad_weights - row_delta) * scaling).astype(jnp.bfloat16)
        query_pieces.append(
            jnp.einsum(
                "hqk,hkd->hqd",
                grad_scores,
                keys_all[:, :finish],
                preferred_element_type=jnp.float32,
            ).astype(jnp.bfloat16)
        )
        grad_keys = grad_keys.at[:, :finish].add(
            jnp.einsum("hqk,hqd->hkd", grad_scores, query_block, preferred_element_type=jnp.float32)
        )
    return (
        jnp.concatenate(query_pieces, axis=1),
        grad_keys.astype(jnp.bfloat16),
        grad_values.astype(jnp.bfloat16),
    )


def transposed_product(left, right):
    return lax.dot_general(
        left, right, (((1,), (1,)), ((), ())), preferred_element_type=jnp.float32
    )


def heads_first(flat, length, local_heads):
    return flat.reshape(length, local_heads, HEAD_SIZE).transpose(1, 0, 2)


def heads_last(stacked, length, local_width):
    return stacked.transpose(1, 0, 2).reshape(1, length, local_width)


def per_device(query_proj, key_proj, value_proj, modality, out_weight, grad_projected):
    context_size = lax.axis_size("ctx")
    row_count = query_proj.shape[1]
    inner_width = query_proj.shape[2]
    length = row_count * context_size
    local_width = inner_width // context_size
    local_heads = local_width // HEAD_SIZE
    head_query, head_key, head_value = (
        exchange_in_pieces(query_proj, "ctx", 2, 2, 1),
        exchange_in_pieces(key_proj, "ctx", 2, 2, 1),
        exchange_in_pieces(value_proj, "ctx", 2, 2, 1),
    )
    head_query = heads_first(head_query, length, local_heads)
    head_key = heads_first(head_key, length, local_heads)
    head_value = heads_first(head_value, length, local_heads)
    attention = attend_forward(head_query, head_key, head_value)
    sending = heads_last(attention, length, local_width)
    attn_rows = lax.all_to_all(sending, "ctx", split_axis=1, concat_axis=2, tiled=True)[0]
    upstream = grad_projected[0]
    weight_piece = lax.all_gather(out_weight, ("fsdp", "ctx"), axis=1, tiled=True)
    text_out = jnp.dot(attn_rows, weight_piece[0], preferred_element_type=jnp.float32)
    image_out = jnp.dot(attn_rows, weight_piece[1], preferred_element_type=jnp.float32)
    text_grad = transposed_product(upstream, weight_piece[0])
    image_grad = transposed_product(upstream, weight_piece[1])
    text_out, image_out, text_grad, image_grad = (text_out, image_out, text_grad, image_grad)
    image_rows = (modality[0] == 1)[:, None]
    projected = jnp.where(image_rows, image_out, text_out).astype(jnp.bfloat16)[None]
    grad_rows = jnp.where(image_rows, image_grad, text_grad).astype(jnp.bfloat16)
    grad_heads = lax.all_to_all(grad_rows[None], "ctx", split_axis=2, concat_axis=1, tiled=True)
    grad_heads = heads_first(grad_heads, length, local_heads)
    grad_q, grad_k, grad_v = attend_backward(
        head_query, head_key, head_value, attention, grad_heads
    )
    grad_query, grad_key, grad_value = sent_together(
        (
            heads_last(grad_q, length, local_width),
            heads_last(grad_k, length, local_width),
            heads_last(grad_v, length, local_width),
        ),
        "ctx",
        1,
        2,
        0,
    )
    return (projected, grad_query, grad_key, grad_value)


def solution(mesh):
    placed = (
        P("fsdp", "ctx", None),
        P("fsdp", "ctx", None),
        P("fsdp", "ctx", None),
        P("fsdp", "ctx"),
        P(None, ("fsdp", "ctx"), None),
        P("fsdp", "ctx", None),
    )
    return jax.shard_map(
        per_device,
        mesh=mesh,
        in_specs=placed,
        out_specs=(
            P("fsdp", "ctx", None),
            P("fsdp", "ctx", None),
            P("fsdp", "ctx", None),
            P("fsdp", "ctx", None),
        ),
        check_vma=False,
    )
```

profile of v0, /device:TPU:0, one launch (start us, length us, event | category | flops | bytes accessed | tf_op | source)
XLA Modules:
  0.0 677.0 jit_solution(4088822224911274134)
XLA Ops:
  11.0 2.3 copy.65
  13.4 10.9 %all-to-all-start.3 = ((bf16[32,1,64,128]{3,2,1,0:T(8,128)(2,1)}), bf16[32,1,64,128]{3,2,1,0:T(8,128)(2,1)S(1)}, u32[]{:S(2)}, u32[]{:S(2)}) async-start(bf16[32,1,64,128]{3,2,1,0:T(8,128)(2,1)} %copy.65), calls=%async_computation.3 | async-start | bytes 1048576 | tf_op jit(solution)/shard_map/all_to_all | solution.py:31
  25.4 14.2 %all-to-all-done.3 = bf16[32,1,64,128]{3,2,1,0:T(8,128)(2,1)S(1)} async-done(((bf16[32,1,64,128]{3,2,1,0:T(8,128)(2,1)}), bf16[32,1,64,128]{3,2,1,0:T(8,128)(2,1)S(1)}, u32[]{:S(2)}, u32[]{:S(2)}) %all-to-all-start.3) | async-done | bytes 524320 | tf_op jit(solution)/shard_map/all_to_all | solution.py:31
  39.6 4.8 all-to-all-start.2
  47.4 2.4 copy.60
  49.8 9.6 %all-to-all-done.2 = bf16[32,1,64,128]{3,2,1,0:T(8,128)(2,1)} async-done(((bf16[32,1,64,128]{3,2,1,0:T(8,128)(2,1)}), bf16[32,1,64,128]{3,2,1,0:T(8,128)(2,1)}, u32[]{:S(2)}, u32[]{:S(2)}) %all-to-all-start.2) | async-done | bytes 524320 | tf_op jit(solution)/shard_map/all_to_all | solution.py:31
  59.4 4.2 all-to-all-start.1
  64.8 12.7 %all-to-all-done.1 = bf16[32,1,64,128]{3,2,1,0:T(8,128)(2,1)S(1)} async-done(((bf16[32,1,64,128]{3,2,1,0:T(8,128)(2,1)}), bf16[32,1,64,128]{3,2,1,0:T(8,128)(2,1)S(1)}, u32[]{:S(2)}, u32[]{:S(2)}) %all-to-all-start.1) | async-done | bytes 524320 | tf_op jit(solution)/shard_map/all_to_all | solution.py:31
  78.3 5.1 all-to-all-start
  86.5 2.4 copy.70
  90.0 6.0 all-to-all-done
  96.0 4.6 all-to-all-start.5
  100.7 13.0 %all-to-all-done.5 = bf16[32,1,64,128]{3,2,1,0:T(8,128)(2,1)S(1)} async-done(((bf16[32,1,64,128]{3,2,1,0:T(8,128)(2,1)}), bf16[32,1,64,128]{3,2,1,0:T(8,128)(2,1)S(1)}, u32[]{:S(2)}, u32[]{:S(2)}) %all-to-all-start.5) | async-done | bytes 524320 | tf_op jit(solution)/shard_map/all_to_all | solution.py:31
  113.7 4.9 all-to-all-start.4
  121.9 9.4 %all-to-all-done.4 = bf16[32,1,64,128]{3,2,1,0:T(8,128)(2,1)} async-done(((bf16[32,1,64,128]{3,2,1,0:T(8,128)(2,1)}), bf16[32,1,64,128]{3,2,1,0:T(8,128)(2,1)}, u32[]{:S(2)}, u32[]{:S(2)}) %all-to-all-start.4) | async-done | bytes 524320 | tf_op jit(solution)/shard_map/all_to_all | solution.py:31
  160.2 4.0 fusion.8
  164.1 3.7 fusion.6
  167.9 4.5 fusion.4
  172.4 208.8 %all-gather.2.cloned.1.call-done = bf16[2,4096,2048]{2,1,0:T(8,128)(2,1)} async-done(((bf16[2,32,2048]{2,1,0:T(8,128)(2,1)}), bf16[2,4096,2048]{2,1,0:T(8,128)(2,1)}) %all-gather.2.cloned.1.call-update) | async-done | bytes 33554448 | tf_op jit(solution)/shard_map/all_gather | solution.py:157
  381.2 12.4 %fusion = bf16[128,4096]{1,0:T(8,128)(2,1)} fusion(bf16[2,4096,2048]{2,1,0:T(8,128)(2,1)} %all-gather.2.cloned.1.call-done, bf16[1,128,2048]{2,1,0:T(8,128)(2,1)S(1)} %copy-done), kind=kOutput, calls=%fused_computation.2 | convolution fusion | flops 2147483648 | bytes 18350080 | tf_op jit(solution)/shard_map/dot_general | solution.py:125
  393.6 11.6 %fusion.20 = bf16[1,128,4096]{2,1,0:T(8,128)(2,1)S(1)} fusion(bf16[128,4096]{1,0:T(8,128)(2,1)} %fusion, bf16[2,4096,2048]{2,1,0:T(8,128)(2,1)} %all-gather.2.cloned.1.call-done, pred[128]{0:T(512)(128)(4,1)S(1)} %compare_bitcast_fusion, bf16[1,128,2048]{2,1,0:T(8,128)(2,1)S(1)} %copy-done), kind=kOutput, calls=%fused_computation.42 | convolution fusion | flops 2148007936 | bytes 19398784 | tf_op jit(solution)/shard_map/dot_general | solution.py:125
  405.2 3.9 copy.75
  409.6 23.6 %reduce.73 = bf16[4096,128]{1,0:T(8,128)(2,1)S(1)} reduce(bf16[4096,1,128]{2,1,0:T(2,128)(2,1)} %bitcast.454, bf16[]{:T(256)} %broadcast.495), dimensions={1}, to_apply=%bitcast.334.reduce_sub_computation | reduce | bytes 2097154
  434.4 9.8 %all-to-all-start.7 = ((bf16[32,2,8192]{2,1,0:T(2,128)(2,1)}), bf16[32,2,8192]{2,1,0:T(2,128)(2,1)S(1)}, u32[]{:S(2)}, u32[]{:S(2)}) async-start(bf16[32,2,8192]{2,1,0:T(2,128)(2,1)} %reshape.1112), calls=%async_computation.7 | async-start | bytes 2097152 | tf_op jit(solution)/shard_map/all_to_all | solution.py:166
  444.2 4.6 constant_dynamic-update-slice_fusion.2
  448.8 5.0 constant_dynamic-update-slice_fusion.1
  455.7 4.3 copy.86
  460.1 24.4 %reduce.72 = bf16[4096,128]{1,0:T(8,128)(2,1)} reduce(bf16[4096,1,128]{2,1,0:T(2,128)(2,1)} %bitcast.455, bf16[]{:T(256)} %broadcast.495), dimensions={1}, to_apply=%bitcast.405.reduce_sub_computation | reduce | bytes 2097154
  484.5 2.1 reshape.1110
  486.6 10.0 %all-to-all-start.6 = ((bf16[32,2,8192]{2,1,0:T(2,128)(2,1)}), bf16[32,2,8192]{2,1,0:T(2,128)(2,1)}, u32[]{:S(2)}, u32[]{:S(2)}) async-start(bf16[32,2,8192]{2,1,0:T(2,128)(2,1)} %reshape.1110), calls=%async_computation.6 | async-start | bytes 2097152 | tf_op jit(solution)/shard_map/all_to_all | solution.py:155
  496.7 3.5 reshape.1113
  500.1 2.7 copy.84
  523.2 2.1 fusion.36
  526.0 2.4 multiply_convert_fusion.3
  528.4 2.8 multiply_convert_fusion.2
  556.1 20.5 %copy.78 = bf16[3,4096,128]{2,0,1:T(4,128)(2,1)} copy(bf16[3,4096,128]{2,1,0:T(8,128)(2,1)S(1)} %pad_maximum_fusion) | data formatting | bytes 6291456 | tf_op jit(solution)/shard_map/concatenate | solution.py:37
  576.6 10.1 %all-to-all-start.8 = ((bf16[3,4096,128]{2,0,1:T(4,128)(2,1)}), bf16[3,4096,128]{2,0,1:T(4,128)(2,1)}, u32[]{:S(2)}, u32[]{:S(2)}) async-start(bf16[3,4096,128]{2,0,1:T(4,128)(2,1)} %copy.78), calls=%async_computation.8 | async-start | bytes 8388608 | tf_op jit(solution)/shard_map/all_to_all | solution.py:38
  586.8 4.3 reshape.1111
  593.8 8.1 %fusion.1 = bf16[128,2048]{1,0:T(8,128)(2,1)S(1)} fusion(bf16[128,4096]{0,1:T(8,128)(2,1)S(1)} %bitcast.493, bf16[2,4096,2048]{2,1,0:T(8,128)(2,1)} %all-gather.2.cloned.1.call-done), kind=kOutput, calls=%fused_computation.3 | convolution fusion | flops 2147483648 | bytes 18350080 | tf_op jit(solution)/shard_map/dot_general | solution.py:159
  602.0 8.9 %fusion.49 = bf16[1,128,2048]{2,1,0:T(8,128)(2,1)} fusion(bf16[128,2048]{1,0:T(8,128)(2,1)S(1)} %fusion.1, bf16[128,4096]{0,1:T(8,128)(2,1)S(1)} %bitcast.494, bf16[2,4096,2048]{2,1,0:T(8,128)(2,1)} %all-gather.2.cloned.1.call-done, pred[128]{0:T(512)(128)(4,1)S(1)} %copy-done.29), kind=kOutput, calls=%fused_computation.88 | convolution fusion | flops 2147745792 | bytes 18874496 | tf_op jit(solution)/shard_map/dot_general | solution.py:158
  610.9 32.9 %all-to-all-done.8 = bf16[3,4096,128]{2,0,1:T(4,128)(2,1)} async-done(((bf16[3,4096,128]{2,0,1:T(4,128)(2,1)}), bf16[3,4096,128]{2,0,1:T(4,128)(2,1)}, u32[]{:S(2)}, u32[]{:S(2)}) %all-to-all-start.8) | async-done | bytes 3145760 | tf_op jit(solution)/shard_map/all_to_all | solution.py:38
  643.8 10.9 %fusion.163 = (bf16[1,128,32,128]{3,0,1,2:T(2,128)(2,1)S(1)}, bf16[1,128,32,128]{3,0,1,2:T(2,128)(2,1)}, bf16[1,128,32,128]{3,0,1,2:T(2,128)(2,1)S(1)}) fusion(bf16[3,128,32,128]{3,0,1,2:T(4,128)(2,1)} %bitcast.93), kind=kLoop, calls=%fused_computation.257 | loop fusion | bytes 6291456 | tf_op jit(solution)/shard_map/split | solution.py:39
  654.6 2.2 copy.79
  656.8 2.3 split.40
  659.1 3.8 copy.80
  662.9 2.4 split.42
  665.3 2.2 copy.81
  667.5 2.3 split.44
  (172 shorter events, 98.2 us)
Async XLA Ops:
  7.2 374.0 %copy-start = (bf16[1,128,2048]{2,1,0:T(8,128)(2,1)S(1)}, bf16[1,128,2048]{2,1,0:T(8,128)(2,1)}, u32[]{:S(2)}) copy-start(bf16[1,128,2048]{2,1,0:T(8,128)(2,1)} %param.47) | copy-start | bytes 1572868
  7.2 374.0 %all-gather.2.cloned.1.call-start = ((), (), s32[]{:S(2)}) async-start(), calls=%async_computation.9 | async-start | bytes 33816576 | tf_op jit(solution)/shard_map/all_gather | solution.py:157
  13.4 26.2 %all-to-all-start.3 = ((bf16[32,1,64,128]{3,2,1,0:T(8,128)(2,1)}), bf16[32,1,64,128]{3,2,1,0:T(8,128)(2,1)S(1)}, u32[]{:S(2)}, u32[]{:S(2)}) async-start(bf16[32,1,64,128]{3,2,1,0:T(8,128)(2,1)} %copy.65), calls=%async_computation.3 | async-start | bytes 1048576 | tf_op jit(solution)/shard_map/all_to_all | solution.py:31
  39.6 19.9 %all-to-all-start.2 = ((bf16[32,1,64,128]{3,2,1,0:T(8,128)(2,1)}), bf16[32,1,64,128]{3,2,1,0:T(8,128)(2,1)}, u32[]{:S(2)}, u32[]{:S(2)}) async-start(bf16[32,1,64,128]{3,2,1,0:T(8,128)(2,1)} %copy.64), calls=%async_computation.2 | async-start | bytes 1048576 | tf_op jit(solution)/shard_map/all_to_all | solution.py:31
  59.4 18.1 %all-to-all-start.1 = ((bf16[32,1,64,128]{3,2,1,0:T(8,128)(2,1)}), bf16[32,1,64,128]{3,2,1,0:T(8,128)(2,1)S(1)}, u32[]{:S(2)}, u32[]{:S(2)}) async-start(bf16[32,1,64,128]{3,2,1,0:T(8,128)(2,1)} %copy.60), calls=%async_computation.1 | async-start | bytes 1048576 | tf_op jit(solution)/shard_map/all_to_all | solution.py:31
  78.3 17.8 %all-to-all-start = ((bf16[32,1,64,128]{3,2,1,0:T(8,128)(2,1)}), bf16[32,1,64,128]{3,2,1,0:T(8,128)(2,1)}, u32[]{:S(2)}, u32[]{:S(2)}) async-start(bf16[32,1,64,128]{3,2,1,0:T(8,128)(2,1)} %copy.59), calls=%async_computation | async-start | bytes 1048576 | tf_op jit(solution)/shard_map/all_to_all | solution.py:31
  86.5 32.2 %copy-start.27 = (s32[1,128]{1,0:T(1,128)S(1)}, s32[1,128]{1,0:T(1,128)}, u32[]{:S(2)}) copy-start(s32[1,128]{1,0:T(1,128)} %param.45) | copy-start | bytes 1540
  88.8 31.9 %copy-start.15 = (bf16[32,1,64,128]{3,2,1,0:T(8,128)(2,1)S(1)}, bf16[32,1,64,128]{3,2,1,0:T(8,128)(2,1)}, u32[]{:S(2)}) copy-start(bf16[32,1,64,128]{3,2,1,0:T(8,128)(2,1)} %copy-done.14) | copy-start | bytes 1572868
  96.0 17.7 %all-to-all-start.5 = ((bf16[32,1,64,128]{3,2,1,0:T(8,128)(2,1)}), bf16[32,1,64,128]{3,2,1,0:T(8,128)(2,1)S(1)}, u32[]{:S(2)}, u32[]{:S(2)}) async-start(bf16[32,1,64,128]{3,2,1,0:T(8,128)(2,1)} %copy.70), calls=%async_computation.5 | async-start | bytes 1048576 | tf_op jit(solution)/shard_map/all_to_all | solution.py:31
  113.7 17.6 %copy-start.16 = (bf16[32,1,64,128]{3,2,1,0:T(8,128)(2,1)}, bf16[32,1,64,128]{3,2,1,0:T(8,128)(2,1)S(1)}, u32[]{:S(2)}) copy-start(bf16[32,1,64,128]{3,2,1,0:T(8,128)(2,1)S(1)} %all-to-all-done.5) | copy-start | bytes 1572868
  113.7 17.6 %all-to-all-start.4 = ((bf16[32,1,64,128]{3,2,1,0:T(8,128)(2,1)}), bf16[32,1,64,128]{3,2,1,0:T(8,128)(2,1)}, u32[]{:S(2)}, u32[]{:S(2)}) async-start(bf16[32,1,64,128]{3,2,1,0:T(8,128)(2,1)} %copy.69), calls=%async_computation.4 | async-start | bytes 1048576 | tf_op jit(solution)/shard_map/all_to_all | solution.py:31
  118.7 274.9 %copy-start.28 = (pred[128]{0:T(512)(128)(4,1)}, pred[128]{0:T(512)(128)(4,1)S(1)}, u32[]{:S(2)}) copy-start(pred[128]{0:T(512)(128)(4,1)S(1)} %compare_bitcast_fusion) | copy-start | bytes 388
  121.9 35.0 %copy-start.7 = (bf16[32,1,128,128]{3,2,0,1:T(8,128)(2,1)}, bf16[32,1,128,128]{3,2,0,1:T(8,128)(2,1)S(1)}, u32[]{:S(2)}) copy-start(bf16[32,1,128,128]{3,2,0,1:T(8,128)(2,1)S(1)} %pad_maximum_fusion.1) | copy-start | bytes 3145732
  133.9 2.6 copy-start.9
  134.1 2.8 copy-start.19
  135.8 6.1 copy-start.12
  135.8 6.1 copy-start.23
  136.3 5.6 copy-start.25
  137.6 5.5 copy-start.10
  145.5 2.1 copy-start.3
  149.6 3.7 copy-start.2
  151.7 1.6 copy-start.18
  434.4 52.2 %all-to-all-start.7 = ((bf16[32,2,8192]{2,1,0:T(2,128)(2,1)}), bf16[32,2,8192]{2,1,0:T(2,128)(2,1)S(1)}, u32[]{:S(2)}, u32[]{:S(2)}) async-start(bf16[32,2,8192]{2,1,0:T(2,128)(2,1)} %reshape.1112), calls=%async_computation.7 | async-start | bytes 2097152 | tf_op jit(solution)/shard_map/all_to_all | solution.py:166
  444.2 9.6 %slice-start = ((s8[8388608]{0:T(1024)(128)(4,1)}), s8[4194304]{0:T(1024)(128)(4,1)S(1)}, s32[]{:S(2)}) async-start(s8[8388608]{0:T(1024)(128)(4,1)} %bitcast.406), calls=%async_computation.10 | async-start | bytes 8388608
  448.8 5.0 slice-start.1
  486.6 90.0 %all-to-all-start.6 = ((bf16[32,2,8192]{2,1,0:T(2,128)(2,1)}), bf16[32,2,8192]{2,1,0:T(2,128)(2,1)}, u32[]{:S(2)}, u32[]{:S(2)}) async-start(bf16[32,2,8192]{2,1,0:T(2,128)(2,1)} %reshape.1110), calls=%async_computation.6 | async-start | bytes 2097152 | tf_op jit(solution)/shard_map/all_to_all | solution.py:155
  505.2 3.3 copy-start.8
  508.5 2.5 copy-start.13
  508.5 2.5 copy-start.24
  508.5 2.5 copy-start.26
  511.1 1.9 copy-start.11
  511.1 5.2 slice-start.8
  513.0 2.4 copy-start.4
  513.0 3.3 slice-start.9
  513.0 4.5 slice-start.6
  515.4 2.3 slice-start.7
  516.3 2.7 slice-start.4
  517.7 2.1 slice-start.5
  528.4 4.0 slice-start.2
  531.2 2.2 slice-start.3
  533.4 1.8 copy-start.20
  534.7 1.6 copy-start.17
  537.1 2.1 copy-start.21
  538.3 2.3 copy-start.6
  541.7 1.9 copy-start.5
  576.6 67.1 %all-to-all-start.8 = ((bf16[3,4096,128]{2,0,1:T(4,128)(2,1)}), bf16[3,4096,128]{2,0,1:T(4,128)(2,1)}, u32[]{:S(2)}, u32[]{:S(2)}) async-start(bf16[3,4096,128]{2,0,1:T(4,128)(2,1)} %copy.78), calls=%async_computation.8 | async-start | bytes 8388608 | tf_op jit(solution)/shard_map/all_to_all | solution.py:38
  593.8 8.1 %copy-start.29 = (pred[128]{0:T(512)(128)(4,1)S(1)}, pred[128]{0:T(512)(128)(4,1)}, u32[]{:S(2)}) copy-start(pred[128]{0:T(512)(128)(4,1)} %copy-done.28) | copy-start | bytes 388
  662.9 6.8 %copy-start.1 = (bf16[1,128,2048]{2,1,0:T(8,128)(2,1)S(1)}, bf16[1,128,2048]{2,1,0:T(8,128)(2,1)}, u32[]{:S(2)}) copy-start(bf16[1,128,2048]{2,1,0:T(8,128)(2,1)} %param.47) | copy-start | bytes 1572868
  (2 other events, 2.1 us)
Sparse Core Ops, SparseCore 0:
  9.7 371.4 all-gather.1
where the time goes:
time: 687 us; the launch traced here: 677 us
  waiting for transfers between devices  307 us (45%)
  matrix products  112 us (16%)
  local copies, waits for them, and re-layouts  102 us (15%)
  other arithmetic  76.6 us (11%)
  starting transfers between devices  64.5 us (9%)
  between operations  15.2 us (2%)
    all_gather x1, waiting for transfers between devices, per_device(): lax.all_gather(out_weight, ('fsdp', 'ctx'), axis=1, tiled=True)  209 us
    all_to_all x6, waiting for transfers between devices, exchange_in_pieces(): lax.all_to_all(share, axis, split_axis=0, concat_axis=0, tiled=True)  65 us
    unnamed x7, other arithmetic  48 us
    all_to_all x6, starting transfers between devices, exchange_in_pieces(): lax.all_to_all(share, axis, split_axis=0, concat_axis=0, tiled=True)  34.5 us
    all_to_all x1, waiting for transfers between devices, sent_together(): lax.all_to_all(both, axis, split_axis=split_dim, concat_axis=concat_dim,...  32.9 us
    unnamed x90, local copies, waits for them, and re-layouts  28.1 us
    split x7, local copies, waits for them, and re-layouts, sent_together(): jnp.split(filled, [sum(widths[:k]) for k in range(1, len(widths))], axis=...  26 us
    dot_general x2, matrix products, transposed_product(): lax.dot_general(left, right, (((1,), (1,)), ((), ())), preferred_element_...  24 us
  transfers between devices with their start and end apart: 10, of which 8 were waited for; matrix products, arithmetic and copies ran while one was open for 30% of the time, Pallas kernels for 0%

commit v1 on v0

v1 whole, which is shorter than its diff:
```python
import functools, math
import jax, jax.numpy as jnp
from jax import lax
from jax.experimental import pallas as pl
from jax.experimental.pallas import tpu as pltpu
from jax.sharding import PartitionSpec as P

HEAD_SIZE = 128
LOG2E = math.log2(math.e)
NT = (((1,), (1,)), ((), ()))
TN = (((0,), (0,)), ((), ()))
VMEM_LIMIT = 56 * 1024 * 1024
FWD_ROWS = 1024
BWD_ROWS = 1024


def mm(a, b, dims=(((1,), (0,)), ((), ()))):
    return lax.dot_general(a, b, dims, preferred_element_type=jnp.float32)


def fwd_kernel(qkv_ref, out_ref, lse_ref, s_ref, *, rows):
    blocks, _, step, _ = qkv_ref.shape
    per = rows // step
    count = blocks // per
    factor = HEAD_SIZE**-0.5 * LOG2E

    def get(which, index):
        return qkv_ref[pl.ds(index * per, per), which].reshape(rows, HEAD_SIZE)

    def query_block(i, _):
        query = get(0, i)

        def scores(j, top):
            s = mm(query, get(1, j), NT)
            s_ref[j] = s
            for c in range(0, rows, HEAD_SIZE):
                top = jnp.maximum(top, s[:, c : c + HEAD_SIZE])
            return top

        top = lax.fori_loop(0, i, scores, jnp.full((rows, HEAD_SIZE), -jnp.inf, jnp.float32))
        s = mm(query, get(1, i), NT)
        keep = lax.broadcasted_iota(jnp.int32, s.shape, 1) <= lax.broadcasted_iota(
            jnp.int32, s.shape, 0
        )
        s = jnp.where(keep, s, -jnp.inf)
        s_ref[i] = s
        for c in range(0, rows, HEAD_SIZE):
            top = jnp.maximum(top, s[:, c : c + HEAD_SIZE])
        high = jnp.max(top, axis=1, keepdims=True) * factor

        def values(j, carry):
            total, acc = carry
            p = jnp.exp2(s_ref[j] * factor - high)
            for c in range(0, rows, HEAD_SIZE):
                total = total + p[:, c : c + HEAD_SIZE]
            return total, acc + mm(p.astype(jnp.bfloat16), get(2, j))

        zero = jnp.zeros((rows, HEAD_SIZE), jnp.float32)
        total, acc = lax.fori_loop(0, i + 1, values, (zero, zero))
        total = jnp.sum(total, axis=1, keepdims=True)
        out = (acc / total).astype(jnp.bfloat16)
        out_ref[pl.ds(i * per, per)] = out.reshape(per, step, HEAD_SIZE)
        lse = jnp.broadcast_to(high + jnp.log2(total), (rows, HEAD_SIZE))
        lse_ref[pl.ds(i, 1)] = lse.T[0:1].reshape(1, 1, rows)
        return 0

    lax.fori_loop(0, count, query_block, 0)


def attend_forward(qkv, rows=512):
    blocks, _, step, _ = qkv.shape
    length = blocks * step
    return pl.pallas_call(
        functools.partial(fwd_kernel, rows=rows),
        out_shape=(
            jax.ShapeDtypeStruct((blocks, step, HEAD_SIZE), jnp.bfloat16),
            jax.ShapeDtypeStruct((length // rows, 1, rows), jnp.float32),
        ),
        in_specs=[pl.BlockSpec(memory_space=pltpu.VMEM)],
        out_specs=[pl.BlockSpec(memory_space=pltpu.VMEM)] * 2,
        scratch_shapes=[pltpu.VMEM((length // rows, rows, rows), jnp.float32)],
        compiler_params=pltpu.CompilerParams(vmem_limit_bytes=VMEM_LIMIT),
        cost_estimate=pl.CostEstimate(
            flops=2 * length * length * HEAD_SIZE,
            bytes_accessed=8 * length * HEAD_SIZE,
            transcendentals=length * length // 2,
        ),
        name="attend_forward",
    )(qkv)


def bwd_kernel(qkv_ref, out_ref, lse_ref, grad_ref, res_ref, dq_ref, dk_ref, dv_ref, *, rows):
    blocks, _, step, _ = qkv_ref.shape
    per = rows // step
    count = blocks // per
    scale = HEAD_SIZE**-0.5
    factor = scale * LOG2E

    def get(which, index):
        return qkv_ref[pl.ds(index * per, per), which].reshape(rows, HEAD_SIZE)

    dk_ref[...] = jnp.zeros_like(dk_ref)
    dv_ref[...] = jnp.zeros_like(dv_ref)

    def query_block(i, _):
        query = get(0, i)
        grad = grad_ref[pl.ds(i * per, per)].reshape(rows, HEAD_SIZE)
        attn = out_ref[pl.ds(i * per, per)].reshape(rows, HEAD_SIZE)
        prod = grad.astype(jnp.float32) * attn.astype(jnp.float32)
        delta = jnp.sum(prod.T, axis=0, keepdims=True)
        lse = lse_ref[i]
        dq_ref[...] = jnp.zeros_like(dq_ref)

        def key_block(j, diagonal):
            key = get(1, j)
            at = pl.ds(j * rows, rows)
            p = jnp.exp2(mm(key, query, NT) * factor - lse)
            if diagonal:
                keep = lax.broadcasted_iota(jnp.int32, p.shape, 0) <= lax.broadcasted_iota(
                    jnp.int32, p.shape, 1
                )
                p = jnp.where(keep, p, 0.0)
            dv_ref[at] += mm(p.astype(jnp.bfloat16), grad)
            ds = (p * (mm(get(2, j), grad, NT) - delta) * scale).astype(jnp.bfloat16)
            dk_ref[at] += mm(ds, query)
            dq_ref[...] += mm(ds, key, TN)

        def body(j, _):
            key_block(j, False)
            return 0

        lax.fori_loop(0, i, body, 0)
        key_block(i, True)
        res_ref[pl.ds(i * per, per), 0] = (
            dq_ref[...].astype(jnp.bfloat16).reshape(per, step, HEAD_SIZE)
        )
        return 0

    lax.fori_loop(0, count, query_block, 0)
    res_ref[:, 1] = dk_ref[...].astype(jnp.bfloat16).reshape(blocks, step, HEAD_SIZE)
    res_ref[:, 2] = dv_ref[...].astype(jnp.bfloat16).reshape(blocks, step, HEAD_SIZE)


def attend_backward(qkv, out, lse, grad, rows=512):
    blocks, _, step, _ = qkv.shape
    length = blocks * step
    lse = lse.reshape(length // rows, 1, rows)
    return pl.pallas_call(
        functools.partial(bwd_kernel, rows=rows),
        out_shape=jax.ShapeDtypeStruct((blocks, 3, step, HEAD_SIZE), jnp.bfloat16),
        in_specs=[pl.BlockSpec(memory_space=pltpu.VMEM)] * 4,
        out_specs=pl.BlockSpec(memory_space=pltpu.VMEM),
        scratch_shapes=[
            pltpu.VMEM((rows, HEAD_SIZE), jnp.float32),
            pltpu.VMEM((length, HEAD_SIZE), jnp.float32),
            pltpu.VMEM((length, HEAD_SIZE), jnp.float32),
        ],
        compiler_params=pltpu.CompilerParams(vmem_limit_bytes=VMEM_LIMIT),
        cost_estimate=pl.CostEstimate(
            flops=5 * length * length * HEAD_SIZE,
            bytes_accessed=16 * length * HEAD_SIZE,
            transcendentals=length * length // 2,
        ),
        name="attend_backward",
    )(qkv, out, lse, grad)


def pack_kernel(q_ref, k_ref, v_ref, out_ref):
    for h in range(out_ref.shape[0]):
        at = slice(h * HEAD_SIZE, (h + 1) * HEAD_SIZE)
        for w, ref in enumerate((q_ref, k_ref, v_ref)):
            out_ref[h, w] = ref[:, at]


def pack_heads(arrays, group=4):
    step, width = arrays[0].shape
    heads = width // HEAD_SIZE
    flat = pl.BlockSpec((step, group * HEAD_SIZE), lambda g: (0, g))
    return pl.pallas_call(
        pack_kernel,
        grid=(heads // group,),
        out_shape=jax.ShapeDtypeStruct((heads, 3, step, HEAD_SIZE), jnp.bfloat16),
        in_specs=[flat] * 3,
        out_specs=pl.BlockSpec((group, 3, step, HEAD_SIZE), lambda g: (g, 0, 0, 0)),
        name="pack_heads",
    )(*arrays)


def unpack_kernel(in_ref, q_ref, k_ref, v_ref):
    for h in range(in_ref.shape[0]):
        at = slice(h * HEAD_SIZE, (h + 1) * HEAD_SIZE)
        for w, ref in enumerate((q_ref, k_ref, v_ref)):
            ref[:, at] = in_ref[h, w]


def unpack_heads(stacked, group=4):
    heads, _, step, _ = stacked.shape
    flat = pl.BlockSpec((step, group * HEAD_SIZE), lambda g: (0, g))
    return pl.pallas_call(
        unpack_kernel,
        grid=(heads // group,),
        out_shape=[jax.ShapeDtypeStruct((step, heads * HEAD_SIZE), jnp.bfloat16)] * 3,
        in_specs=[pl.BlockSpec((group, 3, step, HEAD_SIZE), lambda g: (g, 0, 0, 0))],
        out_specs=[flat] * 3,
        name="unpack_heads",
    )(stacked)


def weight_pair(w_ref, kind):
    pair = [w_ref[0, :, y, kind].reshape(HEAD_SIZE, w_ref.shape[-1]) for y in range(2)]
    return jnp.concatenate(pair, axis=0)


def project_back_kernel(pay_ref, w_ref, out_ref):
    groups, step, _ = pay_ref.shape
    width = w_ref.shape[-1]
    upstream = pay_ref[:, :, :width].reshape(groups * step, width)
    text = mm(upstream, weight_pair(w_ref, 0), NT)
    image = mm(upstream, weight_pair(w_ref, 1), NT)
    for b in range(groups):
        mask = pay_ref[b, :, width:].astype(jnp.float32) > 0.5
        rows = slice(b * step, (b + 1) * step)
        for y in range(2):
            at = slice(y * HEAD_SIZE, (y + 1) * HEAD_SIZE)
            out_ref[b, y] = jnp.where(mask, image[rows, at], text[rows, at]).astype(jnp.bfloat16)


def weight_spec(weights):
    return pl.BlockSpec((1, *weights.shape[1:]), lambda z: (z, 0, 0, 0, 0, 0))


def project_back(payload, weights):
    groups, step, _ = payload.shape
    return pl.pallas_call(
        project_back_kernel,
        grid=(weights.shape[0],),
        out_shape=jax.ShapeDtypeStruct(
            (groups, 2 * weights.shape[0], step, HEAD_SIZE), jnp.bfloat16
        ),
        in_specs=[pl.BlockSpec(memory_space=pltpu.VMEM), weight_spec(weights)],
        out_specs=pl.BlockSpec((groups, 2, step, HEAD_SIZE), lambda z: (0, z, 0, 0)),
        compiler_params=pltpu.CompilerParams(vmem_limit_bytes=VMEM_LIMIT),
        cost_estimate=pl.CostEstimate(
            flops=2 * groups * step * weights.size, bytes_accessed=2 * weights.size, transcendentals=0
        ),
        name="project_back",
    )(payload, weights)


def project_kernel(attn_ref, pay_ref, w_ref, out_ref, acc_ref):
    groups, _, step, _ = attn_ref.shape
    width = w_ref.shape[-1]

    @pl.when(pl.program_id(0) == 0)
    def _():
        acc_ref[...] = jnp.zeros_like(acc_ref)

    text, image = [], []
    for b in range(groups):
        mask = pay_ref[b, :, width:].astype(jnp.float32) > 0.5
        parts = [attn_ref[b, y].astype(jnp.float32) for y in range(2)]
        text.append(jnp.concatenate([jnp.where(mask, 0.0, p) for p in parts], axis=1))
        image.append(jnp.concatenate([jnp.where(mask, p, 0.0) for p in parts], axis=1))
    text = jnp.concatenate(text, axis=0).astype(jnp.bfloat16)
    image = jnp.concatenate(image, axis=0).astype(jnp.bfloat16)
    acc_ref[...] += mm(text, weight_pair(w_ref, 0)) + mm(image, weight_pair(w_ref, 1))

    @pl.when(pl.program_id(0) == pl.num_programs(0) - 1)
    def _():
        out_ref[...] = acc_ref[...].astype(out_ref.dtype).reshape(out_ref.shape)


def project(attn, payload, weights):
    groups, _, step, _ = attn.shape
    width = weights.shape[-1]
    return pl.pallas_call(
        project_kernel,
        grid=(weights.shape[0],),
        out_shape=jax.ShapeDtypeStruct((groups, step, width), jnp.bfloat16),
        in_specs=[
            pl.BlockSpec((groups, 2, step, HEAD_SIZE), lambda z: (0, z, 0, 0)),
            pl.BlockSpec(memory_space=pltpu.VMEM),
            weight_spec(weights),
        ],
        out_specs=pl.BlockSpec((groups, step, width), lambda z: (0, 0, 0)),
        scratch_shapes=[pltpu.VMEM((groups * step, width), jnp.float32)],
        compiler_params=pltpu.CompilerParams(vmem_limit_bytes=VMEM_LIMIT),
        cost_estimate=pl.CostEstimate(
            flops=2 * groups * step * weights.size, bytes_accessed=2 * weights.size, transcendentals=0
        ),
        name="project",
    )(attn, payload, weights)


CTX = ("z", "yh", "x")


def exchange(blocks, axis):
    return lax.all_to_all(blocks, axis, split_axis=0, concat_axis=0, tiled=True)


def per_device(query_proj, key_proj, value_proj, modality, out_weight, grad_projected):
    groups = lax.axis_size("fsdp")
    step, inner = query_proj.shape[1:]
    heads = inner // HEAD_SIZE
    quarter = heads // groups
    pair = lax.all_gather(out_weight, "yh", axis=0)
    weights = lax.all_gather(pair, ("z", "x"), axis=0)
    weights = weights.reshape(lax.axis_size("z"), lax.axis_size("x"), *pair.shape)

    qkv = exchange(pack_heads((query_proj[0], key_proj[0], value_proj[0])), CTX)
    kind = jnp.broadcast_to(modality[0][:, None], (step, HEAD_SIZE)).astype(jnp.bfloat16)
    payload = jnp.concatenate([grad_projected[0], kind], axis=1)
    payload = exchange(jnp.broadcast_to(payload, (groups, *payload.shape)), "fsdp")

    attention, lse = attend_forward(qkv, FWD_ROWS)
    attn_rows = exchange(attention, CTX).reshape(groups, quarter, step, HEAD_SIZE)
    attn_rows = exchange(attn_rows, "fsdp")

    grad_rows = exchange(project_back(payload, weights), "fsdp")
    grad_heads = exchange(grad_rows.reshape(heads, step, HEAD_SIZE), CTX)
    partial = exchange(project(attn_rows, payload, weights), "fsdp")
    total = partial[0].astype(jnp.float32)
    for f in range(1, groups):
        total = total + partial[f].astype(jnp.float32)
    projected = total.astype(jnp.bfloat16)[None]

    grads = attend_backward(qkv, attention, lse, grad_heads, BWD_ROWS)
    grad_query, grad_key, grad_value = unpack_heads(exchange(grads, CTX))
    return projected, grad_query[None], grad_key[None], grad_value[None]


def solution(mesh):
    grid = jax.sharding.Mesh(mesh.devices.reshape(-1, 4, 2, 4), ("fsdp", *CTX))
    rows = P("fsdp", CTX, None)
    placed = (rows, rows, rows, P("fsdp", CTX), P(None, ("fsdp", *CTX), None), rows)
    return jax.shard_map(
        per_device,
        mesh=grid,
        in_specs=placed,
        out_specs=(rows,) * 4,
        check_vma=False,
    )
```

time: 687 us -> 307 us (0.45)
  waiting for transfers between devices: 307 us -> 101 us
  matrix products: 112 us -> 0 us
  local copies, waits for them, and re-layouts: 102 us -> 6.04 us
  Pallas kernels: 0 us -> 89.8 us
  other arithmetic: 76.6 us -> 4.54 us
  blocking collectives: 0 us -> 57.2 us
  starting transfers between devices: 64.5 us -> 30.5 us
    all_gather x1, waiting for transfers between devices: 209 us -> 0.02 us  [per_device(): weights = lax.all_gather(pair, ('z', 'x'), axis=0)]
    dot_general x52 -> x0, matrix products: 112 us -> none  [the longest x2 24 us: transposed_product(): lax.dot_general(left, right, (((1,), (1,)), ((), ())), preferred_element_...]
    pallas_call x0 -> x6, Pallas kernels: none -> 89.8 us  [the longest x1 34.8 us: attend_backward(): pl.pallas_call(functools.partial(bwd_kernel, rows=rows), out_shape=jax.Sh...]
    unnamed x7 -> x0, other arithmetic: 48 us -> none
    all_to_all x0 -> x2, blocking collectives: none -> 43.8 us  [exchange(): return lax.all_to_all(blocks, axis, split_axis=0, concat_axis=0, tiled=True)]
    split x16 -> x0, local copies, waits for them, and re-layouts: 40.9 us -> none  [the longest x7 26 us: sent_together(): jnp.split(filled, [sum(widths[:k]) for k in range(1, len(widths))], axis=...]
    all_to_all x9 -> x6, starting transfers between devices: 64.4 us -> 30.5 us  [exchange(): return lax.all_to_all(blocks, axis, split_axis=0, concat_axis=0, tiled=True)]
    unnamed x90 -> x12, local copies, waits for them, and re-layouts: 28.1 us -> 3.01 us
  transfers between devices with their start and end apart: 10 -> 7, of which waited for: 8 -> 5; matrix products, arithmetic and copies ran while one was open for 30% -> 2% of each run, Pallas kernels for 0% -> 28%
where the time goes in v1:
time: 307 us; the launch traced here: 303 us
  waiting for transfers between devices  101 us (33%)
  Pallas kernels  89.8 us (29%)
  blocking collectives  57.2 us (19%)
  starting transfers between devices  30.5 us (10%)
  between operations  14.1 us (5%)
  local copies, waits for them, and re-layouts  6.04 us (2%)
  other arithmetic  4.54 us (1%)
    all_to_all x6, waiting for transfers between devices, exchange(): return lax.all_to_all(blocks, axis, split_axis=0, concat_axis=0, tiled=True)  101 us
    all_to_all x2, blocking collectives, exchange(): return lax.all_to_all(blocks, axis, split_axis=0, concat_axis=0, tiled=True)  43.8 us
    pallas_call x1, Pallas kernels, attend_backward(): pl.pallas_call(functools.partial(bwd_kernel, rows=rows), out_shape=jax.Sh...  34.8 us
    all_to_all x6, starting transfers between devices, exchange(): return lax.all_to_all(blocks, axis, split_axis=0, concat_axis=0, tiled=True)  30.5 us
    pallas_call x1, Pallas kernels, attend_forward(): pl.pallas_call(functools.partial(fwd_kernel, rows=rows), out_shape=(jax.S...  23.9 us
    all_gather x1, blocking collectives, per_device(): pair = lax.all_gather(out_weight, 'yh', axis=0)  13.5 us
    pallas_call x1, Pallas kernels, project(): pl.pallas_call(project_kernel, grid=(weights.shape[0],), out_shape=jax.Sh...  9.77 us
    pallas_call x1, Pallas kernels, project_back(): pl.pallas_call(project_back_kernel, grid=(weights.shape[0],), out_shape=j...  8.65 us
  transfers between devices with their start and end apart: 7, of which 5 were waited for; matrix products, arithmetic and copies ran while one was open for 2% of the time, Pallas kernels for 28%

profile of v1, /device:TPU:0, one launch (start us, length us, event | category | flops | bytes accessed | tf_op | source)
XLA Modules:
  0.0 303.0 jit_solution(815664133168246591)
XLA Ops:
  7.2 0.0 all-gather.4.cloned.1.call-start
  7.2 13.5 %all-gather = bf16[4,32,2048]{2,1,0:T(8,128)(2,1)} all-gather(bf16[2,32,2048]{2,1,0:T(8,128)(2,1)} %param.10), channel_id=2, replica_groups=mesh['fsdp'=4,'z'=4,'yh'=2,'x'=4] {'yh'}, dimensions={0}, use_global_device_ids=true | all-gather | bytes 786432 | tf_op jit(solution)/shard_map/all_gather | solution.py:307
  20.7 0.0 all-gather.4.cloned.1.call-update
  20.7 6.4 %pack_heads.1 = bf16[32,3,128,128]{3,2,1,0:T(8,128)(2,1)} custom-call(bf16[128,4096]{1,0:T(8,128)(2,1)} %bitcast.14, bf16[128,4096]{1,0:T(8,128)(2,1)} %bitcast.15, bf16[128,4096]{1,0:T(8,128)(2,1)} %bitcast.16), custom_call_target="tpu_custom_call" | custom-call | tf_op jit(solution)/shard_map/pack_heads/pallas_call | solution.py:179
  27.2 0.0 copy-start.5
  27.2 8.3 %all-to-all-start = ((bf16[32,3,128,128]{3,2,1,0:T(8,128)(2,1)}), bf16[32,3,128,128]{3,2,1,0:T(8,128)(2,1)S(1)}, u32[]{:S(2)}, u32[]{:S(2)}) async-start(bf16[32,3,128,128]{3,2,1,0:T(8,128)(2,1)} %pack_heads.1), calls=%async_computation | async-start | bytes 6291456 | tf_op jit(solution)/shard_map/all_to_all | solution.py:299
  35.5 0.0 copy-done.5
  35.5 0.1 broadcast_in_dim.18
  35.6 1.9 pad_maximum_fusion
  37.5 44.9 %all-to-all-done.qkv_ref = bf16[32,3,128,128]{3,2,1,0:T(8,128)(2,1)S(1)} async-done(((bf16[32,3,128,128]{3,2,1,0:T(8,128)(2,1)}), bf16[32,3,128,128]{3,2,1,0:T(8,128)(2,1)S(1)}, u32[]{:S(2)}, u32[]{:S(2)}) %all-to-all-start) | async-done | bytes 3145760 | tf_op jit(solution)/shard_map/all_to_all | solution.py:299
  82.4 0.0 copy-start.2
  82.4 2.9 broadcast_in_dim.19
  85.3 0.0 copy-done.2
  85.3 4.5 %all-to-all-start.3 = ((bf16[4,128,2176]{2,1,0:T(8,128)(2,1)}), bf16[4,128,2176]{2,1,0:T(8,128)(2,1)}, u32[]{:S(2)}, u32[]{:S(2)}) async-start(bf16[4,128,2176]{2,1,0:T(8,128)(2,1)} %broadcast_in_dim.19), calls=%async_computation.3 | async-start | bytes 4456448 | tf_op jit(solution)/shard_map/all_to_all | solution.py:299
  89.8 23.9 %attend_forward.1 = (bf16[32,128,128]{2,1,0:T(8,128)(2,1)}, f32[4,1,1024]{2,1,0:T(1,128)}) custom-call(bf16[32,3,128,128]{3,2,1,0:T(8,128)(2,1)} %copy-done.2), custom_call_target="tpu_custom_call" | custom-call | flops 4294967296 | bytes 4194304 | tf_op jit(solution)/shard_map/attend_forward/pallas_call | solution.py:73
  113.7 3.3 %all-to-all-done.3.pay_ref = bf16[4,128,2176]{2,1,0:T(8,128)(2,1)} async-done(((bf16[4,128,2176]{2,1,0:T(8,128)(2,1)}), bf16[4,128,2176]{2,1,0:T(8,128)(2,1)}, u32[]{:S(2)}, u32[]{:S(2)}) %all-to-all-start.3) | async-done | bytes 2228256 | tf_op jit(solution)/shard_map/all_to_all | solution.py:299
  117.0 25.0 %all_to_all.40 = bf16[32,128,128]{2,1,0:T(8,128)(2,1)} all-to-all(bf16[32,128,128]{2,1,0:T(8,128)(2,1)} %get-tuple-element.9.out_ref), channel_id=1, replica_groups=mesh['fsdp'=4,'z'=4,'yh'=2,'x'=4] {'z','yh','x'}, dimensions={0} | all-to-all | bytes 2097152 | tf_op jit(solution)/shard_map/all_to_all | solution.py:299
  141.9 3.5 %all-to-all-start.2 = ((bf16[4,8,128,128]{3,2,1,0:T(8,128)(2,1)}), bf16[4,8,128,128]{3,2,1,0:T(8,128)(2,1)S(1)}, u32[]{:S(2)}, u32[]{:S(2)}) async-start(bf16[4,8,128,128]{3,2,1,0:T(8,128)(2,1)} %bitcast.3), calls=%async_computation.2 | async-start | bytes 2097152 | tf_op jit(solution)/shard_map/all_to_all | solution.py:299
  145.5 0.0 all-gather.4.cloned.1.call-done
  145.5 8.7 %project_back.1 = bf16[4,8,128,128]{3,2,1,0:T(8,128)(2,1)} custom-call(bf16[4,128,2176]{2,1,0:T(8,128)(2,1)} %all-to-all-done.3.pay_ref, bf16[4,4,2,2,32,2048]{5,4,3,2,1,0:T(8,128)(2,1)} %bitcast.18), custom_call_target="tpu_custom_call" | custom-call | flops 4294967296 | bytes 8388608 | tf_op jit(solution)/shard_map/project_back/pallas_call | solution.py:234
  154.1 5.7 %all-to-all-done.2.attn_ref = bf16[4,8,128,128]{3,2,1,0:T(8,128)(2,1)S(1)} async-done(((bf16[4,8,128,128]{3,2,1,0:T(8,128)(2,1)}), bf16[4,8,128,128]{3,2,1,0:T(8,128)(2,1)S(1)}, u32[]{:S(2)}, u32[]{:S(2)}) %all-to-all-start.2) | async-done | bytes 1048608 | tf_op jit(solution)/shard_map/all_to_all | solution.py:299
  159.9 0.0 copy-start.3
  159.9 18.8 %all_to_all.41 = bf16[4,8,128,128]{3,2,1,0:T(8,128)(2,1)} all-to-all(bf16[4,8,128,128]{3,2,1,0:T(8,128)(2,1)} %project_back.1), channel_id=1, replica_groups=mesh['fsdp'=4,'z'=4,'yh'=2,'x'=4] {'fsdp'}, dimensions={0} | all-to-all | bytes 2097152 | tf_op jit(solution)/shard_map/all_to_all | solution.py:299
  178.7 5.2 %all-to-all-start.6 = ((bf16[32,128,128]{2,1,0:T(8,128)(2,1)}), bf16[32,128,128]{2,1,0:T(8,128)(2,1)S(1)}, u32[]{:S(2)}, u32[]{:S(2)}) async-start(bf16[32,128,128]{2,1,0:T(8,128)(2,1)} %bitcast.8), calls=%async_computation.6 | async-start | bytes 2097152 | tf_op jit(solution)/shard_map/all_to_all | solution.py:299
  183.9 0.0 copy-done.3
  183.9 9.8 %project.1 = bf16[4,128,2048]{2,1,0:T(8,128)(2,1)} custom-call(bf16[4,8,128,128]{3,2,1,0:T(8,128)(2,1)} %copy-done.3, bf16[4,128,2176]{2,1,0:T(8,128)(2,1)} %all-to-all-done.3.pay_ref, bf16[4,4,2,2,32,2048]{5,4,3,2,1,0:T(8,128)(2,1)} %bitcast.19), custom_call_target="tpu_custom_call" | custom-call | flops 4294967296 | bytes 8388608 | tf_op jit(solution)/shard_map/project/pallas_call | solution.py:276
  193.7 7.9 %all-to-all-done.6.grad_ref = bf16[32,128,128]{2,1,0:T(8,128)(2,1)S(1)} async-done(((bf16[32,128,128]{2,1,0:T(8,128)(2,1)}), bf16[32,128,128]{2,1,0:T(8,128)(2,1)S(1)}, u32[]{:S(2)}, u32[]{:S(2)}) %all-to-all-start.6) | async-done | bytes 1048608 | tf_op jit(solution)/shard_map/all_to_all | solution.py:299
  201.6 0.0 copy-start.4
  201.6 3.8 %all-to-all-start.4 = ((bf16[4,128,2048]{2,1,0:T(8,128)(2,1)}), bf16[4,128,2048]{2,1,0:T(8,128)(2,1)S(1)}, u32[]{:S(2)}, u32[]{:S(2)}) async-start(bf16[4,128,2048]{2,1,0:T(8,128)(2,1)} %project.1), calls=%async_computation.4 | async-start | bytes 4194304 | tf_op jit(solution)/shard_map/all_to_all | solution.py:299
  205.4 0.0 copy-done.4
  205.4 34.8 %attend_backward.1 = bf16[32,3,128,128]{3,2,1,0:T(8,128)(2,1)} custom-call(bf16[32,3,128,128]{3,2,1,0:T(8,128)(2,1)} %copy-done.2, bf16[32,128,128]{2,1,0:T(8,128)(2,1)} %get-tuple-element.9.out_ref, f32[4,1,1024]{2,1,0:T(1,128)} %get-tuple-element.10.lse_ref, bf16[32,128,128]{2,1,0:T(8,128)(2,1)} %copy-done.4), custom_call_target="tpu_custom_call" | custom-call | flops 10737418240 | bytes 8388608 | tf_op jit(solution)/shard_map/attend_backward/pallas_call | solution.py:148
  240.2 0.0 all-to-all-done.4
  240.2 0.0 copy-start.1
  240.2 1.4 copy-done.1
  241.6 5.2 %all-to-all-start.7 = ((bf16[32,3,128,128]{3,2,1,0:T(8,128)(2,1)}), bf16[32,3,128,128]{3,2,1,0:T(8,128)(2,1)S(1)}, u32[]{:S(2)}, u32[]{:S(2)}) async-start(bf16[32,3,128,128]{3,2,1,0:T(8,128)(2,1)} %attend_backward.1), calls=%async_computation.7 | async-start | bytes 6291456 | tf_op jit(solution)/shard_map/all_to_all | solution.py:299
  246.7 2.6 add_convert_fusion
  249.4 38.9 %all-to-all-done.7.in_ref = bf16[32,3,128,128]{3,2,1,0:T(8,128)(2,1)S(1)} async-done(((bf16[32,3,128,128]{3,2,1,0:T(8,128)(2,1)}), bf16[32,3,128,128]{3,2,1,0:T(8,128)(2,1)S(1)}, u32[]{:S(2)}, u32[]{:S(2)}) %all-to-all-start.7) | async-done | bytes 3145760 | tf_op jit(solution)/shard_map/all_to_all | solution.py:299
  288.3 0.0 copy-start
  288.3 1.6 copy-done
  289.9 6.3 %unpack_heads.1 = (bf16[128,4096]{1,0:T(8,128)(2,1)}, bf16[128,4096]{1,0:T(8,128)(2,1)}, bf16[128,4096]{1,0:T(8,128)(2,1)}) custom-call(bf16[32,3,128,128]{3,2,1,0:T(8,128)(2,1)} %copy-done), custom_call_target="tpu_custom_call" | custom-call | tf_op jit(solution)/shard_map/unpack_heads/pallas_call | solution.py:199
  (1 shorter events, 0.0 us)
Async XLA Ops:
  7.2 138.3 %all-gather.4.cloned.1.call-start = ((), (), s32[]{:S(2)}) async-start(), calls=%async_computation.8 | async-start | bytes 8912896 | tf_op jit(solution)/shard_map/all_gather | solution.py:308
  27.2 8.3 %copy-start.5 = (s32[1,128]{1,0:T(1,128)S(1)}, s32[1,128]{1,0:T(1,128)}, u32[]{:S(2)}) copy-start(s32[1,128]{1,0:T(1,128)} %param.9) | copy-start | bytes 1540
  27.2 55.2 %all-to-all-start = ((bf16[32,3,128,128]{3,2,1,0:T(8,128)(2,1)}), bf16[32,3,128,128]{3,2,1,0:T(8,128)(2,1)S(1)}, u32[]{:S(2)}, u32[]{:S(2)}) async-start(bf16[32,3,128,128]{3,2,1,0:T(8,128)(2,1)} %pack_heads.1), calls=%async_computation | async-start | bytes 6291456 | tf_op jit(solution)/shard_map/all_to_all | solution.py:299
  82.4 2.9 copy-start.2
  85.3 31.7 %all-to-all-start.3 = ((bf16[4,128,2176]{2,1,0:T(8,128)(2,1)}), bf16[4,128,2176]{2,1,0:T(8,128)(2,1)}, u32[]{:S(2)}, u32[]{:S(2)}) async-start(bf16[4,128,2176]{2,1,0:T(8,128)(2,1)} %broadcast_in_dim.19), calls=%async_computation.3 | async-start | bytes 4456448 | tf_op jit(solution)/shard_map/all_to_all | solution.py:299
  141.9 18.0 %all-to-all-start.2 = ((bf16[4,8,128,128]{3,2,1,0:T(8,128)(2,1)}), bf16[4,8,128,128]{3,2,1,0:T(8,128)(2,1)S(1)}, u32[]{:S(2)}, u32[]{:S(2)}) async-start(bf16[4,8,128,128]{3,2,1,0:T(8,128)(2,1)} %bitcast.3), calls=%async_computation.2 | async-start | bytes 2097152 | tf_op jit(solution)/shard_map/all_to_all | solution.py:299
  159.9 24.0 %copy-start.3 = (bf16[4,8,128,128]{3,2,1,0:T(8,128)(2,1)}, bf16[4,8,128,128]{3,2,1,0:T(8,128)(2,1)S(1)}, u32[]{:S(2)}) copy-start(bf16[4,8,128,128]{3,2,1,0:T(8,128)(2,1)S(1)} %all-to-all-done.2.attn_ref) | copy-start | bytes 3145732
  178.7 22.9 %all-to-all-start.6 = ((bf16[32,128,128]{2,1,0:T(8,128)(2,1)}), bf16[32,128,128]{2,1,0:T(8,128)(2,1)S(1)}, u32[]{:S(2)}, u32[]{:S(2)}) async-start(bf16[32,128,128]{2,1,0:T(8,128)(2,1)} %bitcast.8), calls=%async_computation.6 | async-start | bytes 2097152 | tf_op jit(solution)/shard_map/all_to_all | solution.py:299
  201.6 3.8 %copy-start.4 = (bf16[32,128,128]{2,1,0:T(8,128)(2,1)}, bf16[32,128,128]{2,1,0:T(8,128)(2,1)S(1)}, u32[]{:S(2)}) copy-start(bf16[32,128,128]{2,1,0:T(8,128)(2,1)S(1)} %all-to-all-done.6.grad_ref) | copy-start | bytes 3145732
  201.6 38.6 %all-to-all-start.4 = ((bf16[4,128,2048]{2,1,0:T(8,128)(2,1)}), bf16[4,128,2048]{2,1,0:T(8,128)(2,1)S(1)}, u32[]{:S(2)}, u32[]{:S(2)}) async-start(bf16[4,128,2048]{2,1,0:T(8,128)(2,1)} %project.1), calls=%async_computation.4 | async-start | bytes 4194304 | tf_op jit(solution)/shard_map/all_to_all | solution.py:299
  240.2 1.4 copy-start.1
  241.6 46.7 %all-to-all-start.7 = ((bf16[32,3,128,128]{3,2,1,0:T(8,128)(2,1)}), bf16[32,3,128,128]{3,2,1,0:T(8,128)(2,1)S(1)}, u32[]{:S(2)}, u32[]{:S(2)}) async-start(bf16[32,3,128,128]{3,2,1,0:T(8,128)(2,1)} %attend_backward.1), calls=%async_computation.7 | async-start | bytes 6291456 | tf_op jit(solution)/shard_map/all_to_all | solution.py:299
  288.3 1.6 copy-start
Sparse Core Ops, SparseCore 0:
  20.8 102.2 all-gather.3

commit v2 on v1

v2 whole, which is shorter than its diff:
```python
import functools, math
import jax, jax.numpy as jnp
from jax import lax
from jax.experimental import pallas as pl
from jax.experimental.pallas import tpu as pltpu
from jax.sharding import PartitionSpec as P

HEAD_SIZE = 128
LOG2E = math.log2(math.e)
NT = (((1,), (1,)), ((), ()))
TN = (((0,), (0,)), ((), ()))
VMEM_LIMIT = 56 * 1024 * 1024
FWD_ROWS = 1024
BWD_ROWS = 1024
KIND_ROWS = 16
PACK = 2


def mm(a, b, dims=(((1,), (0,)), ((), ()))):
    return lax.dot_general(a, b, dims, preferred_element_type=jnp.float32)


def visible(shape, key_dim, shift):
    keys = lax.broadcasted_iota(jnp.int32, shape, key_dim)
    return keys + shift <= lax.broadcasted_iota(jnp.int32, shape, 1 - key_dim)


def fwd_kernel(me_ref, qkv_ref, out_ref, own_ref, other_ref, lse_ref, s_ref, *, rows):
    blocks = qkv_ref.shape[0]
    step = HEAD_SIZE
    per = rows // step
    count = blocks // per
    half = rows // 2
    factor = HEAD_SIZE**-0.5 * LOG2E

    def get(which, first, size):
        part = qkv_ref[pl.ds(first, size // step), which * step : (which + 1) * step]
        return part.reshape(size, HEAD_SIZE)

    def fold(op, start, s):
        for c in range(0, s.shape[1], HEAD_SIZE):
            start = op(start, s[:, c : c + HEAD_SIZE])
        return start

    def query_block(i, _):
        query = get(0, i * per, rows)

        def scores(j, top):
            s = mm(query, get(1, j * per, rows), NT)
            s_ref[j] = s
            return fold(jnp.maximum, top, s)

        top = lax.fori_loop(0, i, scores, jnp.full((rows, HEAD_SIZE), -jnp.inf, jnp.float32))
        highs = []
        for part in range(2):
            size = half * (part + 1)
            at = slice(part * half, (part + 1) * half)
            s = mm(query[at], get(1, i * per, size), NT)
            s = jnp.where(visible(s.shape, 1, -part * half), s, -jnp.inf)
            s_ref[i, at, :size] = s
            highs.append(jnp.max(fold(jnp.maximum, top[at], s), axis=1, keepdims=True) * factor)
        high = jnp.concatenate(highs, axis=0)

        def values(j, carry):
            total, acc = carry
            p = jnp.exp2(s_ref[j] * factor - high)
            total = fold(jnp.add, total, p)
            return total, acc + mm(p.astype(jnp.bfloat16), get(2, j * per, rows))

        zero = jnp.zeros((rows, HEAD_SIZE), jnp.float32)
        totals, accs = lax.fori_loop(0, i, values, (zero, zero))
        for part in range(2):
            size = half * (part + 1)
            at = slice(part * half, (part + 1) * half)
            p = jnp.exp2(s_ref[i, at, :size] * factor - highs[part])
            total = jnp.sum(fold(jnp.add, totals[at], p), axis=1, keepdims=True)
            acc = accs[at] + mm(p.astype(jnp.bfloat16), get(2, i * per, size))
            out = (acc / total).astype(jnp.bfloat16)
            out_ref[pl.ds(i * per + part * per // 2, per // 2)] = out.reshape(-1, step, HEAD_SIZE)
            lse = jnp.broadcast_to(highs[part] + jnp.log2(total), (half, HEAD_SIZE))
            lse_ref[i, :, at] = lse.T[0:1]
        return 0

    lax.fori_loop(0, count, query_block, 0)
    me = me_ref[0]
    half = blocks // 8
    for z in range(4):
        own_ref[z * half : (z + 1) * half] = out_ref[pl.ds((2 * z + me) * half, half)]
        other_ref[z * half : (z + 1) * half] = out_ref[pl.ds((2 * z + 1 - me) * half, half)]


def attend_forward(me, qkv, rows):
    blocks, step = qkv.shape[0], HEAD_SIZE
    length = blocks * step
    return pl.pallas_call(
        functools.partial(fwd_kernel, rows=rows),
        out_shape=(
            jax.ShapeDtypeStruct((blocks, step, HEAD_SIZE), jnp.bfloat16),
            jax.ShapeDtypeStruct((blocks // 2, step, HEAD_SIZE), jnp.bfloat16),
            jax.ShapeDtypeStruct((blocks // 2, step, HEAD_SIZE), jnp.bfloat16),
            jax.ShapeDtypeStruct((length // rows, 1, rows), jnp.float32),
        ),
        in_specs=[
            pl.BlockSpec(memory_space=pltpu.SMEM),
            pl.BlockSpec(memory_space=pltpu.VMEM),
        ],
        out_specs=[pl.BlockSpec(memory_space=pltpu.VMEM)] * 4,
        scratch_shapes=[pltpu.VMEM((length // rows, rows, rows), jnp.float32)],
        compiler_params=pltpu.CompilerParams(vmem_limit_bytes=VMEM_LIMIT),
        cost_estimate=pl.CostEstimate(
            flops=12 * length * length * HEAD_SIZE,
            bytes_accessed=8 * length * HEAD_SIZE,
            transcendentals=length * length // 2,
        ),
        name="attend_forward",
    )(me, qkv)


def bwd_kernel(
    me_ref, qkv_ref, out_ref, lse_ref, own_ref, other_ref, res_ref, grad_ref, dq_ref, dk_ref, dv_ref, *, rows
):
    blocks = qkv_ref.shape[0]
    step = HEAD_SIZE
    per = rows // step
    count = blocks // per
    scale = HEAD_SIZE**-0.5
    factor = scale * LOG2E

    def get(which, first, size):
        part = qkv_ref[pl.ds(first, size // step), which * step : (which + 1) * step]
        return part.reshape(size, HEAD_SIZE)

    me = me_ref[0]
    half = blocks // 8
    for z in range(4):
        grad_ref[pl.ds((2 * z + me) * half, half)] = own_ref[z * half : (z + 1) * half]
        grad_ref[pl.ds((2 * z + 1 - me) * half, half)] = other_ref[z * half : (z + 1) * half]
    dk_ref[...] = jnp.zeros_like(dk_ref)
    dv_ref[...] = jnp.zeros_like(dv_ref)

    def query_block(i, _):
        query = get(0, i * per, rows)
        grad = grad_ref[pl.ds(i * per, per)].reshape(rows, HEAD_SIZE)
        attn = out_ref[pl.ds(i * per, per)].reshape(rows, HEAD_SIZE)
        prod = grad.astype(jnp.float32) * attn.astype(jnp.float32)
        delta = jnp.sum(prod.T, axis=0, keepdims=True)
        lse = lse_ref[i]
        dq_ref[...] = jnp.zeros_like(dq_ref)

        def key_block(j, size, at, shift=None):
            key = get(1, j * per, size)
            to = pl.ds(j * rows, size)
            p = jnp.exp2(mm(key, query[at], NT) * factor - lse[:, at])
            if shift is not None:
                p = jnp.where(visible(p.shape, 0, shift), p, 0.0)
            dv_ref[to] += mm(p.astype(jnp.bfloat16), grad[at])
            ds = p * (mm(get(2, j * per, size), grad[at], NT) - delta[:, at]) * scale
            ds = ds.astype(jnp.bfloat16)
            dk_ref[to] += mm(ds, query[at])
            dq_ref[at] += mm(ds, key, TN)

        def body(j, _):
            key_block(j, rows, slice(0, rows))
            return 0

        lax.fori_loop(0, i, body, 0)
        middle = rows // 2
        key_block(i, middle, slice(0, middle), 0)
        key_block(i, rows, slice(middle, rows), -middle)
        done = dq_ref[...].astype(jnp.bfloat16).reshape(per, step, HEAD_SIZE)
        res_ref[pl.ds(i * per, per), 0] = done
        return 0

    lax.fori_loop(0, count, query_block, 0)
    res_ref[:, 1] = dk_ref[...].astype(jnp.bfloat16).reshape(blocks, step, HEAD_SIZE)
    res_ref[:, 2] = dv_ref[...].astype(jnp.bfloat16).reshape(blocks, step, HEAD_SIZE)


def attend_backward(me, qkv, out, lse, grad_own, grad_other, rows):
    blocks, step = qkv.shape[0], HEAD_SIZE
    length = blocks * step
    lse = lse.reshape(length // rows, 1, rows)
    return pl.pallas_call(
        functools.partial(bwd_kernel, rows=rows),
        out_shape=jax.ShapeDtypeStruct((blocks, 3, step, HEAD_SIZE), jnp.bfloat16),
        in_specs=[pl.BlockSpec(memory_space=pltpu.SMEM)]
        + [pl.BlockSpec(memory_space=pltpu.VMEM)] * 5,
        out_specs=pl.BlockSpec(memory_space=pltpu.VMEM),
        scratch_shapes=[
            pltpu.VMEM((blocks, step, HEAD_SIZE), jnp.bfloat16),
            pltpu.VMEM((rows, HEAD_SIZE), jnp.float32),
            pltpu.VMEM((length, HEAD_SIZE), jnp.float32),
            pltpu.VMEM((length, HEAD_SIZE), jnp.float32),
        ],
        compiler_params=pltpu.CompilerParams(vmem_limit_bytes=VMEM_LIMIT),
        cost_estimate=pl.CostEstimate(
            flops=20 * length * length * HEAD_SIZE,
            bytes_accessed=16 * length * HEAD_SIZE,
            transcendentals=length * length // 2,
        ),
        name="attend_backward",
    )(me, qkv, out, lse, grad_own, grad_other)


def pack_kernel(q_ref, k_ref, v_ref, kind_ref, out_ref):
    step = q_ref.shape[0]
    kind = jnp.broadcast_to(kind_ref[...].astype(jnp.float32), (KIND_ROWS, HEAD_SIZE))
    for h in range(2 * PACK):
        at = slice(h * HEAD_SIZE, (h + 1) * HEAD_SIZE)
        for w, ref in enumerate((q_ref, k_ref, v_ref)):
            out_ref[h // 2, h % 2, 0, w * step : (w + 1) * step] = ref[:, at]
        out_ref[h // 2, h % 2, 0, 3 * step :] = kind.astype(jnp.bfloat16)


def owner(*tail):
    per = 4 // PACK
    return pl.BlockSpec(
        (PACK, 2, 1, *tail), lambda g: (g % per, 0, g // per, *([0] * len(tail)))
    )


def pack_heads(arrays, kind):
    step, width = arrays[0].shape
    flat = pl.BlockSpec((step, 2 * PACK * HEAD_SIZE), lambda g: (0, g))
    tall = 3 * step + KIND_ROWS
    return pl.pallas_call(
        pack_kernel,
        grid=(16 // PACK,),
        out_shape=jax.ShapeDtypeStruct((4, 2, 4, tall, HEAD_SIZE), jnp.bfloat16),
        in_specs=[flat] * 3 + [pl.BlockSpec((1, step), lambda g: (0, 0))],
        out_specs=owner(tall, HEAD_SIZE),
        name="pack_heads",
    )(*arrays, kind)


def unpack_kernel(in_ref, q_ref, k_ref, v_ref):
    for h in range(2 * PACK):
        at = slice(h * HEAD_SIZE, (h + 1) * HEAD_SIZE)
        for w, ref in enumerate((q_ref, k_ref, v_ref)):
            ref[:, at] = in_ref[h // 2, h % 2, 0, w]


def unpack_heads(stacked):
    step = stacked.shape[-2]
    flat = pl.BlockSpec((step, 2 * PACK * HEAD_SIZE), lambda g: (0, g))
    return pl.pallas_call(
        unpack_kernel,
        grid=(16 // PACK,),
        out_shape=[jax.ShapeDtypeStruct((step, 32 * HEAD_SIZE), jnp.bfloat16)] * 3,
        in_specs=[owner(3, step, HEAD_SIZE)],
        out_specs=[flat] * 3,
        name="unpack_heads",
    )(stacked)


def kind_spec(step):
    return pl.BlockSpec((1, 2, 4, KIND_ROWS, HEAD_SIZE), lambda g: (g, 0, 0, 3 * step // KIND_ROWS, 0))


def is_image(kind_ref, me, b):
    row = kind_ref[0, me, b].astype(jnp.float32)[0:1]
    return jnp.broadcast_to(row, (row.shape[1], row.shape[1])).T > 0.5


def pair_rows(w_ref, kind, me):
    return [w_ref[:, y, kind].reshape(HEAD_SIZE, w_ref.shape[-1]) for y in (me, 1 - me)]


def project_back_kernel(me_ref, up_ref, kind_ref, w_ref, own_ref, other_ref):
    count, step, width = up_ref.shape
    me = me_ref[0]
    upstream = up_ref[...].reshape(count * step, width)
    text = mm(upstream, jnp.concatenate(pair_rows(w_ref, 0, me), axis=0), NT)
    image = mm(upstream, jnp.concatenate(pair_rows(w_ref, 1, me), axis=0), NT)
    for b in range(count):
        mask = is_image(kind_ref, me, b)
        rows = slice(b * step, (b + 1) * step)
        for y, ref in enumerate((own_ref, other_ref)):
            at = slice(y * HEAD_SIZE, (y + 1) * HEAD_SIZE)
            ref[b] = jnp.where(mask, image[rows, at], text[rows, at]).astype(jnp.bfloat16)


def project_back(me, upstream, kinds, weights, group=4):
    count, step, width = upstream.shape
    half = pl.BlockSpec((group, step, HEAD_SIZE), lambda g: (g, 0, 0))
    return pl.pallas_call(
        project_back_kernel,
        grid=(count // group,),
        out_shape=[jax.ShapeDtypeStruct((count, step, HEAD_SIZE), jnp.bfloat16)] * 2,
        in_specs=[
            pl.BlockSpec(memory_space=pltpu.SMEM),
            pl.BlockSpec((group, step, width), lambda g: (g, 0, 0)),
            kind_spec(step),
            pl.BlockSpec(memory_space=pltpu.VMEM),
        ],
        out_specs=[half] * 2,
        compiler_params=pltpu.CompilerParams(vmem_limit_bytes=VMEM_LIMIT),
        cost_estimate=pl.CostEstimate(
            flops=2 * count * step * weights.size, bytes_accessed=2 * upstream.size, transcendentals=0
        ),
        name="project_back",
    )(me, upstream, kinds, weights)


def project_kernel(me_ref, own_ref, other_ref, kind_ref, w_ref, out_ref):
    count, step, _ = own_ref.shape
    me = me_ref[0]
    rows = []
    for b in range(count):
        mask = is_image(kind_ref, me, b)
        parts = [ref[b].astype(jnp.float32) for ref in (own_ref, other_ref)]
        masked = [jnp.where(mask, 0.0, p) for p in parts] + [jnp.where(mask, p, 0.0) for p in parts]
        rows.append(jnp.concatenate(masked, axis=1))
    left = jnp.concatenate(rows, axis=0).astype(jnp.bfloat16)
    right = jnp.concatenate(pair_rows(w_ref, 0, me) + pair_rows(w_ref, 1, me), axis=0)
    out_ref[...] = mm(left, right).astype(out_ref.dtype)


def project(me, own, other, kinds, weights, group=4):
    count, step, _ = own.shape
    width = weights.shape[-1]
    half = pl.BlockSpec((group, step, HEAD_SIZE), lambda g: (g, 0, 0))
    return pl.pallas_call(
        project_kernel,
        grid=(count // group,),
        out_shape=jax.ShapeDtypeStruct((count * step, width), jnp.bfloat16),
        in_specs=[
            pl.BlockSpec(memory_space=pltpu.SMEM),
            half,
            half,
            kind_spec(step),
            pl.BlockSpec(memory_space=pltpu.VMEM),
        ],
        out_specs=pl.BlockSpec((group * step, width), lambda g: (g, 0)),
        compiler_params=pltpu.CompilerParams(vmem_limit_bytes=VMEM_LIMIT),
        cost_estimate=pl.CostEstimate(
            flops=2 * count * step * weights.size,
            bytes_accessed=2 * count * step * width,
            transcendentals=0,
        ),
        name="project",
    )(me, own, other, kinds, weights)


CTX = ("z", "yh", "x")


def exchange(blocks, axis):
    return lax.all_to_all(blocks, axis, split_axis=0, concat_axis=0, tiled=True)


def per_device(query_proj, key_proj, value_proj, modality, out_weight, grad_projected):
    step = query_proj.shape[1]
    me = lax.axis_index("yh").astype(jnp.int32).reshape(1)
    partner = [(0, 1), (1, 0)]
    swap = [(f * 4 + x, x * 4 + f) for f in range(4) for x in range(4)]

    upstream = lax.all_gather(grad_projected[0], ("z", "x"), axis=0)
    shard = lax.ppermute(out_weight, ("fsdp", "x"), swap)

    packed = pack_heads((query_proj[0], key_proj[0], value_proj[0]), modality)
    qkv = exchange(packed.reshape(32, *packed.shape[3:]), CTX)
    kinds = qkv.reshape(packed.shape)
    shard, qkv = lax.optimization_barrier((shard, qkv))
    weights = exchange(jnp.broadcast_to(shard, (8, *shard.shape)), ("fsdp", "yh"))
    weights = weights.reshape(4, 2, *shard.shape)

    attention, own, other, lse = attend_forward(me, qkv, FWD_ROWS)
    other = lax.ppermute(other, "yh", partner)
    partial = project(me, own, other, kinds, weights)
    projected = lax.psum_scatter(partial, ("z", "x"), scatter_dimension=0, tiled=True)
    upstream, partial = lax.optimization_barrier((upstream, partial))
    grad_own, grad_other = project_back(me, upstream, kinds, weights)
    grad_other = lax.ppermute(grad_other, "yh", partner)

    grads = attend_backward(me, qkv, attention, lse, grad_own, grad_other, BWD_ROWS)
    grads = exchange(grads, CTX).reshape(4, 2, 4, *grads.shape[1:])
    grad_query, grad_key, grad_value = unpack_heads(grads)
    return projected[None], grad_query[None], grad_key[None], grad_value[None]


def solution(mesh):
    grid = jax.sharding.Mesh(mesh.devices.reshape(-1, 4, 2, 4), ("fsdp", *CTX))
    rows = P("fsdp", CTX, None)
    placed = (rows, rows, rows, P("fsdp", CTX), P(None, ("fsdp", *CTX), None), rows)
    return jax.shard_map(
        per_device,
        mesh=grid,
        in_specs=placed,
        out_specs=(rows,) * 4,
        check_vma=False,
    )
```

time: 307 us -> 261 us (0.85); the launches traced: 303 us -> 260 us
  waiting for transfers between devices: 101 us -> 77.4 us
  starting transfers between devices: 30.5 us -> 22.6 us
  Pallas kernels: 89.8 us -> 83.8 us
  other arithmetic: 4.54 us -> 0 us
    all_to_all x6 -> x2, waiting for transfers between devices: 101 us -> 50.5 us  [exchange(): return lax.all_to_all(blocks, axis, split_axis=0, concat_axis=0, tiled=True)]
    ppermute x0 -> x3, waiting for transfers between devices: none -> 26.3 us  [the longest x1 13.4 us: per_device(): other = lax.ppermute(other, 'yh', partner)]
    all_to_all x6 -> x2, starting transfers between devices: 30.5 us -> 15.2 us  [exchange(): return lax.all_to_all(blocks, axis, split_axis=0, concat_axis=0, tiled=True)]
    all_to_all x2 -> x1, blocking collectives: 43.8 us -> 58.9 us  [exchange(): return lax.all_to_all(blocks, axis, split_axis=0, concat_axis=0, tiled=True)]
    all_gather x1 -> x0, blocking collectives: 13.5 us -> none  [per_device(): pair = lax.all_gather(out_weight, 'yh', axis=0)]
    ppermute x0 -> x3, starting transfers between devices: none -> 7.28 us  [the longest x1 3.35 us: per_device(): other = lax.ppermute(other, 'yh', partner)]
  transfers between devices with their start and end apart: 7 -> 7, of which waited for: 5 -> 3; matrix products, arithmetic and copies ran while one was open for 2% -> 1% of each run, Pallas kernels for 28% -> 32%
where the time goes in v2:
time: 261 us; the launch traced here: 260 us
  Pallas kernels  83.8 us (32%)
  waiting for transfers between devices  77.4 us (30%)
  blocking collectives  58.9 us (23%)
  starting transfers between devices  22.6 us (9%)
  between operations  14.1 us (5%)
  local copies, waits for them, and re-layouts  3.38 us (1%)
    all_to_all x1, blocking collectives, exchange(): return lax.all_to_all(blocks, axis, split_axis=0, concat_axis=0, tiled=True)  58.9 us
    all_to_all x2, waiting for transfers between devices, exchange(): return lax.all_to_all(blocks, axis, split_axis=0, concat_axis=0, tiled=True)  50.5 us
    pallas_call x1, Pallas kernels, attend_backward(): pl.pallas_call(functools.partial(bwd_kernel, rows=rows), out_shape=jax.Sh...  32.4 us
    pallas_call x1, Pallas kernels, attend_forward(): pl.pallas_call(functools.partial(fwd_kernel, rows=rows), out_shape=(jax.S...  21.6 us
    all_to_all x2, starting transfers between devices, exchange(): return lax.all_to_all(blocks, axis, split_axis=0, concat_axis=0, tiled=True)  15.2 us
    ppermute x1, waiting for transfers between devices, per_device(): other = lax.ppermute(other, 'yh', partner)  13.4 us
    ppermute x1, waiting for transfers between devices, per_device(): grad_other = lax.ppermute(grad_other, 'yh', partner)  12.9 us
    pallas_call x1, Pallas kernels, project_back(): pl.pallas_call(project_back_kernel, grid=(count // group,), out_shape=[ja...  8.65 us
  transfers between devices with their start and end apart: 7, of which 3 were waited for; matrix products, arithmetic and copies ran while one was open for 1% of the time, Pallas kernels for 32%

profile of v2, /device:TPU:0, one launch (start us, length us, event | category | flops | bytes accessed | tf_op | source)
XLA Modules:
  0.0 260.1 jit_solution(12409585065564751828)
XLA Ops:
  7.2 0.0 all-gather.2.cloned.1.call-start
  7.2 0.7 all-gather.2.cloned.1.call-update
  7.9 6.5 %pack_heads.1 = bf16[4,2,4,400,128]{4,3,2,1,0:T(8,128)(2,1)} custom-call(bf16[128,4096]{1,0:T(8,128)(2,1)} %bitcast.16, bf16[128,4096]{1,0:T(8,128)(2,1)} %bitcast.17, bf16[128,4096]{1,0:T(8,128)(2,1)} %bitcast.18, s32[1,128]{1,0:T(1,128)} %kind_ref.1), custom_call_target="tpu_custom_call" | custom-call | tf_op jit(solution)/shard_map/pack_heads/pallas_call | solution.py:226
  14.4 10.9 %all-to-all-start = ((bf16[32,400,128]{2,1,0:T(8,128)(2,1)}), bf16[32,400,128]{2,1,0:T(8,128)(2,1)S(1)}, u32[]{:S(2)}, u32[]{:S(2)}) async-start(bf16[32,400,128]{2,1,0:T(8,128)(2,1)} %bitcast.12), calls=%async_computation | async-start | bytes 6553600 | tf_op jit(solution)/shard_map/all_to_all | solution.py:349
  25.3 1.6 collective-permute-start
  26.9 0.0 collective-permute-done
  26.9 50.5 %all-to-all-done.qkv_ref = bf16[32,400,128]{2,1,0:T(8,128)(2,1)S(1)} async-done(((bf16[32,400,128]{2,1,0:T(8,128)(2,1)}), bf16[32,400,128]{2,1,0:T(8,128)(2,1)S(1)}, u32[]{:S(2)}, u32[]{:S(2)}) %all-to-all-start) | async-done | bytes 3276832 | tf_op jit(solution)/shard_map/all_to_all | solution.py:349
  77.4 0.0 copy-start
  77.4 1.8 broadcast_in_dim.15
  79.2 4.4 %all-to-all-start.1 = ((bf16[8,2,32,2048]{3,2,1,0:T(8,128)(2,1)}), bf16[8,2,32,2048]{3,2,1,0:T(8,128)(2,1)}, u32[]{:S(2)}, u32[]{:S(2)}) async-start(bf16[8,2,32,2048]{3,2,1,0:T(8,128)(2,1)} %broadcast_in_dim.15), calls=%async_computation.1 | async-start | bytes 4194304 | tf_op jit(solution)/shard_map/all_to_all | solution.py:349
  83.5 0.0 reduce-scatter.2.cloned.1.call-start
  83.6 0.0 copy-done
  83.6 21.6 %attend_forward.1 = (bf16[32,128,128]{2,1,0:T(8,128)(2,1)}, bf16[16,128,128]{2,1,0:T(8,128)(2,1)}, bf16[16,128,128]{2,1,0:T(8,128)(2,1)}, f32[4,1,1024]{2,1,0:T(1,128)}) custom-call(s32[1]{0:T(128)} %bitcast.me_ref, bf16[32,400,128]{2,1,0:T(8,128)(2,1)} %copy-done), custom_call_target="tpu_custom_call" | custom-call | flops 25769803776 | bytes 4194304 | tf_op jit(solution)/shard_map/attend_forward/pallas_call | solution.py:95
  105.2 3.4 %collective-permute-start.1 = (bf16[16,128,128]{2,1,0:T(8,128)(2,1)}, bf16[16,128,128]{2,1,0:T(8,128)(2,1)S(1)}, u32[]{:S(2)}, u32[]{:S(2)}) collective-permute-start(bf16[16,128,128]{2,1,0:T(8,128)(2,1)} %get-tuple-element.18), channel_id=1, source_target_pairs={{0,4},{4,0},{1,5},{5,1},{2,6},{6,2},{3,7},{7,3},{8,12},{12,8},{9,1... | collective-permute-start | bytes 1572872 | tf_op jit(solution)/shard_map/ppermute | solution.py:369
  108.5 13.4 %collective-permute-done.1.other_ref = bf16[16,128,128]{2,1,0:T(8,128)(2,1)S(1)} collective-permute-done((bf16[16,128,128]{2,1,0:T(8,128)(2,1)}, bf16[16,128,128]{2,1,0:T(8,128)(2,1)S(1)}, u32[]{:S(2)}, u32[]{:S(2)}) %collective-permute-start.1) | collective-permute-done | bytes 524320 | tf_op jit(solution)/shard_map/ppermute | solution.py:369
  121.9 0.0 copy-start.2
  121.9 0.0 all-to-all-done.1
  121.9 0.8 copy-done.2
  122.7 8.4 %project.1 = bf16[2048,2048]{1,0:T(8,128)(2,1)} custom-call(s32[1]{0:T(128)} %bitcast.me_ref, bf16[16,128,128]{2,1,0:T(8,128)(2,1)} %get-tuple-element.17.own_ref, bf16[16,128,128]{2,1,0:T(8,128)(2,1)} %copy-done.2, bf16[4,2,4,400,128]{4,3,2,1,0:T(8,128)(2,1)} %bitcast.14, bf16[4,2,2,32,2048]{4,3,2,1,0:T(8,128)(2,1)} %bitcast.6.w_ref), custom_call_target="tpu_custom_call" | custom-call | flops 4294967296 | bytes 8388608 | tf_op jit(solution)/shard_map/project/pallas_call | solution.py:323
  131.1 0.0 reduce-scatter.2.cloned.1.call-update
  131.1 0.0 all-gather.2.cloned.1.call-done.up_ref
  131.2 8.7 %project_back.1 = (bf16[16,128,128]{2,1,0:T(8,128)(2,1)}, bf16[16,128,128]{2,1,0:T(8,128)(2,1)}) custom-call(s32[1]{0:T(128)} %bitcast.me_ref, bf16[16,128,2048]{2,1,0:T(8,128)(2,1)} %all-gather.2.cloned.1.call-done.up_ref, bf16[4,2,4,400,128]{4,3,2,1,0:T(8,128)(2,1)} %bitcast.15, bf16[4,2,2,32,2048]{4,3,2,1,0:T(8,128)(2,1)} %bitcast.6.w_ref), custom_call_target="tpu_custom_call" | custom-call | flops 4294967296 | bytes 8388608 | tf_op jit(solution)/shard_map/project_back/pallas_call | solution.py:286
  139.8 2.3 collective-permute-start.2
  142.1 12.9 %collective-permute-done.2.other_ref = bf16[16,128,128]{2,1,0:T(8,128)(2,1)S(1)} collective-permute-done((bf16[16,128,128]{2,1,0:T(8,128)(2,1)}, bf16[16,128,128]{2,1,0:T(8,128)(2,1)S(1)}, u32[]{:S(2)}, u32[]{:S(2)}) %collective-permute-start.2) | collective-permute-done | bytes 524320 | tf_op jit(solution)/shard_map/ppermute | solution.py:374
  155.0 0.0 copy-start.1
  155.0 0.8 copy-done.1
  155.8 32.4 %attend_backward.1 = bf16[32,3,128,128]{3,2,1,0:T(8,128)(2,1)} custom-call(s32[1]{0:T(128)} %bitcast.me_ref, bf16[32,400,128]{2,1,0:T(8,128)(2,1)} %copy-done, bf16[32,128,128]{2,1,0:T(8,128)(2,1)} %get-tuple-element.20.out_ref, f32[4,1,1024]{2,1,0:T(1,128)} %get-tuple-element.21.lse_ref, bf16[16,128,128]{2,1,0:T(8,128)(2,1)} %get-tuple-element.23.own_ref, ...), custom_call_target="tpu_custom_call" | custom-call | flops 42949672960 | bytes 8388608 | tf_op jit(solution)/shard_map/attend_backward/pallas_call | solution.py:183
  188.2 58.9 %all_to_all.15 = bf16[32,3,128,128]{3,2,1,0:T(8,128)(2,1)} all-to-all(bf16[32,3,128,128]{3,2,1,0:T(8,128)(2,1)} %attend_backward.1), channel_id=1, replica_groups=mesh['fsdp'=4,'z'=4,'yh'=2,'x'=4] {'z','yh','x'}, dimensions={0} | all-to-all | bytes 6291456 | tf_op jit(solution)/shard_map/all_to_all | solution.py:349
  247.0 6.3 %unpack_heads.1 = (bf16[128,4096]{1,0:T(8,128)(2,1)}, bf16[128,4096]{1,0:T(8,128)(2,1)}, bf16[128,4096]{1,0:T(8,128)(2,1)}) custom-call(bf16[4,2,4,3,128,128]{5,4,3,2,1,0:T(8,128)(2,1)} %bitcast.13), custom_call_target="tpu_custom_call" | custom-call | tf_op jit(solution)/shard_map/unpack_heads/pallas_call | solution.py:246
  253.3 0.0 reduce-scatter.2.cloned.1.call-done
Async XLA Ops:
  7.2 124.0 %all-gather.2.cloned.1.call-start = ((), (), s32[]{:S(2)}) async-start(), calls=%async_computation.5 | async-start | bytes 8912896 | tf_op jit(solution)/shard_map/all_gather | solution.py:358
  14.4 63.0 %all-to-all-start = ((bf16[32,400,128]{2,1,0:T(8,128)(2,1)}), bf16[32,400,128]{2,1,0:T(8,128)(2,1)S(1)}, u32[]{:S(2)}, u32[]{:S(2)}) async-start(bf16[32,400,128]{2,1,0:T(8,128)(2,1)} %bitcast.12), calls=%async_computation | async-start | bytes 6553600 | tf_op jit(solution)/shard_map/all_to_all | solution.py:349
  25.3 1.6 collective-permute-start
  77.4 6.2 %copy-start = (bf16[32,400,128]{2,1,0:T(8,128)(2,1)}, bf16[32,400,128]{2,1,0:T(8,128)(2,1)S(1)}, u32[]{:S(2)}) copy-start(bf16[32,400,128]{2,1,0:T(8,128)(2,1)S(1)} %all-to-all-done.qkv_ref) | copy-start | bytes 9830404
  79.2 42.8 %all-to-all-start.1 = ((bf16[8,2,32,2048]{3,2,1,0:T(8,128)(2,1)}), bf16[8,2,32,2048]{3,2,1,0:T(8,128)(2,1)}, u32[]{:S(2)}, u32[]{:S(2)}) async-start(bf16[8,2,32,2048]{3,2,1,0:T(8,128)(2,1)} %broadcast_in_dim.15), calls=%async_computation.1 | async-start | bytes 4194304 | tf_op jit(solution)/shard_map/all_to_all | solution.py:349
  83.5 169.7 %reduce-scatter.2.cloned.1.call-start = ((), (), s32[]{:S(2)}) async-start(), calls=%async_computation.4 | async-start | bytes 8912896 | tf_op jit(solution)/shard_map/reduce_scatter | solution.py:371
  105.2 16.7 %collective-permute-start.1 = (bf16[16,128,128]{2,1,0:T(8,128)(2,1)}, bf16[16,128,128]{2,1,0:T(8,128)(2,1)S(1)}, u32[]{:S(2)}, u32[]{:S(2)}) collective-permute-start(bf16[16,128,128]{2,1,0:T(8,128)(2,1)} %get-tuple-element.18), channel_id=1, source_target_pairs={{0,4},{4,0},{1,5},{5,1},{2,6},{6,2},{3,7},{7,3},{8,12},{12,8},{9,1... | collective-permute-start | bytes 1572872 | tf_op jit(solution)/shard_map/ppermute | solution.py:369
  121.9 0.8 copy-start.2
  139.8 15.2 %collective-permute-start.2 = (bf16[16,128,128]{2,1,0:T(8,128)(2,1)}, bf16[16,128,128]{2,1,0:T(8,128)(2,1)S(1)}, u32[]{:S(2)}, u32[]{:S(2)}) collective-permute-start(bf16[16,128,128]{2,1,0:T(8,128)(2,1)} %get-tuple-element.24), channel_id=1, source_target_pairs={{0,4},{4,0},{1,5},{5,1},{2,6},{6,2},{3,7},{7,3},{8,12},{12,8},{9,1... | collective-permute-start | bytes 1572872 | tf_op jit(solution)/shard_map/ppermute | solution.py:374
  155.0 0.8 copy-start.1
Sparse Core Ops, SparseCore 0:
  10.1 106.6 all-gather.1
  131.3 112.3 reduce-scatter.1

commit v3 on v2

--- a/solution.py
+++ b/solution.py
@@ -13,7 +13,7 @@
 FWD_ROWS = 1024
 BWD_ROWS = 1024
 KIND_ROWS = 16
-PACK = 2
+PACK = 4
 
 
 def mm(a, b, dims=(((1,), (0,)), ((), ()))):
@@ -25,13 +25,16 @@
     return keys + shift <= lax.broadcasted_iota(jnp.int32, shape, 1 - key_dim)
 
 
-def fwd_kernel(me_ref, qkv_ref, out_ref, own_ref, other_ref, lse_ref, s_ref, *, rows):
+def fwd_kernel(
+    me_ref, qkv_ref, out_ref, own_ref, other_ref, lse_ref, even_ref, odd_ref, total_ref, acc_ref, *, rows
+):
     blocks = qkv_ref.shape[0]
     step = HEAD_SIZE
     per = rows // step
     count = blocks // per
     half = rows // 2
     factor = HEAD_SIZE**-0.5 * LOG2E
+    stores = (even_ref, odd_ref)
 
     def get(which, first, size):
         part = qkv_ref[pl.ds(first, size // step), which * step : (which + 1) * step]
@@ -42,46 +45,58 @@
             start = op(start, s[:, c : c + HEAD_SIZE])
         return start
 
-    def query_block(i, _):
-        query = get(0, i * per, rows)
-
-        def scores(j, top):
-            s = mm(query, get(1, j * per, rows), NT)
-            s_ref[j] = s
-            return fold(jnp.maximum, top, s)
-
-        top = lax.fori_loop(0, i, scores, jnp.full((rows, HEAD_SIZE), -jnp.inf, jnp.float32))
+    def scores(i, j, top):
+        s = mm(get(0, i * per, rows), get(1, j * per, rows), NT) * factor
+        stores[i % 2][j] = s
+        return fold(jnp.maximum, top, s)
+
+    def values(i, j, high):
+        p = jnp.exp2(stores[i % 2][j] - high)
+        total_ref[...] = fold(jnp.add, total_ref[...], p)
+        acc_ref[...] += mm(p.astype(jnp.bfloat16), get(2, j * per, rows))
+
+    def last_scores(i, top):
         highs = []
         for part in range(2):
             size = half * (part + 1)
             at = slice(part * half, (part + 1) * half)
-            s = mm(query[at], get(1, i * per, size), NT)
+            s = mm(get(0, i * per + part * per // 2, half), get(1, i * per, size), NT) * factor
             s = jnp.where(visible(s.shape, 1, -part * half), s, -jnp.inf)
-            s_ref[i, at, :size] = s
-            highs.append(jnp.max(fold(jnp.maximum, top[at], s), axis=1, keepdims=True) * factor)
-        high = jnp.concatenate(highs, axis=0)
-
-        def values(j, carry):
-            total, acc = carry
-            p = jnp.exp2(s_ref[j] * factor - high)
-            total = fold(jnp.add, total, p)
-            return total, acc + mm(p.astype(jnp.bfloat16), get(2, j * per, rows))
-
-        zero = jnp.zeros((rows, HEAD_SIZE), jnp.float32)
-        totals, accs = lax.fori_loop(0, i, values, (zero, zero))
+            stores[i % 2][i, at, :size] = s
+            highs.append(jnp.max(fold(jnp.maximum, top[at], s), axis=1, keepdims=True))
+        return highs
+
+    def last_values(i, highs):
         for part in range(2):
             size = half * (part + 1)
             at = slice(part * half, (part + 1) * half)
-            p = jnp.exp2(s_ref[i, at, :size] * factor - highs[part])
-            total = jnp.sum(fold(jnp.add, totals[at], p), axis=1, keepdims=True)
-            acc = accs[at] + mm(p.astype(jnp.bfloat16), get(2, i * per, size))
+            p = jnp.exp2(stores[i % 2][i, at, :size] - highs[part])
+            total = jnp.sum(fold(jnp.add, total_ref[at], p), axis=1, keepdims=True)
+            acc = acc_ref[at] + mm(p.astype(jnp.bfloat16), get(2, i * per, size))
             out = (acc / total).astype(jnp.bfloat16)
-            out_ref[pl.ds(i * per + part * per // 2, per // 2)] = out.reshape(-1, step, HEAD_SIZE)
+            first = i * per + part * per // 2
+            out_ref[first : first + per // 2] = out.reshape(-1, step, HEAD_SIZE)
             lse = jnp.broadcast_to(highs[part] + jnp.log2(total), (half, HEAD_SIZE))
             lse_ref[i, :, at] = lse.T[0:1]
-        return 0
-
-    lax.fori_loop(0, count, query_block, 0)
+
+    low = jnp.full((rows, HEAD_SIZE), -jnp.inf, jnp.float32)
+    highs = last_scores(0, low)
+    for i in range(count):
+        total_ref[...] = jnp.zeros_like(total_ref)
+        acc_ref[...] = jnp.zeros_like(acc_ref)
+        high = jnp.concatenate(highs, axis=0)
+        top = low
+
+        def both(j, top):
+            values(i, j, high)
+            return scores(i + 1, j, top) if i + 1 < count else top
+
+        top = lax.fori_loop(0, i, both, top)
+        if i + 1 < count:
+            top = scores(i + 1, i, top)
+        last_values(i, highs)
+        if i + 1 < count:
+            highs = last_scores(i + 1, top)
     me = me_ref[0]
     half = blocks // 8
     for z in range(4):
@@ -105,7 +120,11 @@
             pl.BlockSpec(memory_space=pltpu.VMEM),
         ],
         out_specs=[pl.BlockSpec(memory_space=pltpu.VMEM)] * 4,
-        scratch_shapes=[pltpu.VMEM((length // rows, rows, rows), jnp.float32)],
+        scratch_shapes=[
+            pltpu.VMEM((length // rows - 1, rows, rows), jnp.float32),
+            pltpu.VMEM((length // rows, rows, rows), jnp.float32),
+        ]
+        + [pltpu.VMEM((rows, HEAD_SIZE), jnp.float32)] * 2,
         compiler_params=pltpu.CompilerParams(vmem_limit_bytes=VMEM_LIMIT),
         cost_estimate=pl.CostEstimate(
             flops=12 * length * length * HEAD_SIZE,
@@ -355,10 +374,9 @@
     partner = [(0, 1), (1, 0)]
     swap = [(f * 4 + x, x * 4 + f) for f in range(4) for x in range(4)]
 
+    packed = pack_heads((query_proj[0], key_proj[0], value_proj[0]), modality)
     upstream = lax.all_gather(grad_projected[0], ("z", "x"), axis=0)
     shard = lax.ppermute(out_weight, ("fsdp", "x"), swap)
-
-    packed = pack_heads((query_proj[0], key_proj[0], value_proj[0]), modality)
     qkv = exchange(packed.reshape(32, *packed.shape[3:]), CTX)
     kinds = qkv.reshape(packed.shape)
     shard, qkv = lax.optimization_barrier((shard, qkv))

time: 261 us -> 257 us (0.985)
  Pallas kernels: 83.8 us -> 75.8 us
  waiting for transfers between devices: 77.4 us -> 84.8 us
    ppermute x1, waiting for transfers between devices: 13.4 us -> 17.7 us  [per_device(): other = lax.ppermute(other, 'yh', partner)]
    pallas_call x1, Pallas kernels: 21.6 us -> 17.3 us  [attend_forward(): pl.pallas_call(functools.partial(fwd_kernel, rows=rows), out_shape=(jax.S...]
  transfers between devices with their start and end apart: 7 -> 7, of which waited for: 3 -> 3; matrix products, arithmetic and copies ran while one was open for 1% -> 1% of each run, Pallas kernels for 32% -> 30%
where the time goes in v3:
time: 257 us
  waiting for transfers between devices  84.8 us (33%)
  Pallas kernels  75.8 us (29%)
  blocking collectives  57.9 us (23%)
  starting transfers between devices  20.6 us (8%)
  between operations  14.1 us (5%)
  local copies, waits for them, and re-layouts  3.38 us (1%)
    all_to_all x1, blocking collectives, exchange(): return lax.all_to_all(blocks, axis, split_axis=0, concat_axis=0, tiled=True)  57.9 us
    all_to_all x2, waiting for transfers between devices, exchange(): return lax.all_to_all(blocks, axis, split_axis=0, concat_axis=0, tiled=True)  51.6 us
    pallas_call x1, Pallas kernels, attend_backward(): pl.pallas_call(functools.partial(bwd_kernel, rows=rows), out_shape=jax.Sh...  32.5 us
    ppermute x1, waiting for transfers between devices, per_device(): other = lax.ppermute(other, 'yh', partner)  17.7 us
    pallas_call x1, Pallas kernels, attend_forward(): pl.pallas_call(functools.partial(fwd_kernel, rows=rows), out_shape=(jax.S...  17.3 us
    all_to_all x2, starting transfers between devices, exchange(): return lax.all_to_all(blocks, axis, split_axis=0, concat_axis=0, tiled=True)  15.2 us
    ppermute x1, waiting for transfers between devices, per_device(): grad_other = lax.ppermute(grad_other, 'yh', partner)  14.8 us
    pallas_call x1, Pallas kernels, project_back(): pl.pallas_call(project_back_kernel, grid=(count // group,), out_shape=[ja...  8.65 us
  transfers between devices with their start and end apart: 7, of which 3 were waited for; matrix products, arithmetic and copies ran while one was open for 1% of the time, Pallas kernels for 30%

profile of v3, /device:TPU:0, one launch (start us, length us, event | category | flops | bytes accessed | tf_op | source)
XLA Modules:
  0.0 256.6 jit_solution(2112837859815903538)
XLA Ops:
  7.2 0.0 all-gather.2.cloned.1.call-start
  7.2 0.7 all-gather.2.cloned.1.call-update
  7.9 4.4 %pack_heads.1 = bf16[4,2,4,400,128]{4,3,2,1,0:T(8,128)(2,1)} custom-call(bf16[128,4096]{1,0:T(8,128)(2,1)} %bitcast.16, bf16[128,4096]{1,0:T(8,128)(2,1)} %bitcast.17, bf16[128,4096]{1,0:T(8,128)(2,1)} %bitcast.18, s32[1,128]{1,0:T(1,128)} %kind_ref.1), custom_call_target="tpu_custom_call" | custom-call | tf_op jit(solution)/shard_map/pack_heads/pallas_call | solution.py:245
  12.3 10.9 %all-to-all-start = ((bf16[32,400,128]{2,1,0:T(8,128)(2,1)}), bf16[32,400,128]{2,1,0:T(8,128)(2,1)S(1)}, u32[]{:S(2)}, u32[]{:S(2)}) async-start(bf16[32,400,128]{2,1,0:T(8,128)(2,1)} %bitcast.12), calls=%async_computation | async-start | bytes 6553600 | tf_op jit(solution)/shard_map/all_to_all | solution.py:368
  23.2 1.6 collective-permute-start
  24.8 0.0 collective-permute-done
  24.8 51.6 %all-to-all-done.qkv_ref = bf16[32,400,128]{2,1,0:T(8,128)(2,1)S(1)} async-done(((bf16[32,400,128]{2,1,0:T(8,128)(2,1)}), bf16[32,400,128]{2,1,0:T(8,128)(2,1)S(1)}, u32[]{:S(2)}, u32[]{:S(2)}) %all-to-all-start) | async-done | bytes 3276832 | tf_op jit(solution)/shard_map/all_to_all | solution.py:368
  76.4 0.0 copy-start
  76.4 1.8 broadcast_in_dim.15
  78.2 4.4 %all-to-all-start.1 = ((bf16[8,2,32,2048]{3,2,1,0:T(8,128)(2,1)}), bf16[8,2,32,2048]{3,2,1,0:T(8,128)(2,1)}, u32[]{:S(2)}, u32[]{:S(2)}) async-start(bf16[8,2,32,2048]{3,2,1,0:T(8,128)(2,1)} %broadcast_in_dim.15), calls=%async_computation.1 | async-start | bytes 4194304 | tf_op jit(solution)/shard_map/all_to_all | solution.py:368
  82.6 0.0 reduce-scatter.2.cloned.1.call-start
  82.6 0.0 copy-done
  82.6 17.3 %attend_forward.1 = (bf16[32,128,128]{2,1,0:T(8,128)(2,1)}, bf16[16,128,128]{2,1,0:T(8,128)(2,1)}, bf16[16,128,128]{2,1,0:T(8,128)(2,1)}, f32[4,1,1024]{2,1,0:T(1,128)}) custom-call(s32[1]{0:T(128)} %bitcast.me_ref, bf16[32,400,128]{2,1,0:T(8,128)(2,1)} %copy-done), custom_call_target="tpu_custom_call" | custom-call | flops 25769803776 | bytes 4194304 | tf_op jit(solution)/shard_map/attend_forward/pallas_call | solution.py:110
  99.9 3.3 %collective-permute-start.1 = (bf16[16,128,128]{2,1,0:T(8,128)(2,1)}, bf16[16,128,128]{2,1,0:T(8,128)(2,1)S(1)}, u32[]{:S(2)}, u32[]{:S(2)}) collective-permute-start(bf16[16,128,128]{2,1,0:T(8,128)(2,1)} %get-tuple-element.18), channel_id=1, source_target_pairs={{0,4},{4,0},{1,5},{5,1},{2,6},{6,2},{3,7},{7,3},{8,12},{12,8},{9,1... | collective-permute-start | bytes 1572872 | tf_op jit(solution)/shard_map/ppermute | solution.py:387
  103.3 17.7 %collective-permute-done.1.other_ref = bf16[16,128,128]{2,1,0:T(8,128)(2,1)S(1)} collective-permute-done((bf16[16,128,128]{2,1,0:T(8,128)(2,1)}, bf16[16,128,128]{2,1,0:T(8,128)(2,1)S(1)}, u32[]{:S(2)}, u32[]{:S(2)}) %collective-permute-start.1) | collective-permute-done | bytes 524320 | tf_op jit(solution)/shard_map/ppermute | solution.py:387
  121.0 0.0 copy-start.2
  121.0 0.0 all-to-all-done.1
  121.0 0.8 copy-done.2
  121.8 8.4 %project.1 = bf16[2048,2048]{1,0:T(8,128)(2,1)} custom-call(s32[1]{0:T(128)} %bitcast.me_ref, bf16[16,128,128]{2,1,0:T(8,128)(2,1)} %get-tuple-element.17.own_ref, bf16[16,128,128]{2,1,0:T(8,128)(2,1)} %copy-done.2, bf16[4,2,4,400,128]{4,3,2,1,0:T(8,128)(2,1)} %bitcast.14, bf16[4,2,2,32,2048]{4,3,2,1,0:T(8,128)(2,1)} %bitcast.6.w_ref), custom_call_target="tpu_custom_call" | custom-call | flops 4294967296 | bytes 8388608 | tf_op jit(solution)/shard_map/project/pallas_call | solution.py:342
  130.2 0.0 reduce-scatter.2.cloned.1.call-update
  130.2 0.0 all-gather.2.cloned.1.call-done.up_ref
  130.2 8.7 %project_back.1 = (bf16[16,128,128]{2,1,0:T(8,128)(2,1)}, bf16[16,128,128]{2,1,0:T(8,128)(2,1)}) custom-call(s32[1]{0:T(128)} %bitcast.me_ref, bf16[16,128,2048]{2,1,0:T(8,128)(2,1)} %all-gather.2.cloned.1.call-done.up_ref, bf16[4,2,4,400,128]{4,3,2,1,0:T(8,128)(2,1)} %bitcast.15, bf16[4,2,2,32,2048]{4,3,2,1,0:T(8,128)(2,1)} %bitcast.6.w_ref), custom_call_target="tpu_custom_call" | custom-call | flops 4294967296 | bytes 8388608 | tf_op jit(solution)/shard_map/project_back/pallas_call | solution.py:305
  138.9 0.4 collective-permute-start.2
  139.2 14.8 %collective-permute-done.2.other_ref = bf16[16,128,128]{2,1,0:T(8,128)(2,1)S(1)} collective-permute-done((bf16[16,128,128]{2,1,0:T(8,128)(2,1)}, bf16[16,128,128]{2,1,0:T(8,128)(2,1)S(1)}, u32[]{:S(2)}, u32[]{:S(2)}) %collective-permute-start.2) | collective-permute-done | bytes 524320 | tf_op jit(solution)/shard_map/ppermute | solution.py:392
  154.0 0.0 copy-start.1
  154.0 0.8 copy-done.1
  154.8 32.5 %attend_backward.1 = bf16[32,3,128,128]{3,2,1,0:T(8,128)(2,1)} custom-call(s32[1]{0:T(128)} %bitcast.me_ref, bf16[32,400,128]{2,1,0:T(8,128)(2,1)} %copy-done, bf16[32,128,128]{2,1,0:T(8,128)(2,1)} %get-tuple-element.20.out_ref, f32[4,1,1024]{2,1,0:T(1,128)} %get-tuple-element.21.lse_ref, bf16[16,128,128]{2,1,0:T(8,128)(2,1)} %get-tuple-element.23.own_ref, ...), custom_call_target="tpu_custom_call" | custom-call | flops 42949672960 | bytes 8388608 | tf_op jit(solution)/shard_map/attend_backward/pallas_call | solution.py:202
  187.4 57.9 %all_to_all.15 = bf16[32,3,128,128]{3,2,1,0:T(8,128)(2,1)} all-to-all(bf16[32,3,128,128]{3,2,1,0:T(8,128)(2,1)} %attend_backward.1), channel_id=1, replica_groups=mesh['fsdp'=4,'z'=4,'yh'=2,'x'=4] {'z','yh','x'}, dimensions={0} | all-to-all | bytes 6291456 | tf_op jit(solution)/shard_map/all_to_all | solution.py:368
  245.2 4.5 %unpack_heads.1 = (bf16[128,4096]{1,0:T(8,128)(2,1)}, bf16[128,4096]{1,0:T(8,128)(2,1)}, bf16[128,4096]{1,0:T(8,128)(2,1)}) custom-call(bf16[4,2,4,3,128,128]{5,4,3,2,1,0:T(8,128)(2,1)} %bitcast.13), custom_call_target="tpu_custom_call" | custom-call | tf_op jit(solution)/shard_map/unpack_heads/pallas_call | solution.py:265
  249.7 0.0 reduce-scatter.2.cloned.1.call-done
Async XLA Ops:
  7.2 123.0 %all-gather.2.cloned.1.call-start = ((), (), s32[]{:S(2)}) async-start(), calls=%async_computation.5 | async-start | bytes 8912896 | tf_op jit(solution)/shard_map/all_gather | solution.py:378
  12.3 64.1 %all-to-all-start = ((bf16[32,400,128]{2,1,0:T(8,128)(2,1)}), bf16[32,400,128]{2,1,0:T(8,128)(2,1)S(1)}, u32[]{:S(2)}, u32[]{:S(2)}) async-start(bf16[32,400,128]{2,1,0:T(8,128)(2,1)} %bitcast.12), calls=%async_computation | async-start | bytes 6553600 | tf_op jit(solution)/shard_map/all_to_all | solution.py:368
  23.2 1.6 collective-permute-start
  76.4 6.2 %copy-start = (bf16[32,400,128]{2,1,0:T(8,128)(2,1)}, bf16[32,400,128]{2,1,0:T(8,128)(2,1)S(1)}, u32[]{:S(2)}) copy-start(bf16[32,400,128]{2,1,0:T(8,128)(2,1)S(1)} %all-to-all-done.qkv_ref) | copy-start | bytes 9830404
  78.2 42.8 %all-to-all-start.1 = ((bf16[8,2,32,2048]{3,2,1,0:T(8,128)(2,1)}), bf16[8,2,32,2048]{3,2,1,0:T(8,128)(2,1)}, u32[]{:S(2)}, u32[]{:S(2)}) async-start(bf16[8,2,32,2048]{3,2,1,0:T(8,128)(2,1)} %broadcast_in_dim.15), calls=%async_computation.1 | async-start | bytes 4194304 | tf_op jit(solution)/shard_map/all_to_all | solution.py:368
  82.6 167.1 %reduce-scatter.2.cloned.1.call-start = ((), (), s32[]{:S(2)}) async-start(), calls=%async_computation.4 | async-start | bytes 8912896 | tf_op jit(solution)/shard_map/reduce_scatter | solution.py:389
  99.9 21.0 %collective-permute-start.1 = (bf16[16,128,128]{2,1,0:T(8,128)(2,1)}, bf16[16,128,128]{2,1,0:T(8,128)(2,1)S(1)}, u32[]{:S(2)}, u32[]{:S(2)}) collective-permute-start(bf16[16,128,128]{2,1,0:T(8,128)(2,1)} %get-tuple-element.18), channel_id=1, source_target_pairs={{0,4},{4,0},{1,5},{5,1},{2,6},{6,2},{3,7},{7,3},{8,12},{12,8},{9,1... | collective-permute-start | bytes 1572872 | tf_op jit(solution)/shard_map/ppermute | solution.py:387
  121.0 0.8 copy-start.2
  138.9 15.2 %collective-permute-start.2 = (bf16[16,128,128]{2,1,0:T(8,128)(2,1)}, bf16[16,128,128]{2,1,0:T(8,128)(2,1)S(1)}, u32[]{:S(2)}, u32[]{:S(2)}) collective-permute-start(bf16[16,128,128]{2,1,0:T(8,128)(2,1)} %get-tuple-element.24), channel_id=1, source_target_pairs={{0,4},{4,0},{1,5},{5,1},{2,6},{6,2},{3,7},{7,3},{8,12},{12,8},{9,1... | collective-permute-start | bytes 1572872 | tf_op jit(solution)/shard_map/ppermute | solution.py:392
  154.0 0.8 copy-start.1
Sparse Core Ops, SparseCore 0:
  10.1 105.9 all-gather.1
  130.3 111.7 reduce-scatter.1

commit v4 on v3

--- a/solution.py
+++ b/solution.py
@@ -281,16 +281,23 @@
     return jnp.broadcast_to(row, (row.shape[1], row.shape[1])).T > 0.5
 
 
-def pair_rows(w_ref, kind, me):
-    return [w_ref[:, y, kind].reshape(HEAD_SIZE, w_ref.shape[-1]) for y in (me, 1 - me)]
-
-
-def project_back_kernel(me_ref, up_ref, kind_ref, w_ref, own_ref, other_ref):
+def head_rows(w_ref, kind, turn):
+    rows = [w_ref[jnp.bitwise_xor(turn, x), kind] for x in range(4)]
+    return jnp.concatenate(rows, axis=0)
+
+
+def project_back_kernel(me_ref, up_ref, kind_ref, mine_ref, theirs_ref, own_ref, other_ref):
     count, step, width = up_ref.shape
     me = me_ref[0]
     upstream = up_ref[...].reshape(count * step, width)
-    text = mm(upstream, jnp.concatenate(pair_rows(w_ref, 0, me), axis=0), NT)
-    image = mm(upstream, jnp.concatenate(pair_rows(w_ref, 1, me), axis=0), NT)
+    text, image = [
+        mm(
+            upstream,
+            jnp.concatenate([head_rows(w, k, me_ref[1]) for w in (mine_ref, theirs_ref)], axis=0),
+            NT,
+        )
+        for k in range(2)
+    ]
     for b in range(count):
         mask = is_image(kind_ref, me, b)
         rows = slice(b * step, (b + 1) * step)
@@ -311,17 +318,18 @@
             pl.BlockSpec((group, step, width), lambda g: (g, 0, 0)),
             kind_spec(step),
             pl.BlockSpec(memory_space=pltpu.VMEM),
+            pl.BlockSpec(memory_space=pltpu.VMEM),
         ],
         out_specs=[half] * 2,
         compiler_params=pltpu.CompilerParams(vmem_limit_bytes=VMEM_LIMIT),
         cost_estimate=pl.CostEstimate(
-            flops=2 * count * step * weights.size, bytes_accessed=2 * upstream.size, transcendentals=0
+            flops=4 * count * step * weights[0].size, bytes_accessed=2 * upstream.size, transcendentals=0
         ),
         name="project_back",
-    )(me, upstream, kinds, weights)
-
-
-def project_kernel(me_ref, own_ref, other_ref, kind_ref, w_ref, out_ref):
+    )(me, upstream, kinds, *weights)
+
+
+def project_kernel(me_ref, own_ref, other_ref, kind_ref, mine_ref, theirs_ref, out_ref):
     count, step, _ = own_ref.shape
     me = me_ref[0]
     rows = []
@@ -331,13 +339,14 @@
         masked = [jnp.where(mask, 0.0, p) for p in parts] + [jnp.where(mask, p, 0.0) for p in parts]
         rows.append(jnp.concatenate(masked, axis=1))
     left = jnp.concatenate(rows, axis=0).astype(jnp.bfloat16)
-    right = jnp.concatenate(pair_rows(w_ref, 0, me) + pair_rows(w_ref, 1, me), axis=0)
+    right = [head_rows(w, k, me_ref[1]) for k in range(2) for w in (mine_ref, theirs_ref)]
+    right = jnp.concatenate(right, axis=0)
     out_ref[...] = mm(left, right).astype(out_ref.dtype)
 
 
 def project(me, own, other, kinds, weights, group=4):
     count, step, _ = own.shape
-    width = weights.shape[-1]
+    width = weights[0].shape[-1]
     half = pl.BlockSpec((group, step, HEAD_SIZE), lambda g: (g, 0, 0))
     return pl.pallas_call(
         project_kernel,
@@ -349,16 +358,17 @@
             half,
             kind_spec(step),
             pl.BlockSpec(memory_space=pltpu.VMEM),
+            pl.BlockSpec(memory_space=pltpu.VMEM),
         ],
         out_specs=pl.BlockSpec((group * step, width), lambda g: (g, 0)),
         compiler_params=pltpu.CompilerParams(vmem_limit_bytes=VMEM_LIMIT),
         cost_estimate=pl.CostEstimate(
-            flops=2 * count * step * weights.size,
+            flops=4 * count * step * weights[0].size,
             bytes_accessed=2 * count * step * width,
             transcendentals=0,
         ),
         name="project",
-    )(me, own, other, kinds, weights)
+    )(me, own, other, kinds, *weights)
 
 
 CTX = ("z", "yh", "x")
@@ -370,18 +380,20 @@
 
 def per_device(query_proj, key_proj, value_proj, modality, out_weight, grad_projected):
     step = query_proj.shape[1]
-    me = lax.axis_index("yh").astype(jnp.int32).reshape(1)
+    me = jnp.stack([lax.axis_index("yh"), lax.axis_index("fsdp")]).astype(jnp.int32)
     partner = [(0, 1), (1, 0)]
     swap = [(f * 4 + x, x * 4 + f) for f in range(4) for x in range(4)]
 
+    upstream = lax.all_gather(grad_projected[0], ("z", "x"), axis=0)
+    mine = lax.ppermute(out_weight, ("fsdp", "x"), swap)[None]
+    for bit in (1, 2):
+        sent = lax.ppermute(mine, "fsdp", [(f, f ^ bit) for f in range(4)])
+        mine = jnp.concatenate([mine, sent], axis=0)
+    weights = mine, lax.ppermute(mine, "yh", partner)
+
     packed = pack_heads((query_proj[0], key_proj[0], value_proj[0]), modality)
-    upstream = lax.all_gather(grad_projected[0], ("z", "x"), axis=0)
-    shard = lax.ppermute(out_weight, ("fsdp", "x"), swap)
     qkv = exchange(packed.reshape(32, *packed.shape[3:]), CTX)
     kinds = qkv.reshape(packed.shape)
-    shard, qkv = lax.optimization_barrier((shard, qkv))
-    weights = exchange(jnp.broadcast_to(shard, (8, *shard.shape)), ("fsdp", "yh"))
-    weights = weights.reshape(4, 2, *shard.shape)
 
     attention, own, other, lse = attend_forward(me, qkv, FWD_ROWS)
     other = lax.ppermute(other, "yh", partner)

time: 257 us -> 268 us (1.043)
  starting transfers between devices: 20.6 us -> 71.9 us
  waiting for transfers between devices: 84.8 us -> 41.4 us
  other arithmetic: 0 us -> 3.67 us
    ppermute x1 -> x4, starting transfers between devices: 1.61 us -> 57.5 us  [the longest x2 53.3 us: per_device(): sent = lax.ppermute(mine, 'fsdp', [(f, f ^ bit) for f in range(4)])]
    all_to_all x2 -> x1, waiting for transfers between devices: 51.6 us -> 0.01 us  [exchange(): return lax.all_to_all(blocks, axis, split_axis=0, concat_axis=0, tiled=True)]
    ppermute x1 -> x4, waiting for transfers between devices: 0.01 us -> 18.5 us  [the longest x2 13.3 us: per_device(): sent = lax.ppermute(mine, 'fsdp', [(f, f ^ bit) for f in range(4)])]
    ppermute x1, waiting for transfers between devices: 17.7 us -> 10.1 us  [per_device(): other = lax.ppermute(other, 'yh', partner)]
    all_to_all x2 -> x1, starting transfers between devices: 15.2 us -> 10.9 us  [exchange(): return lax.all_to_all(blocks, axis, split_axis=0, concat_axis=0, tiled=True)]
    concatenate x0 -> x2, other arithmetic: none -> 3.02 us  [per_device(): mine = jnp.concatenate([mine, sent], axis=0)]
    ppermute x1, waiting for transfers between devices: 14.8 us -> 12.1 us  [per_device(): grad_other = lax.ppermute(grad_other, 'yh', partner)]
  transfers between devices with their start and end apart: 7 -> 9, of which waited for: 3 -> 5; matrix products, arithmetic and copies ran while one was open for 1% -> 1% of each run, Pallas kernels for 30% -> 28%
where the time goes in v4:
time: 268 us; the launch traced here: 267 us
  Pallas kernels  76 us (28%)
  starting transfers between devices  71.9 us (27%)
  blocking collectives  56.1 us (21%)
  waiting for transfers between devices  41.4 us (15%)
  between operations  14.1 us (5%)
  local copies, waits for them, and re-layouts  3.95 us (1%)
  other arithmetic  3.67 us (1%)
    all_to_all x1, blocking collectives, exchange(): return lax.all_to_all(blocks, axis, split_axis=0, concat_axis=0, tiled=True)  56.1 us
    ppermute x2, starting transfers between devices, per_device(): sent = lax.ppermute(mine, 'fsdp', [(f, f ^ bit) for f in range(4)])  53.3 us
    pallas_call x1, Pallas kernels, attend_backward(): pl.pallas_call(functools.partial(bwd_kernel, rows=rows), out_shape=jax.Sh...  32.6 us
    pallas_call x1, Pallas kernels, attend_forward(): pl.pallas_call(functools.partial(fwd_kernel, rows=rows), out_shape=(jax.S...  17.4 us
    ppermute x2, waiting for transfers between devices, per_device(): sent = lax.ppermute(mine, 'fsdp', [(f, f ^ bit) for f in range(4)])  13.3 us
    ppermute x1, waiting for transfers between devices, per_device(): grad_other = lax.ppermute(grad_other, 'yh', partner)  12.1 us
    all_to_all x1, starting transfers between devices, exchange(): return lax.all_to_all(blocks, axis, split_axis=0, concat_axis=0, tiled=True)  10.9 us
    ppermute x1, waiting for transfers between devices, per_device(): other = lax.ppermute(other, 'yh', partner)  10.1 us
  transfers between devices with their start and end apart: 9, of which 5 were waited for; matrix products, arithmetic and copies ran while one was open for 1% of the time, Pallas kernels for 28%

profile of v4, /device:TPU:0, one launch (start us, length us, event | category | flops | bytes accessed | tf_op | source)
XLA Modules:
  0.0 267.1 jit_solution(499682232143413271)
XLA Ops:
  7.2 0.0 all-gather.2.cloned.1.call-start
  7.2 0.7 all-gather.2.cloned.1.call-update
  7.9 4.4 %pack_heads.1 = bf16[4,2,4,400,128]{4,3,2,1,0:T(8,128)(2,1)} custom-call(bf16[128,4096]{1,0:T(8,128)(2,1)} %bitcast.17, bf16[128,4096]{1,0:T(8,128)(2,1)} %bitcast.18, bf16[128,4096]{1,0:T(8,128)(2,1)} %bitcast.19, s32[1,128]{1,0:T(1,128)} %kind_ref.1), custom_call_target="tpu_custom_call" | custom-call | tf_op jit(solution)/shard_map/pack_heads/pallas_call | solution.py:245
  12.3 10.9 %all-to-all-start = ((bf16[32,400,128]{2,1,0:T(8,128)(2,1)}), bf16[32,400,128]{2,1,0:T(8,128)(2,1)S(1)}, u32[]{:S(2)}, u32[]{:S(2)}) async-start(bf16[32,400,128]{2,1,0:T(8,128)(2,1)} %bitcast.13), calls=%async_computation | async-start | bytes 6553600 | tf_op jit(solution)/shard_map/all_to_all | solution.py:378
  23.2 0.0 reduce-scatter.2.cloned.1.call-start
  23.2 1.6 collective-permute-start.1
  24.8 0.0 collective-permute-done.1
  24.8 51.2 %collective-permute-start.2 = (bf16[1,2,32,2048]{3,2,1,0:T(8,128)(2,1)S(1)}, bf16[1,2,32,2048]{3,2,1,0:T(8,128)(2,1)S(1)}, u32[]{:S(2)}, u32[]{:S(2)}) collective-permute-start(bf16[1,2,32,2048]{3,2,1,0:T(8,128)(2,1)S(1)} %bitcast.20), channel_id=1, source_target_pairs={{0,32},{32,0},{64,96},{96,64},{1,33},{33,1},{65,97},{97,65},{2,34}... | collective-permute-start | bytes 786440 | tf_op jit(solution)/shard_map/ppermute | solution.py:390
  76.1 1.2 collective-permute-done.2
  77.2 0.0 copy-start.1
  77.2 0.7 copy-done.1
  77.9 0.8 pad_maximum_fusion.1
  78.8 2.1 collective-permute-start.3
  80.8 0.6 pad_add_fusion.me_ref
  81.5 12.1 %collective-permute-done.3 = bf16[2,2,32,2048]{3,2,1,0:T(8,128)(2,1)} collective-permute-done((bf16[2,2,32,2048]{3,2,1,0:T(8,128)(2,1)}, bf16[2,2,32,2048]{3,2,1,0:T(8,128)(2,1)}, u32[]{:S(2)}, u32[]{:S(2)}) %collective-permute-start.3) | collective-permute-done | bytes 524320 | tf_op jit(solution)/shard_map/ppermute | solution.py:390
  93.6 2.2 pad_maximum_fusion.mine_ref
  95.8 2.6 collective-permute-start.4
  98.4 0.0 all-to-all-done.qkv_ref
  98.4 0.0 copy-start
  98.4 1.7 copy-done
  100.0 17.4 %attend_forward.1 = (bf16[32,128,128]{2,1,0:T(8,128)(2,1)}, bf16[16,128,128]{2,1,0:T(8,128)(2,1)}, bf16[16,128,128]{2,1,0:T(8,128)(2,1)}, f32[4,1,1024]{2,1,0:T(1,128)}) custom-call(s32[2]{0:T(128)} %pad_add_fusion.me_ref, bf16[32,400,128]{2,1,0:T(8,128)(2,1)} %copy-done), custom_call_target="tpu_custom_call" | custom-call | flops 25769803776 | bytes 4194304 | tf_op jit(solution)/shard_map/attend_forward/pallas_call | solution.py:110
  117.5 0.8 collective-permute-start
  118.3 5.2 %collective-permute-done.4.theirs_ref = bf16[4,2,32,2048]{3,2,1,0:T(8,128)(2,1)} collective-permute-done((bf16[4,2,32,2048]{3,2,1,0:T(8,128)(2,1)}, bf16[4,2,32,2048]{3,2,1,0:T(8,128)(2,1)}, u32[]{:S(2)}, u32[]{:S(2)}) %collective-permute-start.4) | collective-permute-done | bytes 1048608 | tf_op jit(solution)/shard_map/ppermute | solution.py:392
  123.5 10.1 %collective-permute-done.other_ref = bf16[16,128,128]{2,1,0:T(8,128)(2,1)S(1)} collective-permute-done((bf16[16,128,128]{2,1,0:T(8,128)(2,1)}, bf16[16,128,128]{2,1,0:T(8,128)(2,1)S(1)}, u32[]{:S(2)}, u32[]{:S(2)}) %collective-permute-start) | collective-permute-done | bytes 524320 | tf_op jit(solution)/shard_map/ppermute | solution.py:399
  133.6 0.0 copy-start.3
  133.6 0.8 copy-done.3
  134.4 8.4 %project.1 = bf16[2048,2048]{1,0:T(8,128)(2,1)} custom-call(s32[2]{0:T(128)} %pad_add_fusion.me_ref, bf16[16,128,128]{2,1,0:T(8,128)(2,1)} %get-tuple-element.14.own_ref, bf16[16,128,128]{2,1,0:T(8,128)(2,1)} %copy-done.3, bf16[4,2,4,400,128]{4,3,2,1,0:T(8,128)(2,1)} %bitcast.15, bf16[4,2,32,2048]{3,2,1,0:T(8,128)(2,1)} %pad_maximum_fusion.mine_ref, ...), custom_call_target="tpu_custom_call" | custom-call | flops 4294967296 | bytes 8388608 | tf_op jit(solution)/shard_map/project/pallas_call | solution.py:351
  142.8 0.0 reduce-scatter.2.cloned.1.call-update
  142.9 0.0 all-gather.2.cloned.1.call-done.up_ref
  142.9 8.6 %project_back.1 = (bf16[16,128,128]{2,1,0:T(8,128)(2,1)}, bf16[16,128,128]{2,1,0:T(8,128)(2,1)}) custom-call(s32[2]{0:T(128)} %pad_add_fusion.me_ref, bf16[16,128,2048]{2,1,0:T(8,128)(2,1)} %all-gather.2.cloned.1.call-done.up_ref, bf16[4,2,4,400,128]{4,3,2,1,0:T(8,128)(2,1)} %bitcast.16, bf16[4,2,32,2048]{3,2,1,0:T(8,128)(2,1)} %pad_maximum_fusion.mine_ref, ...), custom_call_target="tpu_custom_call" | custom-call | flops 4294967296 | bytes 8388608 | tf_op jit(solution)/shard_map/project_back/pallas_call | solution.py:312
  151.5 2.6 collective-permute-start.5
  154.1 12.1 %collective-permute-done.5.other_ref = bf16[16,128,128]{2,1,0:T(8,128)(2,1)S(1)} collective-permute-done((bf16[16,128,128]{2,1,0:T(8,128)(2,1)}, bf16[16,128,128]{2,1,0:T(8,128)(2,1)S(1)}, u32[]{:S(2)}, u32[]{:S(2)}) %collective-permute-start.5) | collective-permute-done | bytes 524320 | tf_op jit(solution)/shard_map/ppermute | solution.py:404
  166.2 0.0 copy-start.2
  166.2 0.8 copy-done.2
  167.0 32.6 %attend_backward.1 = bf16[32,3,128,128]{3,2,1,0:T(8,128)(2,1)} custom-call(s32[2]{0:T(128)} %pad_add_fusion.me_ref, bf16[32,400,128]{2,1,0:T(8,128)(2,1)} %copy-done, bf16[32,128,128]{2,1,0:T(8,128)(2,1)} %get-tuple-element.16.out_ref, f32[4,1,1024]{2,1,0:T(1,128)} %get-tuple-element.17.lse_ref, bf16[16,128,128]{2,1,0:T(8,128)(2,1)} %get-tuple-element.19.own_ref, ...), custom_call_target="tpu_custom_call" | custom-call | flops 42949672960 | bytes 8388608 | tf_op jit(solution)/shard_map/attend_backward/pallas_call | solution.py:202
  199.6 56.1 %all_to_all.10 = bf16[32,3,128,128]{3,2,1,0:T(8,128)(2,1)} all-to-all(bf16[32,3,128,128]{3,2,1,0:T(8,128)(2,1)} %attend_backward.1), channel_id=1, replica_groups=mesh['fsdp'=4,'z'=4,'yh'=2,'x'=4] {'z','yh','x'}, dimensions={0} | all-to-all | bytes 6291456 | tf_op jit(solution)/shard_map/all_to_all | solution.py:378
  255.8 4.5 %unpack_heads.1 = (bf16[128,4096]{1,0:T(8,128)(2,1)}, bf16[128,4096]{1,0:T(8,128)(2,1)}, bf16[128,4096]{1,0:T(8,128)(2,1)}) custom-call(bf16[4,2,4,3,128,128]{5,4,3,2,1,0:T(8,128)(2,1)} %bitcast.14), custom_call_target="tpu_custom_call" | custom-call | tf_op jit(solution)/shard_map/unpack_heads/pallas_call | solution.py:265
  260.3 0.0 reduce-scatter.2.cloned.1.call-done
Async XLA Ops:
  7.2 135.7 %all-gather.2.cloned.1.call-start = ((), (), s32[]{:S(2)}) async-start(), calls=%async_computation.4 | async-start | bytes 8912896 | tf_op jit(solution)/shard_map/all_gather | solution.py:387
  12.3 86.1 %all-to-all-start = ((bf16[32,400,128]{2,1,0:T(8,128)(2,1)}), bf16[32,400,128]{2,1,0:T(8,128)(2,1)S(1)}, u32[]{:S(2)}, u32[]{:S(2)}) async-start(bf16[32,400,128]{2,1,0:T(8,128)(2,1)} %bitcast.13), calls=%async_computation | async-start | bytes 6553600 | tf_op jit(solution)/shard_map/all_to_all | solution.py:378
  23.2 237.1 %reduce-scatter.2.cloned.1.call-start = ((), (), s32[]{:S(2)}) async-start(), calls=%async_computation.3 | async-start | bytes 8912896 | tf_op jit(solution)/shard_map/reduce_scatter | solution.py:401
  23.2 1.6 collective-permute-start.1
  24.8 52.4 %collective-permute-start.2 = (bf16[1,2,32,2048]{3,2,1,0:T(8,128)(2,1)S(1)}, bf16[1,2,32,2048]{3,2,1,0:T(8,128)(2,1)S(1)}, u32[]{:S(2)}, u32[]{:S(2)}) collective-permute-start(bf16[1,2,32,2048]{3,2,1,0:T(8,128)(2,1)S(1)} %bitcast.20), channel_id=1, source_target_pairs={{0,32},{32,0},{64,96},{96,64},{1,33},{33,1},{65,97},{97,65},{2,34}... | collective-permute-start | bytes 786440 | tf_op jit(solution)/shard_map/ppermute | solution.py:390
  77.2 0.7 copy-start.1
  78.8 14.8 %collective-permute-start.3 = (bf16[2,2,32,2048]{3,2,1,0:T(8,128)(2,1)}, bf16[2,2,32,2048]{3,2,1,0:T(8,128)(2,1)}, u32[]{:S(2)}, u32[]{:S(2)}) collective-permute-start(bf16[2,2,32,2048]{3,2,1,0:T(8,128)(2,1)} %pad_maximum_fusion.1), channel_id=1, source_target_pairs={{0,64},{32,96},{64,0},{96,32},{1,65},{33,97},{65,1},{97,33},{2,66}... | collective-permute-start | bytes 1572872 | tf_op jit(solution)/shard_map/ppermute | solution.py:390
  95.8 27.7 %collective-permute-start.4 = (bf16[4,2,32,2048]{3,2,1,0:T(8,128)(2,1)}, bf16[4,2,32,2048]{3,2,1,0:T(8,128)(2,1)}, u32[]{:S(2)}, u32[]{:S(2)}) collective-permute-start(bf16[4,2,32,2048]{3,2,1,0:T(8,128)(2,1)} %pad_maximum_fusion.mine_ref), channel_id=1, source_target_pairs={{0,4},{4,0},{1,5},{5,1},{2,6},{6,2},{3,7},{7,3},{8,12},{12,8},{9,1... | collective-permute-start | bytes 3145736 | tf_op jit(solution)/shard_map/ppermute | solution.py:392
  98.4 1.7 copy-start
  117.5 16.2 %collective-permute-start = (bf16[16,128,128]{2,1,0:T(8,128)(2,1)}, bf16[16,128,128]{2,1,0:T(8,128)(2,1)S(1)}, u32[]{:S(2)}, u32[]{:S(2)}) collective-permute-start(bf16[16,128,128]{2,1,0:T(8,128)(2,1)} %get-tuple-element.15), channel_id=1, source_target_pairs={{0,4},{4,0},{1,5},{5,1},{2,6},{6,2},{3,7},{7,3},{8,12},{12,8},{9,1... | collective-permute-start | bytes 1572872 | tf_op jit(solution)/shard_map/ppermute | solution.py:399
  133.6 0.8 copy-start.3
  151.5 14.7 %collective-permute-start.5 = (bf16[16,128,128]{2,1,0:T(8,128)(2,1)}, bf16[16,128,128]{2,1,0:T(8,128)(2,1)S(1)}, u32[]{:S(2)}, u32[]{:S(2)}) collective-permute-start(bf16[16,128,128]{2,1,0:T(8,128)(2,1)} %get-tuple-element.20), channel_id=1, source_target_pairs={{0,4},{4,0},{1,5},{5,1},{2,6},{6,2},{3,7},{7,3},{8,12},{12,8},{9,1... | collective-permute-start | bytes 1572872 | tf_op jit(solution)/shard_map/ppermute | solution.py:404
  166.2 0.8 copy-start.2
Sparse Core Ops, SparseCore 0:
  10.1 105.9 all-gather.1
  143.0 109.5 reduce-scatter.1

commit v5 on v4

--- a/solution.py
+++ b/solution.py
@@ -135,13 +135,12 @@
     )(me, qkv)
 
 
-def bwd_kernel(
-    me_ref, qkv_ref, out_ref, lse_ref, own_ref, other_ref, res_ref, grad_ref, dq_ref, dk_ref, dv_ref, *, rows
-):
+def bwd_half(y, qkv_ref, out_ref, lse_ref, grad_ref, dq_ref, dk_ref, dv_ref, write, *, rows):
     blocks = qkv_ref.shape[0]
     step = HEAD_SIZE
     per = rows // step
-    count = blocks // per
+    half = per // 2
+    width = rows // 2
     scale = HEAD_SIZE**-0.5
     factor = scale * LOG2E
 
@@ -149,76 +148,109 @@
         part = qkv_ref[pl.ds(first, size // step), which * step : (which + 1) * step]
         return part.reshape(size, HEAD_SIZE)
 
-    me = me_ref[0]
-    half = blocks // 8
-    for z in range(4):
-        grad_ref[pl.ds((2 * z + me) * half, half)] = own_ref[z * half : (z + 1) * half]
-        grad_ref[pl.ds((2 * z + 1 - me) * half, half)] = other_ref[z * half : (z + 1) * half]
+    def query_block(z, _):
+        first = z * per + y * half
+        query = get(0, first, width)
+        grad = grad_ref[pl.ds(z * half, half)].reshape(width, HEAD_SIZE)
+        attn = out_ref[pl.ds(first, half)].reshape(width, HEAD_SIZE)
+        prod = grad.astype(jnp.float32) * attn.astype(jnp.float32)
+        delta = jnp.sum(prod.T, axis=0, keepdims=True)
+        lse = lse_ref[2 * z + y]
+        dq_ref[...] = jnp.zeros_like(dq_ref)
+
+        def key_block(j, size, shift=None):
+            key = get(1, j * per, size)
+            to = pl.ds(j * rows, size)
+            p = jnp.exp2(mm(key, query, NT) * factor - lse)
+            if shift is not None:
+                p = jnp.where(visible(p.shape, 0, shift), p, 0.0)
+            dv_ref[to] += mm(p.astype(jnp.bfloat16), grad)
+            ds = (p * (mm(get(2, j * per, size), grad, NT) - delta) * scale).astype(jnp.bfloat16)
+            dk_ref[to] += mm(ds, query)
+            dq_ref[...] += mm(ds, key, TN)
+
+        def body(j, _):
+            key_block(j, rows)
+            return 0
+
+        lax.fori_loop(0, z, body, 0)
+
+        @pl.when(y == 0)
+        def _():
+            key_block(z, width, 0)
+
+        @pl.when(y == 1)
+        def _():
+            key_block(z, rows, -width)
+
+        write(z, first, dq_ref[...].astype(jnp.bfloat16).reshape(half, step, HEAD_SIZE))
+        return 0
+
+    lax.fori_loop(0, blocks // per, query_block, 0)
+
+
+def bwd_first_kernel(
+    me_ref, qkv_ref, out_ref, lse_ref, grad_ref, done_ref, dk_ref, dv_ref, dq_ref, *, rows
+):
     dk_ref[...] = jnp.zeros_like(dk_ref)
     dv_ref[...] = jnp.zeros_like(dv_ref)
-
-    def query_block(i, _):
-        query = get(0, i * per, rows)
-        grad = grad_ref[pl.ds(i * per, per)].reshape(rows, HEAD_SIZE)
-        attn = out_ref[pl.ds(i * per, per)].reshape(rows, HEAD_SIZE)
-        prod = grad.astype(jnp.float32) * attn.astype(jnp.float32)
-        delta = jnp.sum(prod.T, axis=0, keepdims=True)
-        lse = lse_ref[i]
-        dq_ref[...] = jnp.zeros_like(dq_ref)
-
-        def key_block(j, size, at, shift=None):
-            key = get(1, j * per, size)
-            to = pl.ds(j * rows, size)
-            p = jnp.exp2(mm(key, query[at], NT) * factor - lse[:, at])
-            if shift is not None:
-                p = jnp.where(visible(p.shape, 0, shift), p, 0.0)
-            dv_ref[to] += mm(p.astype(jnp.bfloat16), grad[at])
-            ds = p * (mm(get(2, j * per, size), grad[at], NT) - delta[:, at]) * scale
-            ds = ds.astype(jnp.bfloat16)
-            dk_ref[to] += mm(ds, query[at])
-            dq_ref[at] += mm(ds, key, TN)
-
-        def body(j, _):
-            key_block(j, rows, slice(0, rows))
-            return 0
-
-        lax.fori_loop(0, i, body, 0)
-        middle = rows // 2
-        key_block(i, middle, slice(0, middle), 0)
-        key_block(i, rows, slice(middle, rows), -middle)
-        done = dq_ref[...].astype(jnp.bfloat16).reshape(per, step, HEAD_SIZE)
-        res_ref[pl.ds(i * per, per), 0] = done
-        return 0
-
-    lax.fori_loop(0, count, query_block, 0)
-    res_ref[:, 1] = dk_ref[...].astype(jnp.bfloat16).reshape(blocks, step, HEAD_SIZE)
-    res_ref[:, 2] = dv_ref[...].astype(jnp.bfloat16).reshape(blocks, step, HEAD_SIZE)
+    half = rows // HEAD_SIZE // 2
+
+    def write(z, first, value):
+        done_ref[pl.ds(z * half, half)] = value
+
+    bwd_half(me_ref[0], qkv_ref, out_ref, lse_ref, grad_ref, dq_ref, dk_ref, dv_ref, write, rows=rows)
+
+
+def bwd_second_kernel(
+    me_ref, qkv_ref, out_ref, lse_ref, grad_ref, done_ref, dk_ref, dv_ref, res_ref, dq_ref, *, rows
+):
+    blocks = qkv_ref.shape[0]
+    per = rows // HEAD_SIZE
+    half = per // 2
+    me = me_ref[0]
+    for z in range(blocks // per):
+        res_ref[pl.ds(z * per + me * half, half), 0] = done_ref[z * half : (z + 1) * half]
+
+    def write(z, first, value):
+        res_ref[pl.ds(first, half), 0] = value
+
+    bwd_half(1 - me, qkv_ref, out_ref, lse_ref, grad_ref, dq_ref, dk_ref, dv_ref, write, rows=rows)
+    res_ref[:, 1] = dk_ref[...].astype(jnp.bfloat16).reshape(blocks, HEAD_SIZE, HEAD_SIZE)
+    res_ref[:, 2] = dv_ref[...].astype(jnp.bfloat16).reshape(blocks, HEAD_SIZE, HEAD_SIZE)
 
 
 def attend_backward(me, qkv, out, lse, grad_own, grad_other, rows):
     blocks, step = qkv.shape[0], HEAD_SIZE
     length = blocks * step
-    lse = lse.reshape(length // rows, 1, rows)
-    return pl.pallas_call(
-        functools.partial(bwd_kernel, rows=rows),
-        out_shape=jax.ShapeDtypeStruct((blocks, 3, step, HEAD_SIZE), jnp.bfloat16),
-        in_specs=[pl.BlockSpec(memory_space=pltpu.SMEM)]
-        + [pl.BlockSpec(memory_space=pltpu.VMEM)] * 5,
-        out_specs=pl.BlockSpec(memory_space=pltpu.VMEM),
-        scratch_shapes=[
-            pltpu.VMEM((blocks, step, HEAD_SIZE), jnp.bfloat16),
-            pltpu.VMEM((rows, HEAD_SIZE), jnp.float32),
-            pltpu.VMEM((length, HEAD_SIZE), jnp.float32),
-            pltpu.VMEM((length, HEAD_SIZE), jnp.float32),
-        ],
+    lse = lse.reshape(2 * length // rows, 1, rows // 2)
+    vmem = pl.BlockSpec(memory_space=pltpu.VMEM)
+    common = dict(
+        scratch_shapes=[pltpu.VMEM((rows // 2, HEAD_SIZE), jnp.float32)],
         compiler_params=pltpu.CompilerParams(vmem_limit_bytes=VMEM_LIMIT),
         cost_estimate=pl.CostEstimate(
-            flops=20 * length * length * HEAD_SIZE,
+            flops=10 * length * length * HEAD_SIZE,
             bytes_accessed=16 * length * HEAD_SIZE,
-            transcendentals=length * length // 2,
+            transcendentals=length * length // 4,
         ),
-        name="attend_backward",
-    )(me, qkv, out, lse, grad_own, grad_other)
+    )
+    sums = jax.ShapeDtypeStruct((length, HEAD_SIZE), jnp.float32)
+    done, dk, dv = pl.pallas_call(
+        functools.partial(bwd_first_kernel, rows=rows),
+        out_shape=[jax.ShapeDtypeStruct((blocks // 2, step, HEAD_SIZE), jnp.bfloat16), sums, sums],
+        in_specs=[pl.BlockSpec(memory_space=pltpu.SMEM)] + [vmem] * 4,
+        out_specs=[vmem] * 3,
+        name="backward_own",
+        **common,
+    )(me, qkv, out, lse, grad_own)
+    return pl.pallas_call(
+        functools.partial(bwd_second_kernel, rows=rows),
+        out_shape=jax.ShapeDtypeStruct((blocks, 3, step, HEAD_SIZE), jnp.bfloat16),
+        in_specs=[pl.BlockSpec(memory_space=pltpu.SMEM)] + [vmem] * 7,
+        out_specs=vmem,
+        name="backward_other",
+        **common,
+    )(me, qkv, out, lse, grad_other, done, dk, dv)
 
 
 def pack_kernel(q_ref, k_ref, v_ref, kind_ref, out_ref):
@@ -281,23 +313,36 @@
     return jnp.broadcast_to(row, (row.shape[1], row.shape[1])).T > 0.5
 
 
-def head_rows(w_ref, kind, turn):
-    rows = [w_ref[jnp.bitwise_xor(turn, x), kind] for x in range(4)]
-    return jnp.concatenate(rows, axis=0)
-
-
-def project_back_kernel(me_ref, up_ref, kind_ref, mine_ref, theirs_ref, own_ref, other_ref):
+def assemble(pair_ref, same_ref, cross_ref, core):
+    for low in range(2):
+        for ref, side in ((same_ref, core), (cross_ref, 1 - core)):
+            for y in range(2):
+                pair_ref[:, y, 2 * low + side] = ref[low, y]
+
+
+def pair_rows(pair_ref, kind, me):
+    width = pair_ref.shape[-1]
+    return [pair_ref[kind, y].reshape(HEAD_SIZE, width) for y in (me, 1 - me)]
+
+
+def pair_scratch(weights):
+    _, _, kinds, rows, width = weights[0].shape
+    return pltpu.VMEM((kinds, 2, 4, rows, width), jnp.bfloat16)
+
+
+def project_back_kernel(
+    me_ref, up_ref, kind_ref, same_ref, cross_ref, own_ref, other_ref, pair_ref
+):
     count, step, width = up_ref.shape
     me = me_ref[0]
     upstream = up_ref[...].reshape(count * step, width)
-    text, image = [
-        mm(
-            upstream,
-            jnp.concatenate([head_rows(w, k, me_ref[1]) for w in (mine_ref, theirs_ref)], axis=0),
-            NT,
-        )
-        for k in range(2)
-    ]
+
+    @pl.when(pl.program_id(0) == 0)
+    def _():
+        assemble(pair_ref, same_ref, cross_ref, me_ref[1])
+
+    text = mm(upstream, jnp.concatenate(pair_rows(pair_ref, 0, me), axis=0), NT)
+    image = mm(upstream, jnp.concatenate(pair_rows(pair_ref, 1, me), axis=0), NT)
     for b in range(count):
         mask = is_image(kind_ref, me, b)
         rows = slice(b * step, (b + 1) * step)
@@ -321,6 +366,7 @@
             pl.BlockSpec(memory_space=pltpu.VMEM),
         ],
         out_specs=[half] * 2,
+        scratch_shapes=[pair_scratch(weights)],
         compiler_params=pltpu.CompilerParams(vmem_limit_bytes=VMEM_LIMIT),
         cost_estimate=pl.CostEstimate(
             flops=4 * count * step * weights[0].size, bytes_accessed=2 * upstream.size, transcendentals=0
@@ -329,7 +375,9 @@
     )(me, upstream, kinds, *weights)
 
 
-def project_kernel(me_ref, own_ref, other_ref, kind_ref, mine_ref, theirs_ref, out_ref):
+def project_kernel(
+    me_ref, own_ref, other_ref, kind_ref, same_ref, cross_ref, out_ref, pair_ref
+):
     count, step, _ = own_ref.shape
     me = me_ref[0]
     rows = []
@@ -339,8 +387,12 @@
         masked = [jnp.where(mask, 0.0, p) for p in parts] + [jnp.where(mask, p, 0.0) for p in parts]
         rows.append(jnp.concatenate(masked, axis=1))
     left = jnp.concatenate(rows, axis=0).astype(jnp.bfloat16)
-    right = [head_rows(w, k, me_ref[1]) for k in range(2) for w in (mine_ref, theirs_ref)]
-    right = jnp.concatenate(right, axis=0)
+
+    @pl.when(pl.program_id(0) == 0)
+    def _():
+        assemble(pair_ref, same_ref, cross_ref, me_ref[1])
+
+    right = jnp.concatenate(pair_rows(pair_ref, 0, me) + pair_rows(pair_ref, 1, me), axis=0)
     out_ref[...] = mm(left, right).astype(out_ref.dtype)
 
 
@@ -361,6 +413,7 @@
             pl.BlockSpec(memory_space=pltpu.VMEM),
         ],
         out_specs=pl.BlockSpec((group * step, width), lambda g: (g, 0)),
+        scratch_shapes=[pair_scratch(weights)],
         compiler_params=pltpu.CompilerParams(vmem_limit_bytes=VMEM_LIMIT),
         cost_estimate=pl.CostEstimate(
             flops=4 * count * step * weights[0].size,
@@ -371,6 +424,7 @@
     )(me, own, other, kinds, *weights)
 
 
+FSDP = ("low", "core")
 CTX = ("z", "yh", "x")
 
 
@@ -380,22 +434,22 @@
 
 def per_device(query_proj, key_proj, value_proj, modality, out_weight, grad_projected):
     step = query_proj.shape[1]
-    me = jnp.stack([lax.axis_index("yh"), lax.axis_index("fsdp")]).astype(jnp.int32)
+    me = jnp.stack([lax.axis_index("yh"), lax.axis_index("core")]).astype(jnp.int32)
     partner = [(0, 1), (1, 0)]
     swap = [(f * 4 + x, x * 4 + f) for f in range(4) for x in range(4)]
 
     upstream = lax.all_gather(grad_projected[0], ("z", "x"), axis=0)
-    mine = lax.ppermute(out_weight, ("fsdp", "x"), swap)[None]
-    for bit in (1, 2):
-        sent = lax.ppermute(mine, "fsdp", [(f, f ^ bit) for f in range(4)])
-        mine = jnp.concatenate([mine, sent], axis=0)
-    weights = mine, lax.ppermute(mine, "yh", partner)
-
+    shard = lax.ppermute(out_weight, ("low", "core", "x"), swap)
+    shard = jnp.broadcast_to(shard, (4, *shard.shape))
     packed = pack_heads((query_proj[0], key_proj[0], value_proj[0]), modality)
     qkv = exchange(packed.reshape(32, *packed.shape[3:]), CTX)
     kinds = qkv.reshape(packed.shape)
+    shard, qkv = lax.optimization_barrier((shard, qkv))
+    same = exchange(shard, ("low", "yh")).reshape(2, 2, *out_weight.shape)
 
     attention, own, other, lse = attend_forward(me, qkv, FWD_ROWS)
+    same, other = lax.optimization_barrier((same, other))
+    weights = same, lax.ppermute(same, "core", partner)
     other = lax.ppermute(other, "yh", partner)
     partial = project(me, own, other, kinds, weights)
     projected = lax.psum_scatter(partial, ("z", "x"), scatter_dimension=0, tiled=True)
@@ -410,9 +464,9 @@
 
 
 def solution(mesh):
-    grid = jax.sharding.Mesh(mesh.devices.reshape(-1, 4, 2, 4), ("fsdp", *CTX))
-    rows = P("fsdp", CTX, None)
-    placed = (rows, rows, rows, P("fsdp", CTX), P(None, ("fsdp", *CTX), None), rows)
+    grid = jax.sharding.Mesh(mesh.devices.reshape(2, 2, 4, 2, 4), ("low", "core", *CTX))
+    rows = P(FSDP, CTX, None)
+    placed = (rows, rows, rows, P(FSDP, CTX), P(None, (*FSDP, *CTX), None), rows)
     return jax.shard_map(
         per_device,
         mesh=grid,

time: 268 us -> 250 us (0.933)
  starting transfers between devices: 71.9 us -> 23.6 us
  waiting for transfers between devices: 41.4 us -> 64.4 us
  Pallas kernels: 76 us -> 84.9 us
  other arithmetic: 3.67 us -> 0.61 us
    ppermute x4 -> x2, starting transfers between devices: 57.5 us -> 1.61 us  [the longest x1 1.61 us: per_device(): shard = lax.ppermute(out_weight, ('low', 'core', 'x'), swap)]
    all_to_all x1 -> x2, waiting for transfers between devices: 0.01 us -> 51 us  [exchange(): return lax.all_to_all(blocks, axis, split_axis=0, concat_axis=0, tiled=True)]
    ppermute x4 -> x2, waiting for transfers between devices: 18.5 us -> 0.01 us  [the longest x1 0.01 us: per_device(): shard = lax.ppermute(out_weight, ('low', 'core', 'x'), swap)]
    ppermute x1, waiting for transfers between devices: 12.1 us -> 0.01 us  [per_device(): grad_other = lax.ppermute(grad_other, 'yh', partner)]
    pallas_call x1 -> x2, Pallas kernels: 32.6 us -> 40.7 us  [the longest x1 22 us: attend_backward(): pl.pallas_call(functools.partial(bwd_second_kernel, rows=rows), out_shape...]
    all_to_all x1 -> x2, starting transfers between devices: 10.9 us -> 15.1 us  [exchange(): return lax.all_to_all(blocks, axis, split_axis=0, concat_axis=0, tiled=True)]
    concatenate x2 -> x0, other arithmetic: 3.02 us -> none  [per_device(): mine = jnp.concatenate([mine, sent], axis=0)]
  transfers between devices with their start and end apart: 9 -> 8, of which waited for: 5 -> 2; matrix products, arithmetic and copies ran while one was open for 1% -> 1% of each run, Pallas kernels for 28% -> 34%
where the time goes in v5:
time: 250 us; the launch traced here: 249 us
  Pallas kernels  84.9 us (34%)
  waiting for transfers between devices  64.4 us (26%)
  blocking collectives  58.7 us (23%)
  starting transfers between devices  23.6 us (9%)
  between operations  14.1 us (6%)
  local copies, waits for them, and re-layouts  3.13 us (1%)
    all_to_all x1, blocking collectives, exchange(): return lax.all_to_all(blocks, axis, split_axis=0, concat_axis=0, tiled=True)  58.7 us
    all_to_all x2, waiting for transfers between devices, exchange(): return lax.all_to_all(blocks, axis, split_axis=0, concat_axis=0, tiled=True)  51 us
    pallas_call x1, Pallas kernels, attend_backward(): pl.pallas_call(functools.partial(bwd_second_kernel, rows=rows), out_shape...  22 us
    pallas_call x1, Pallas kernels, attend_backward(): pl.pallas_call(functools.partial(bwd_first_kernel, rows=rows), out_shape=...  18.6 us
    pallas_call x1, Pallas kernels, attend_forward(): pl.pallas_call(functools.partial(fwd_kernel, rows=rows), out_shape=(jax.S...  17.3 us
    all_to_all x2, starting transfers between devices, exchange(): return lax.all_to_all(blocks, axis, split_axis=0, concat_axis=0, tiled=True)  15.1 us
    ppermute x1, waiting for transfers between devices, per_device(): other = lax.ppermute(other, 'yh', partner)  12.7 us
    pallas_call x1, Pallas kernels, project_back(): pl.pallas_call(project_back_kernel, grid=(count // group,), out_shape=[ja...  9.11 us
  transfers between devices with their start and end apart: 8, of which 2 were waited for; matrix products, arithmetic and copies ran while one was open for 1% of the time, Pallas kernels for 34%

profile of v5, /device:TPU:0, one launch (start us, length us, event | category | flops | bytes accessed | tf_op | source)
XLA Modules:
  0.0 249.5 jit_solution(8678058027139581785)
XLA Ops:
  7.2 0.0 all-gather.2.cloned.1.call-start
  7.2 0.7 all-gather.2.cloned.1.call-update
  7.9 4.4 %pack_heads.1 = bf16[4,2,4,400,128]{4,3,2,1,0:T(8,128)(2,1)} custom-call(bf16[128,4096]{1,0:T(8,128)(2,1)} %bitcast.18, bf16[128,4096]{1,0:T(8,128)(2,1)} %bitcast.19, bf16[128,4096]{1,0:T(8,128)(2,1)} %bitcast.20, s32[1,128]{1,0:T(1,128)} %kind_ref.1), custom_call_target="tpu_custom_call" | custom-call | tf_op jit(solution)/shard_map/pack_heads/pallas_call | solution.py:277
  12.3 10.9 %all-to-all-start = ((bf16[32,400,128]{2,1,0:T(8,128)(2,1)}), bf16[32,400,128]{2,1,0:T(8,128)(2,1)S(1)}, u32[]{:S(2)}, u32[]{:S(2)}) async-start(bf16[32,400,128]{2,1,0:T(8,128)(2,1)} %bitcast.14), calls=%async_computation | async-start | bytes 6553600 | tf_op jit(solution)/shard_map/all_to_all | solution.py:432
  23.2 1.6 collective-permute-start
  24.8 0.6 pad_add_fusion.me_ref
  25.4 0.0 collective-permute-done
  25.4 51.0 %all-to-all-done.qkv_ref = bf16[32,400,128]{2,1,0:T(8,128)(2,1)S(1)} async-done(((bf16[32,400,128]{2,1,0:T(8,128)(2,1)}), bf16[32,400,128]{2,1,0:T(8,128)(2,1)S(1)}, u32[]{:S(2)}, u32[]{:S(2)}) %all-to-all-start) | async-done | bytes 3276832 | tf_op jit(solution)/shard_map/all_to_all | solution.py:432
  76.4 0.0 copy-start
  76.4 1.2 broadcast_in_dim.15
  77.6 4.3 %all-to-all-start.1 = ((bf16[4,2,32,2048]{3,2,1,0:T(8,128)(2,1)}), bf16[4,2,32,2048]{3,2,1,0:T(8,128)(2,1)}, u32[]{:S(2)}, u32[]{:S(2)}) async-start(bf16[4,2,32,2048]{3,2,1,0:T(8,128)(2,1)} %broadcast_in_dim.15), calls=%async_computation.1 | async-start | bytes 2097152 | tf_op jit(solution)/shard_map/all_to_all | solution.py:432
  81.9 0.0 reduce-scatter.2.cloned.1.call-start
  81.9 0.0 copy-done
  81.9 17.3 %attend_forward.1 = (bf16[32,128,128]{2,1,0:T(8,128)(2,1)}, bf16[16,128,128]{2,1,0:T(8,128)(2,1)}, bf16[16,128,128]{2,1,0:T(8,128)(2,1)}, f32[4,1,1024]{2,1,0:T(1,128)}) custom-call(s32[2]{0:T(128)} %pad_add_fusion.me_ref, bf16[32,400,128]{2,1,0:T(8,128)(2,1)} %copy-done), custom_call_target="tpu_custom_call" | custom-call | flops 25769803776 | bytes 4194304 | tf_op jit(solution)/shard_map/attend_forward/pallas_call | solution.py:110
  99.2 0.0 all-to-all-done.1
  99.2 0.0 collective-permute-start.2
  99.3 3.5 %collective-permute-start.1 = (bf16[16,128,128]{2,1,0:T(8,128)(2,1)}, bf16[16,128,128]{2,1,0:T(8,128)(2,1)S(1)}, u32[]{:S(2)}, u32[]{:S(2)}) collective-permute-start(bf16[16,128,128]{2,1,0:T(8,128)(2,1)} %get-tuple-element.25), channel_id=1, source_target_pairs={{0,4},{4,0},{1,5},{5,1},{2,6},{6,2},{3,7},{7,3},{8,12},{12,8},{9,1... | collective-permute-start | bytes 1572872 | tf_op jit(solution)/shard_map/ppermute | solution.py:453
  102.8 12.7 %collective-permute-done.1.other_ref = bf16[16,128,128]{2,1,0:T(8,128)(2,1)S(1)} collective-permute-done((bf16[16,128,128]{2,1,0:T(8,128)(2,1)}, bf16[16,128,128]{2,1,0:T(8,128)(2,1)S(1)}, u32[]{:S(2)}, u32[]{:S(2)}) %collective-permute-start.1) | collective-permute-done | bytes 524320 | tf_op jit(solution)/shard_map/ppermute | solution.py:453
  115.5 0.0 copy-start.3
  115.5 0.0 collective-permute-done.2.cross_ref
  115.5 0.0 copy-start.1
  115.5 0.8 copy-done.3
  116.3 0.3 copy-done.1
  116.6 8.9 %project.1 = bf16[2048,2048]{1,0:T(8,128)(2,1)} custom-call(s32[2]{0:T(128)} %pad_add_fusion.me_ref, bf16[16,128,128]{2,1,0:T(8,128)(2,1)} %get-tuple-element.22.own_ref, bf16[16,128,128]{2,1,0:T(8,128)(2,1)} %copy-done.3, bf16[4,2,4,400,128]{4,3,2,1,0:T(8,128)(2,1)} %bitcast.16, bf16[2,2,2,32,2048]{4,3,2,1,0:T(8,128)(2,1)} %bitcast.6.same_ref, ...), custom_call_target="tpu_custom_call" | custom-call | flops 4294967296 | bytes 8388608 | tf_op jit(solution)/shard_map/project/pallas_call | solution.py:403
  125.6 0.0 reduce-scatter.2.cloned.1.call-update
  125.6 0.0 all-gather.2.cloned.1.call-done.up_ref
  125.6 9.1 %project_back.1 = (bf16[16,128,128]{2,1,0:T(8,128)(2,1)}, bf16[16,128,128]{2,1,0:T(8,128)(2,1)}) custom-call(s32[2]{0:T(128)} %pad_add_fusion.me_ref, bf16[16,128,2048]{2,1,0:T(8,128)(2,1)} %all-gather.2.cloned.1.call-done.up_ref, bf16[4,2,4,400,128]{4,3,2,1,0:T(8,128)(2,1)} %bitcast.17, bf16[2,2,2,32,2048]{4,3,2,1,0:T(8,128)(2,1)} %bitcast.6.same_ref, ...), custom_call_target="tpu_custom_call" | custom-call | flops 4294967296 | bytes 8388608 | tf_op jit(solution)/shard_map/project_back/pallas_call | solution.py:357
  134.7 3.3 %collective-permute-start.3 = (bf16[16,128,128]{2,1,0:T(8,128)(2,1)}, bf16[16,128,128]{2,1,0:T(8,128)(2,1)S(1)}, u32[]{:S(2)}, u32[]{:S(2)}) collective-permute-start(bf16[16,128,128]{2,1,0:T(8,128)(2,1)} %get-tuple-element.30), channel_id=1, source_target_pairs={{0,4},{4,0},{1,5},{5,1},{2,6},{6,2},{3,7},{7,3},{8,12},{12,8},{9,1... | collective-permute-start | bytes 1572872 | tf_op jit(solution)/shard_map/ppermute | solution.py:458
  138.0 18.6 %backward_own.1 = (bf16[16,128,128]{2,1,0:T(8,128)(2,1)}, f32[4096,128]{1,0:T(8,128)}, f32[4096,128]{1,0:T(8,128)}) custom-call(s32[2]{0:T(128)} %pad_add_fusion.me_ref, bf16[32,400,128]{2,1,0:T(8,128)(2,1)} %copy-done, bf16[32,128,128]{2,1,0:T(8,128)(2,1)} %get-tuple-element.27.out_ref, f32[8,1,512]{2,1,0:T(1,128)} %bitcast.25, ...), custom_call_target="tpu_custom_call" | custom-call | flops 21474836480 | bytes 8388608 | tf_op jit(solution)/shard_map/backward_own/pallas_call | solution.py:238
  156.6 0.0 collective-permute-done.3.grad_ref
  156.6 0.0 copy-start.2
  156.6 0.8 copy-done.2
  157.4 22.0 %backward_other.1 = bf16[32,3,128,128]{3,2,1,0:T(8,128)(2,1)} custom-call(s32[2]{0:T(128)} %pad_add_fusion.me_ref, bf16[32,400,128]{2,1,0:T(8,128)(2,1)} %copy-done, bf16[32,128,128]{2,1,0:T(8,128)(2,1)} %get-tuple-element.27.out_ref, f32[8,1,512]{2,1,0:T(1,128)} %bitcast.26, bf16[16,128,128]{2,1,0:T(8,128)(2,1)} %copy-done.2, ...), custom_call_target="tpu_custom_call" | custom-call | flops 21474836480 | bytes 8388608 | tf_op jit(solution)/shard_map/backward_other/pallas_call | solution.py:246
  179.4 58.7 %all_to_all.15 = bf16[32,3,128,128]{3,2,1,0:T(8,128)(2,1)} all-to-all(bf16[32,3,128,128]{3,2,1,0:T(8,128)(2,1)} %backward_other.1), channel_id=1, replica_groups=mesh['low'=2,'core'=2,'z'=4,'yh'=2,'x'=4] {'z','yh','x'}, dimensions={0} | all-to-all | bytes 6291456 | tf_op jit(solution)/shard_map/all_to_all | solution.py:432
  238.1 4.5 %unpack_heads.1 = (bf16[128,4096]{1,0:T(8,128)(2,1)}, bf16[128,4096]{1,0:T(8,128)(2,1)}, bf16[128,4096]{1,0:T(8,128)(2,1)}) custom-call(bf16[4,2,4,3,128,128]{5,4,3,2,1,0:T(8,128)(2,1)} %bitcast.15), custom_call_target="tpu_custom_call" | custom-call | tf_op jit(solution)/shard_map/unpack_heads/pallas_call | solution.py:297
  242.6 0.0 reduce-scatter.2.cloned.1.call-done
Async XLA Ops:
  7.2 118.4 %all-gather.2.cloned.1.call-start = ((), (), s32[]{:S(2)}) async-start(), calls=%async_computation.5 | async-start | bytes 8912896 | tf_op jit(solution)/shard_map/all_gather | solution.py:441
  12.3 64.1 %all-to-all-start = ((bf16[32,400,128]{2,1,0:T(8,128)(2,1)}), bf16[32,400,128]{2,1,0:T(8,128)(2,1)S(1)}, u32[]{:S(2)}, u32[]{:S(2)}) async-start(bf16[32,400,128]{2,1,0:T(8,128)(2,1)} %bitcast.14), calls=%async_computation | async-start | bytes 6553600 | tf_op jit(solution)/shard_map/all_to_all | solution.py:432
  23.2 2.2 collective-permute-start
  76.4 5.5 %copy-start = (bf16[32,400,128]{2,1,0:T(8,128)(2,1)}, bf16[32,400,128]{2,1,0:T(8,128)(2,1)S(1)}, u32[]{:S(2)}) copy-start(bf16[32,400,128]{2,1,0:T(8,128)(2,1)S(1)} %all-to-all-done.qkv_ref) | copy-start | bytes 9830404
  77.6 21.7 %all-to-all-start.1 = ((bf16[4,2,32,2048]{3,2,1,0:T(8,128)(2,1)}), bf16[4,2,32,2048]{3,2,1,0:T(8,128)(2,1)}, u32[]{:S(2)}, u32[]{:S(2)}) async-start(bf16[4,2,32,2048]{3,2,1,0:T(8,128)(2,1)} %broadcast_in_dim.15), calls=%async_computation.1 | async-start | bytes 2097152 | tf_op jit(solution)/shard_map/all_to_all | solution.py:432
  81.9 160.8 %reduce-scatter.2.cloned.1.call-start = ((), (), s32[]{:S(2)}) async-start(), calls=%async_computation.4 | async-start | bytes 8912896 | tf_op jit(solution)/shard_map/reduce_scatter | solution.py:455
  99.2 16.2 %collective-permute-start.2 = (bf16[2,2,2,32,2048]{4,3,2,1,0:T(8,128)(2,1)}, bf16[2,2,2,32,2048]{4,3,2,1,0:T(8,128)(2,1)S(1)}, u32[]{:S(2)}, u32[]{:S(2)}) collective-permute-start(bf16[2,2,2,32,2048]{4,3,2,1,0:T(8,128)(2,1)} %bitcast.6.same_ref), channel_id=1, source_target_pairs={{0,32},{32,0},{1,33},{33,1},{2,34},{34,2},{3,35},{35,3},{4,36},{36... | collective-permute-start | bytes 3145736 | tf_op jit(solution)/shard_map/ppermute | solution.py:452
  99.3 16.2 %collective-permute-start.1 = (bf16[16,128,128]{2,1,0:T(8,128)(2,1)}, bf16[16,128,128]{2,1,0:T(8,128)(2,1)S(1)}, u32[]{:S(2)}, u32[]{:S(2)}) collective-permute-start(bf16[16,128,128]{2,1,0:T(8,128)(2,1)} %get-tuple-element.25), channel_id=1, source_target_pairs={{0,4},{4,0},{1,5},{5,1},{2,6},{6,2},{3,7},{7,3},{8,12},{12,8},{9,1... | collective-permute-start | bytes 1572872 | tf_op jit(solution)/shard_map/ppermute | solution.py:453
  115.5 0.8 copy-start.3
  115.5 1.1 copy-start.1
  134.7 21.9 %collective-permute-start.3 = (bf16[16,128,128]{2,1,0:T(8,128)(2,1)}, bf16[16,128,128]{2,1,0:T(8,128)(2,1)S(1)}, u32[]{:S(2)}, u32[]{:S(2)}) collective-permute-start(bf16[16,128,128]{2,1,0:T(8,128)(2,1)} %get-tuple-element.30), channel_id=1, source_target_pairs={{0,4},{4,0},{1,5},{5,1},{2,6},{6,2},{3,7},{7,3},{8,12},{12,8},{9,1... | collective-permute-start | bytes 1572872 | tf_op jit(solution)/shard_map/ppermute | solution.py:458
  156.6 0.8 copy-start.2
Sparse Core Ops, SparseCore 0:
  10.1 105.9 all-gather.1
  125.7 109.9 reduce-scatter.1

commit v6 on v5

--- a/solution.py
+++ b/solution.py
@@ -12,6 +12,7 @@
 VMEM_LIMIT = 56 * 1024 * 1024
 FWD_ROWS = 1024
 BWD_ROWS = 1024
+BWD_VMEM_LIMIT = 36 * 1024 * 1024
 KIND_ROWS = 16
 PACK = 4
 
@@ -227,7 +228,7 @@
     vmem = pl.BlockSpec(memory_space=pltpu.VMEM)
     common = dict(
         scratch_shapes=[pltpu.VMEM((rows // 2, HEAD_SIZE), jnp.float32)],
-        compiler_params=pltpu.CompilerParams(vmem_limit_bytes=VMEM_LIMIT),
+        compiler_params=pltpu.CompilerParams(vmem_limit_bytes=BWD_VMEM_LIMIT),
         cost_estimate=pl.CostEstimate(
             flops=10 * length * length * HEAD_SIZE,
             bytes_accessed=16 * length * HEAD_SIZE,

time: 250 us -> 250 us (level)
  waiting for transfers between devices: 64.4 us -> 79.3 us
  Pallas kernels: 84.9 us -> 75.5 us
  blocking collectives: 58.7 us -> 52.6 us
    reduce_scatter x1, waiting for transfers between devices: 0.01 us -> 15.4 us  [per_device(): lax.psum_scatter(partial, ('z', 'x'), scatter_dimension=0, tiled=True)]
    all_to_all x1, blocking collectives: 58.7 us -> 52.6 us  [exchange(): return lax.all_to_all(blocks, axis, split_axis=0, concat_axis=0, tiled=True)]
    pallas_call x1, Pallas kernels: 22 us -> 16.9 us  [attend_backward(): pl.pallas_call(functools.partial(bwd_second_kernel, rows=rows), out_shape...]
    pallas_call x1, Pallas kernels: 18.6 us -> 14.3 us  [attend_backward(): pl.pallas_call(functools.partial(bwd_first_kernel, rows=rows), out_shape=...]
  transfers between devices with their start and end apart: 8 -> 8, of which waited for: 2 -> 3; matrix products, arithmetic and copies ran while one was open for 1% -> 1% of each run, Pallas kernels for 34% -> 30%
where the time goes in v6:
time: 250 us; the launch traced here: 249 us
  waiting for transfers between devices  79.3 us (32%)
  Pallas kernels  75.5 us (30%)
  blocking collectives  52.6 us (21%)
  starting transfers between devices  23.6 us (9%)
  between operations  14.1 us (6%)
  local copies, waits for them, and re-layouts  3.4 us (1%)
    all_to_all x1, blocking collectives, exchange(): return lax.all_to_all(blocks, axis, split_axis=0, concat_axis=0, tiled=True)  52.6 us
    all_to_all x2, waiting for transfers between devices, exchange(): return lax.all_to_all(blocks, axis, split_axis=0, concat_axis=0, tiled=True)  50.5 us
    pallas_call x1, Pallas kernels, attend_forward(): pl.pallas_call(functools.partial(fwd_kernel, rows=rows), out_shape=(jax.S...  17.3 us
    pallas_call x1, Pallas kernels, attend_backward(): pl.pallas_call(functools.partial(bwd_second_kernel, rows=rows), out_shape...  16.9 us
    reduce_scatter x1, waiting for transfers between devices, per_device(): lax.psum_scatter(partial, ('z', 'x'), scatter_dimension=0, tiled=True)  15.4 us
    all_to_all x2, starting transfers between devices, exchange(): return lax.all_to_all(blocks, axis, split_axis=0, concat_axis=0, tiled=True)  15.2 us
    pallas_call x1, Pallas kernels, attend_backward(): pl.pallas_call(functools.partial(bwd_first_kernel, rows=rows), out_shape=...  14.3 us
    ppermute x1, waiting for transfers between devices, per_device(): other = lax.ppermute(other, 'yh', partner)  12.7 us
  transfers between devices with their start and end apart: 8, of which 3 were waited for; matrix products, arithmetic and copies ran while one was open for 1% of the time, Pallas kernels for 30%

profile of v6, /device:TPU:0, one launch (start us, length us, event | category | flops | bytes accessed | tf_op | source)
XLA Modules:
  0.0 249.3 jit_solution(10850481093191935694)
XLA Ops:
  7.2 0.0 all-gather.2.cloned.1.call-start
  7.2 0.7 all-gather.2.cloned.1.call-update
  7.9 4.4 %pack_heads.1 = bf16[4,2,4,400,128]{4,3,2,1,0:T(8,128)(2,1)} custom-call(bf16[128,4096]{1,0:T(8,128)(2,1)} %bitcast.20, bf16[128,4096]{1,0:T(8,128)(2,1)} %bitcast.21, bf16[128,4096]{1,0:T(8,128)(2,1)} %bitcast.22, s32[1,128]{1,0:T(1,128)} %kind_ref.1), custom_call_target="tpu_custom_call" | custom-call | tf_op jit(solution)/shard_map/pack_heads/pallas_call | solution.py:278
  12.3 10.9 %all-to-all-start = ((bf16[32,400,128]{2,1,0:T(8,128)(2,1)}), bf16[32,400,128]{2,1,0:T(8,128)(2,1)S(1)}, u32[]{:S(2)}, u32[]{:S(2)}) async-start(bf16[32,400,128]{2,1,0:T(8,128)(2,1)} %bitcast.18), calls=%async_computation | async-start | bytes 6553600 | tf_op jit(solution)/shard_map/all_to_all | solution.py:433
  23.2 1.6 collective-permute-start
  24.8 0.6 pad_add_fusion.me_ref
  25.4 0.0 collective-permute-done
  25.4 50.5 %all-to-all-done.qkv_ref = bf16[32,400,128]{2,1,0:T(8,128)(2,1)S(1)} async-done(((bf16[32,400,128]{2,1,0:T(8,128)(2,1)}), bf16[32,400,128]{2,1,0:T(8,128)(2,1)S(1)}, u32[]{:S(2)}, u32[]{:S(2)}) %all-to-all-start) | async-done | bytes 3276832 | tf_op jit(solution)/shard_map/all_to_all | solution.py:433
  75.9 0.0 copy-start
  75.9 1.2 broadcast_in_dim.15
  77.1 4.3 %all-to-all-start.1 = ((bf16[4,2,32,2048]{3,2,1,0:T(8,128)(2,1)}), bf16[4,2,32,2048]{3,2,1,0:T(8,128)(2,1)}, u32[]{:S(2)}, u32[]{:S(2)}) async-start(bf16[4,2,32,2048]{3,2,1,0:T(8,128)(2,1)} %broadcast_in_dim.15), calls=%async_computation.1 | async-start | bytes 2097152 | tf_op jit(solution)/shard_map/all_to_all | solution.py:433
  81.4 0.0 reduce-scatter.2.cloned.1.call-start
  81.5 0.0 copy-done
  81.5 17.3 %attend_forward.1 = (bf16[32,128,128]{2,1,0:T(8,128)(2,1)}, bf16[16,128,128]{2,1,0:T(8,128)(2,1)}, bf16[16,128,128]{2,1,0:T(8,128)(2,1)}, f32[4,1,1024]{2,1,0:T(1,128)}) custom-call(s32[2]{0:T(128)} %pad_add_fusion.me_ref, bf16[32,400,128]{2,1,0:T(8,128)(2,1)} %copy-done), custom_call_target="tpu_custom_call" | custom-call | flops 25769803776 | bytes 4194304 | tf_op jit(solution)/shard_map/attend_forward/pallas_call | solution.py:111
  98.8 0.0 all-to-all-done.1
  98.8 0.1 collective-permute-start.2
  98.9 3.4 %collective-permute-start.1 = (bf16[16,128,128]{2,1,0:T(8,128)(2,1)}, bf16[16,128,128]{2,1,0:T(8,128)(2,1)S(1)}, u32[]{:S(2)}, u32[]{:S(2)}) collective-permute-start(bf16[16,128,128]{2,1,0:T(8,128)(2,1)} %get-tuple-element.25), channel_id=1, source_target_pairs={{0,4},{4,0},{1,5},{5,1},{2,6},{6,2},{3,7},{7,3},{8,12},{12,8},{9,1... | collective-permute-start | bytes 1572872 | tf_op jit(solution)/shard_map/ppermute | solution.py:454
  102.3 12.7 %collective-permute-done.1.other_ref = bf16[16,128,128]{2,1,0:T(8,128)(2,1)S(1)} collective-permute-done((bf16[16,128,128]{2,1,0:T(8,128)(2,1)}, bf16[16,128,128]{2,1,0:T(8,128)(2,1)S(1)}, u32[]{:S(2)}, u32[]{:S(2)}) %collective-permute-start.1) | collective-permute-done | bytes 524320 | tf_op jit(solution)/shard_map/ppermute | solution.py:454
  115.0 0.0 copy-start.7
  115.0 0.0 collective-permute-done.2.cross_ref
  115.0 0.0 copy-start.6
  115.0 0.8 copy-done.7
  115.8 0.3 copy-done.6
  116.2 9.0 %project.1 = bf16[2048,2048]{1,0:T(8,128)(2,1)} custom-call(s32[2]{0:T(128)} %pad_add_fusion.me_ref, bf16[16,128,128]{2,1,0:T(8,128)(2,1)} %get-tuple-element.22.own_ref, bf16[16,128,128]{2,1,0:T(8,128)(2,1)} %copy-done.7, bf16[4,2,4,400,128]{4,3,2,1,0:T(8,128)(2,1)} %bitcast.14, bf16[2,2,2,32,2048]{4,3,2,1,0:T(8,128)(2,1)} %bitcast.6.same_ref, ...), custom_call_target="tpu_custom_call" | custom-call | flops 4294967296 | bytes 8388608 | tf_op jit(solution)/shard_map/project/pallas_call | solution.py:404
  125.1 0.0 reduce-scatter.2.cloned.1.call-update
  125.1 0.0 copy-start.1
  125.1 0.0 copy-start.2
  125.2 0.0 copy-start.3
  125.2 0.0 all-gather.2.cloned.1.call-done.up_ref
  125.2 0.0 copy-start.5
  125.2 9.3 %project_back.1 = (bf16[16,128,128]{2,1,0:T(8,128)(2,1)}, bf16[16,128,128]{2,1,0:T(8,128)(2,1)}) custom-call(s32[2]{0:T(128)} %pad_add_fusion.me_ref, bf16[16,128,2048]{2,1,0:T(8,128)(2,1)} %all-gather.2.cloned.1.call-done.up_ref, bf16[4,2,4,400,128]{4,3,2,1,0:T(8,128)(2,1)} %bitcast.15, bf16[2,2,2,32,2048]{4,3,2,1,0:T(8,128)(2,1)} %bitcast.6.same_ref, ...), custom_call_target="tpu_custom_call" | custom-call | flops 4294967296 | bytes 8388608 | tf_op jit(solution)/shard_map/project_back/pallas_call | solution.py:358
  134.5 3.3 %collective-permute-start.3 = (bf16[16,128,128]{2,1,0:T(8,128)(2,1)}, bf16[16,128,128]{2,1,0:T(8,128)(2,1)S(1)}, u32[]{:S(2)}, u32[]{:S(2)}) collective-permute-start(bf16[16,128,128]{2,1,0:T(8,128)(2,1)} %get-tuple-element.30), channel_id=1, source_target_pairs={{0,4},{4,0},{1,5},{5,1},{2,6},{6,2},{3,7},{7,3},{8,12},{12,8},{9,1... | collective-permute-start | bytes 1572872 | tf_op jit(solution)/shard_map/ppermute | solution.py:459
  137.7 0.0 copy-done.1
  137.7 0.0 copy-done.2
  137.7 0.0 copy-done.3
  137.7 0.0 copy-done.5
  137.7 0.0 copy-start.4
  137.7 1.0 copy-done.4
  138.8 14.3 %backward_own.1 = (bf16[16,128,128]{2,1,0:T(8,128)(2,1)S(1)}, f32[4096,128]{1,0:T(8,128)S(1)}, f32[4096,128]{1,0:T(8,128)S(1)}) custom-call(s32[2]{0:T(128)S(1)} %copy-done.3, bf16[32,400,128]{2,1,0:T(8,128)(2,1)S(1)} %copy-done.1, bf16[32,128,128]{2,1,0:T(8,128)(2,1)S(1)} %copy-done.5, f32[8,1,512]{2,1,0:T(1,128)S(1)} %bitcast.16, ...), custom_call_target="tpu_custom_call" | custom-call | flops 21474836480 | bytes 8388608 | tf_op jit(solution)/shard_map/backward_own/pallas_call | solution.py:239
  153.1 0.0 collective-permute-done.3.grad_ref
  153.1 16.9 %backward_other.1 = bf16[32,3,128,128]{3,2,1,0:T(8,128)(2,1)S(1)} custom-call(s32[2]{0:T(128)S(1)} %copy-done.3, bf16[32,400,128]{2,1,0:T(8,128)(2,1)S(1)} %copy-done.1, bf16[32,128,128]{2,1,0:T(8,128)(2,1)S(1)} %copy-done.5, f32[8,1,512]{2,1,0:T(1,128)S(1)} %bitcast.17, bf16[16,128,128]{2,1,0:T(8,128)(2,1)S(1)} %collective-permute-done.3.grad_ref, ...), custom_call_target="tpu_custom_call" | custom-call | flops 21474836480 | bytes 8388608 | tf_op jit(solution)/shard_map/backward_other/pallas_call | solution.py:247
  169.9 52.6 %all_to_all.15 = bf16[32,3,128,128]{3,2,1,0:T(8,128)(2,1)} all-to-all(bf16[32,3,128,128]{3,2,1,0:T(8,128)(2,1)S(1)} %backward_other.1), channel_id=1, replica_groups=mesh['low'=2,'core'=2,'z'=4,'yh'=2,'x'=4] {'z','yh','x'}, dimensions={0} | all-to-all | bytes 6291456 | tf_op jit(solution)/shard_map/all_to_all | solution.py:433
  222.6 4.5 %unpack_heads.1 = (bf16[128,4096]{1,0:T(8,128)(2,1)}, bf16[128,4096]{1,0:T(8,128)(2,1)}, bf16[128,4096]{1,0:T(8,128)(2,1)}) custom-call(bf16[4,2,4,3,128,128]{5,4,3,2,1,0:T(8,128)(2,1)} %bitcast.19), custom_call_target="tpu_custom_call" | custom-call | tf_op jit(solution)/shard_map/unpack_heads/pallas_call | solution.py:298
  227.1 15.4 %reduce-scatter.2.cloned.1.call-done = bf16[128,2048]{1,0:T(8,128)(2,1)} async-done(((bf16[2048,2048]{1,0:T(8,128)(2,1)}), bf16[128,2048]{1,0:T(8,128)(2,1)}) %reduce-scatter.2.cloned.1.call-update) | async-done | bytes 524304 | tf_op jit(solution)/shard_map/reduce_scatter | solution.py:456
Async XLA Ops:
  7.2 118.0 %all-gather.2.cloned.1.call-start = ((), (), s32[]{:S(2)}) async-start(), calls=%async_computation.5 | async-start | bytes 8912896 | tf_op jit(solution)/shard_map/all_gather | solution.py:442
  12.3 63.6 %all-to-all-start = ((bf16[32,400,128]{2,1,0:T(8,128)(2,1)}), bf16[32,400,128]{2,1,0:T(8,128)(2,1)S(1)}, u32[]{:S(2)}, u32[]{:S(2)}) async-start(bf16[32,400,128]{2,1,0:T(8,128)(2,1)} %bitcast.18), calls=%async_computation | async-start | bytes 6553600 | tf_op jit(solution)/shard_map/all_to_all | solution.py:433
  23.2 2.2 collective-permute-start
  75.9 5.6 %copy-start = (bf16[32,400,128]{2,1,0:T(8,128)(2,1)}, bf16[32,400,128]{2,1,0:T(8,128)(2,1)S(1)}, u32[]{:S(2)}) copy-start(bf16[32,400,128]{2,1,0:T(8,128)(2,1)S(1)} %all-to-all-done.qkv_ref) | copy-start | bytes 9830404
  77.1 21.7 %all-to-all-start.1 = ((bf16[4,2,32,2048]{3,2,1,0:T(8,128)(2,1)}), bf16[4,2,32,2048]{3,2,1,0:T(8,128)(2,1)}, u32[]{:S(2)}, u32[]{:S(2)}) async-start(bf16[4,2,32,2048]{3,2,1,0:T(8,128)(2,1)} %broadcast_in_dim.15), calls=%async_computation.1 | async-start | bytes 2097152 | tf_op jit(solution)/shard_map/all_to_all | solution.py:433
  81.4 161.0 %reduce-scatter.2.cloned.1.call-start = ((), (), s32[]{:S(2)}) async-start(), calls=%async_computation.4 | async-start | bytes 8912896 | tf_op jit(solution)/shard_map/reduce_scatter | solution.py:456
  98.8 16.2 %collective-permute-start.2 = (bf16[2,2,2,32,2048]{4,3,2,1,0:T(8,128)(2,1)}, bf16[2,2,2,32,2048]{4,3,2,1,0:T(8,128)(2,1)S(1)}, u32[]{:S(2)}, u32[]{:S(2)}) collective-permute-start(bf16[2,2,2,32,2048]{4,3,2,1,0:T(8,128)(2,1)} %bitcast.6.same_ref), channel_id=1, source_target_pairs={{0,32},{32,0},{1,33},{33,1},{2,34},{34,2},{3,35},{35,3},{4,36},{36... | collective-permute-start | bytes 3145736 | tf_op jit(solution)/shard_map/ppermute | solution.py:453
  98.9 16.1 %collective-permute-start.1 = (bf16[16,128,128]{2,1,0:T(8,128)(2,1)}, bf16[16,128,128]{2,1,0:T(8,128)(2,1)S(1)}, u32[]{:S(2)}, u32[]{:S(2)}) collective-permute-start(bf16[16,128,128]{2,1,0:T(8,128)(2,1)} %get-tuple-element.25), channel_id=1, source_target_pairs={{0,4},{4,0},{1,5},{5,1},{2,6},{6,2},{3,7},{7,3},{8,12},{12,8},{9,1... | collective-permute-start | bytes 1572872 | tf_op jit(solution)/shard_map/ppermute | solution.py:454
  115.0 0.8 copy-start.7
  115.0 1.1 copy-start.6
  125.1 12.6 %copy-start.1 = (bf16[32,400,128]{2,1,0:T(8,128)(2,1)S(1)}, bf16[32,400,128]{2,1,0:T(8,128)(2,1)}, u32[]{:S(2)}) copy-start(bf16[32,400,128]{2,1,0:T(8,128)(2,1)} %copy-done) | copy-start | bytes 9830404
  125.1 12.6 %copy-start.2 = (f32[4,1,1024]{2,1,0:T(1,128)S(1)}, f32[4,1,1024]{2,1,0:T(1,128)}, u32[]{:S(2)}) copy-start(f32[4,1,1024]{2,1,0:T(1,128)} %get-tuple-element.28) | copy-start | bytes 49156
  125.2 12.6 %copy-start.3 = (s32[2]{0:T(128)S(1)}, s32[2]{0:T(128)}, u32[]{:S(2)}) copy-start(s32[2]{0:T(128)} %pad_add_fusion.me_ref) | copy-start | bytes 28
  125.2 12.5 %copy-start.5 = (bf16[32,128,128]{2,1,0:T(8,128)(2,1)S(1)}, bf16[32,128,128]{2,1,0:T(8,128)(2,1)}, u32[]{:S(2)}) copy-start(bf16[32,128,128]{2,1,0:T(8,128)(2,1)} %get-tuple-element.27.out_ref) | copy-start | bytes 3145732
  134.5 18.6 %collective-permute-start.3 = (bf16[16,128,128]{2,1,0:T(8,128)(2,1)}, bf16[16,128,128]{2,1,0:T(8,128)(2,1)S(1)}, u32[]{:S(2)}, u32[]{:S(2)}) collective-permute-start(bf16[16,128,128]{2,1,0:T(8,128)(2,1)} %get-tuple-element.30), channel_id=1, source_target_pairs={{0,4},{4,0},{1,5},{5,1},{2,6},{6,2},{3,7},{7,3},{8,12},{12,8},{9,1... | collective-permute-start | bytes 1572872 | tf_op jit(solution)/shard_map/ppermute | solution.py:459
  137.7 1.1 copy-start.4
Sparse Core Ops, SparseCore 0:
  10.1 105.8 all-gather.1
  125.3 117.1 reduce-scatter.1

commit v7 on v6

--- a/solution.py
+++ b/solution.py
@@ -439,10 +439,11 @@
     partner = [(0, 1), (1, 0)]
     swap = [(f * 4 + x, x * 4 + f) for f in range(4) for x in range(4)]
 
-    upstream = lax.all_gather(grad_projected[0], ("z", "x"), axis=0)
     shard = lax.ppermute(out_weight, ("low", "core", "x"), swap)
     shard = jnp.broadcast_to(shard, (4, *shard.shape))
     packed = pack_heads((query_proj[0], key_proj[0], value_proj[0]), modality)
+    packed, upstream = lax.optimization_barrier((packed, grad_projected[0]))
+    upstream = lax.all_gather(upstream, ("z", "x"), axis=0)
     qkv = exchange(packed.reshape(32, *packed.shape[3:]), CTX)
     kinds = qkv.reshape(packed.shape)
     shard, qkv = lax.optimization_barrier((shard, qkv))

time: 250 us -> 247 us (0.988)
  waiting for transfers between devices: 79.3 us -> 76.5 us
  transfers between devices with their start and end apart: 8 -> 8, of which waited for: 3 -> 3; matrix products, arithmetic and copies ran while one was open for 1% -> 1% of each run, Pallas kernels for 30% -> 29%
where the time goes in v7:
time: 247 us
  waiting for transfers between devices  76.5 us (31%)
  Pallas kernels  75.8 us (31%)
  blocking collectives  51.9 us (21%)
  starting transfers between devices  24.3 us (10%)
  between operations  14.1 us (6%)
  local copies, waits for them, and re-layouts  3.41 us (1%)
    all_to_all x1, blocking collectives, exchange(): return lax.all_to_all(blocks, axis, split_axis=0, concat_axis=0, tiled=True)  51.9 us
    all_to_all x2, waiting for transfers between devices, exchange(): return lax.all_to_all(blocks, axis, split_axis=0, concat_axis=0, tiled=True)  48.4 us
    pallas_call x1, Pallas kernels, attend_forward(): pl.pallas_call(functools.partial(fwd_kernel, rows=rows), out_shape=(jax.S...  17.6 us
    pallas_call x1, Pallas kernels, attend_backward(): pl.pallas_call(functools.partial(bwd_second_kernel, rows=rows), out_shape...  16.8 us
    reduce_scatter x1, waiting for transfers between devices, per_device(): lax.psum_scatter(partial, ('z', 'x'), scatter_dimension=0, tiled=True)  15.6 us
    all_to_all x2, starting transfers between devices, exchange(): return lax.all_to_all(blocks, axis, split_axis=0, concat_axis=0, tiled=True)  15.1 us
    pallas_call x1, Pallas kernels, attend_backward(): pl.pallas_call(functools.partial(bwd_first_kernel, rows=rows), out_shape=...  14.3 us
    ppermute x1, waiting for transfers between devices, per_device(): other = lax.ppermute(other, 'yh', partner)  12.4 us
  transfers between devices with their start and end apart: 8, of which 3 were waited for; matrix products, arithmetic and copies ran while one was open for 1% of the time, Pallas kernels for 29%

profile of v7, /device:TPU:0, one launch (start us, length us, event | category | flops | bytes accessed | tf_op | source)
XLA Modules:
  0.0 246.6 jit_solution(17843641076199561164)
XLA Ops:
  7.2 0.0 all-gather.3.cloned.1.call-start
  7.2 4.4 %pack_heads.1 = bf16[4,2,4,400,128]{4,3,2,1,0:T(8,128)(2,1)} custom-call(bf16[128,4096]{1,0:T(8,128)(2,1)} %bitcast.22, bf16[128,4096]{1,0:T(8,128)(2,1)} %bitcast.23, bf16[128,4096]{1,0:T(8,128)(2,1)} %bitcast.24, s32[1,128]{1,0:T(1,128)} %kind_ref.1), custom_call_target="tpu_custom_call" | custom-call | tf_op jit(solution)/shard_map/pack_heads/pallas_call | solution.py:278
  11.6 0.0 all-gather.3.cloned.1.call-update
  11.6 10.9 %all-to-all-start = ((bf16[32,400,128]{2,1,0:T(8,128)(2,1)}), bf16[32,400,128]{2,1,0:T(8,128)(2,1)S(1)}, u32[]{:S(2)}, u32[]{:S(2)}) async-start(bf16[32,400,128]{2,1,0:T(8,128)(2,1)} %bitcast.20), calls=%async_computation | async-start | bytes 6553600 | tf_op jit(solution)/shard_map/all_to_all | solution.py:433
  22.5 1.6 collective-permute-start
  24.1 0.6 pad_add_fusion.me_ref
  24.7 0.0 collective-permute-done
  24.7 48.4 %all-to-all-done.qkv_ref = bf16[32,400,128]{2,1,0:T(8,128)(2,1)S(1)} async-done(((bf16[32,400,128]{2,1,0:T(8,128)(2,1)}), bf16[32,400,128]{2,1,0:T(8,128)(2,1)S(1)}, u32[]{:S(2)}, u32[]{:S(2)}) %all-to-all-start) | async-done | bytes 3276832 | tf_op jit(solution)/shard_map/all_to_all | solution.py:433
  73.2 0.0 copy-start
  73.2 1.2 broadcast_in_dim.15
  74.4 4.2 %all-to-all-start.1 = ((bf16[4,2,32,2048]{3,2,1,0:T(8,128)(2,1)}), bf16[4,2,32,2048]{3,2,1,0:T(8,128)(2,1)}, u32[]{:S(2)}, u32[]{:S(2)}) async-start(bf16[4,2,32,2048]{3,2,1,0:T(8,128)(2,1)} %broadcast_in_dim.15), calls=%async_computation.1 | async-start | bytes 2097152 | tf_op jit(solution)/shard_map/all_to_all | solution.py:433
  78.6 0.0 reduce-scatter.2.cloned.1.call-start
  78.7 0.0 copy-done
  78.7 17.6 %attend_forward.1 = (bf16[32,128,128]{2,1,0:T(8,128)(2,1)}, bf16[16,128,128]{2,1,0:T(8,128)(2,1)}, bf16[16,128,128]{2,1,0:T(8,128)(2,1)}, f32[4,1,1024]{2,1,0:T(1,128)}) custom-call(s32[2]{0:T(128)} %pad_add_fusion.me_ref, bf16[32,400,128]{2,1,0:T(8,128)(2,1)} %copy-done), custom_call_target="tpu_custom_call" | custom-call | flops 25769803776 | bytes 4194304 | tf_op jit(solution)/shard_map/attend_forward/pallas_call | solution.py:111
  96.3 0.0 all-to-all-done.1
  96.3 0.9 collective-permute-start.2
  97.2 3.3 %collective-permute-start.1 = (bf16[16,128,128]{2,1,0:T(8,128)(2,1)}, bf16[16,128,128]{2,1,0:T(8,128)(2,1)S(1)}, u32[]{:S(2)}, u32[]{:S(2)}) collective-permute-start(bf16[16,128,128]{2,1,0:T(8,128)(2,1)} %get-tuple-element.28), channel_id=1, source_target_pairs={{0,4},{4,0},{1,5},{5,1},{2,6},{6,2},{3,7},{7,3},{8,12},{12,8},{9,1... | collective-permute-start | bytes 1572872 | tf_op jit(solution)/shard_map/ppermute | solution.py:455
  100.5 12.4 %collective-permute-done.1.other_ref = bf16[16,128,128]{2,1,0:T(8,128)(2,1)S(1)} collective-permute-done((bf16[16,128,128]{2,1,0:T(8,128)(2,1)}, bf16[16,128,128]{2,1,0:T(8,128)(2,1)S(1)}, u32[]{:S(2)}, u32[]{:S(2)}) %collective-permute-start.1) | collective-permute-done | bytes 524320 | tf_op jit(solution)/shard_map/ppermute | solution.py:455
  112.8 0.0 copy-start.7
  112.8 0.0 collective-permute-done.2.cross_ref
  112.8 0.0 copy-start.6
  112.8 0.8 copy-done.7
  113.6 0.3 copy-done.6
  114.0 9.0 %project.1 = bf16[2048,2048]{1,0:T(8,128)(2,1)} custom-call(s32[2]{0:T(128)} %pad_add_fusion.me_ref, bf16[16,128,128]{2,1,0:T(8,128)(2,1)} %get-tuple-element.25.own_ref, bf16[16,128,128]{2,1,0:T(8,128)(2,1)} %copy-done.7, bf16[4,2,4,400,128]{4,3,2,1,0:T(8,128)(2,1)} %bitcast.16, bf16[2,2,2,32,2048]{4,3,2,1,0:T(8,128)(2,1)} %bitcast.7.same_ref, ...), custom_call_target="tpu_custom_call" | custom-call | flops 4294967296 | bytes 8388608 | tf_op jit(solution)/shard_map/project/pallas_call | solution.py:404
  122.9 0.0 reduce-scatter.2.cloned.1.call-update
  123.0 0.0 all-gather.3.cloned.1.call-done
  123.0 0.0 copy-start.1
  123.0 0.0 copy-start.2
  123.0 0.0 copy-start.3
  123.0 0.0 copy-start.5
  123.0 9.3 %project_back.1 = (bf16[16,128,128]{2,1,0:T(8,128)(2,1)}, bf16[16,128,128]{2,1,0:T(8,128)(2,1)}) custom-call(s32[2]{0:T(128)} %pad_add_fusion.me_ref, bf16[16,128,2048]{2,1,0:T(8,128)(2,1)} %bitcast.26, bf16[4,2,4,400,128]{4,3,2,1,0:T(8,128)(2,1)} %bitcast.17, bf16[2,2,2,32,2048]{4,3,2,1,0:T(8,128)(2,1)} %bitcast.7.same_ref, ...), custom_call_target="tpu_custom_call" | custom-call | flops 4294967296 | bytes 8388608 | tf_op jit(solution)/shard_map/project_back/pallas_call | solution.py:358
  132.3 3.2 %collective-permute-start.3 = (bf16[16,128,128]{2,1,0:T(8,128)(2,1)}, bf16[16,128,128]{2,1,0:T(8,128)(2,1)S(1)}, u32[]{:S(2)}, u32[]{:S(2)}) collective-permute-start(bf16[16,128,128]{2,1,0:T(8,128)(2,1)} %get-tuple-element.34), channel_id=1, source_target_pairs={{0,4},{4,0},{1,5},{5,1},{2,6},{6,2},{3,7},{7,3},{8,12},{12,8},{9,1... | collective-permute-start | bytes 1572872 | tf_op jit(solution)/shard_map/ppermute | solution.py:460
  135.5 0.0 copy-done.1
  135.5 0.0 copy-done.2
  135.5 0.0 copy-done.3
  135.5 0.0 copy-done.5
  135.5 0.0 copy-start.4
  135.6 1.0 copy-done.4
  136.6 14.3 %backward_own.1 = (bf16[16,128,128]{2,1,0:T(8,128)(2,1)S(1)}, f32[4096,128]{1,0:T(8,128)S(1)}, f32[4096,128]{1,0:T(8,128)S(1)}) custom-call(s32[2]{0:T(128)S(1)} %copy-done.3, bf16[32,400,128]{2,1,0:T(8,128)(2,1)S(1)} %copy-done.1, bf16[32,128,128]{2,1,0:T(8,128)(2,1)S(1)} %copy-done.5, f32[8,1,512]{2,1,0:T(1,128)S(1)} %bitcast.18, ...), custom_call_target="tpu_custom_call" | custom-call | flops 21474836480 | bytes 8388608 | tf_op jit(solution)/shard_map/backward_own/pallas_call | solution.py:239
  150.9 0.0 collective-permute-done.3.grad_ref
  150.9 16.8 %backward_other.1 = bf16[32,3,128,128]{3,2,1,0:T(8,128)(2,1)S(1)} custom-call(s32[2]{0:T(128)S(1)} %copy-done.3, bf16[32,400,128]{2,1,0:T(8,128)(2,1)S(1)} %copy-done.1, bf16[32,128,128]{2,1,0:T(8,128)(2,1)S(1)} %copy-done.5, f32[8,1,512]{2,1,0:T(1,128)S(1)} %bitcast.19, bf16[16,128,128]{2,1,0:T(8,128)(2,1)S(1)} %collective-permute-done.3.grad_ref, ...), custom_call_target="tpu_custom_call" | custom-call | flops 21474836480 | bytes 8388608 | tf_op jit(solution)/shard_map/backward_other/pallas_call | solution.py:247
  167.8 51.9 %all_to_all.15 = bf16[32,3,128,128]{3,2,1,0:T(8,128)(2,1)} all-to-all(bf16[32,3,128,128]{3,2,1,0:T(8,128)(2,1)S(1)} %backward_other.1), channel_id=1, replica_groups=mesh['low'=2,'core'=2,'z'=4,'yh'=2,'x'=4] {'z','yh','x'}, dimensions={0} | all-to-all | bytes 6291456 | tf_op jit(solution)/shard_map/all_to_all | solution.py:433
  219.7 4.5 %unpack_heads.1 = (bf16[128,4096]{1,0:T(8,128)(2,1)}, bf16[128,4096]{1,0:T(8,128)(2,1)}, bf16[128,4096]{1,0:T(8,128)(2,1)}) custom-call(bf16[4,2,4,3,128,128]{5,4,3,2,1,0:T(8,128)(2,1)} %bitcast.21), custom_call_target="tpu_custom_call" | custom-call | tf_op jit(solution)/shard_map/unpack_heads/pallas_call | solution.py:298
  224.2 15.6 %reduce-scatter.2.cloned.1.call-done = bf16[128,2048]{1,0:T(8,128)(2,1)} async-done(((bf16[2048,2048]{1,0:T(8,128)(2,1)}), bf16[128,2048]{1,0:T(8,128)(2,1)}) %reduce-scatter.2.cloned.1.call-update) | async-done | bytes 524304 | tf_op jit(solution)/shard_map/reduce_scatter | solution.py:457
Async XLA Ops:
  7.2 115.8 %all-gather.3.cloned.1.call-start = ((), (), s32[]{:S(2)}) async-start(), calls=%async_computation.5 | async-start | bytes 8912896 | tf_op jit(solution)/shard_map/all_gather | solution.py:446
  11.6 61.6 %all-to-all-start = ((bf16[32,400,128]{2,1,0:T(8,128)(2,1)}), bf16[32,400,128]{2,1,0:T(8,128)(2,1)S(1)}, u32[]{:S(2)}, u32[]{:S(2)}) async-start(bf16[32,400,128]{2,1,0:T(8,128)(2,1)} %bitcast.20), calls=%async_computation | async-start | bytes 6553600 | tf_op jit(solution)/shard_map/all_to_all | solution.py:433
  22.5 2.2 collective-permute-start
  73.2 5.5 %copy-start = (bf16[32,400,128]{2,1,0:T(8,128)(2,1)}, bf16[32,400,128]{2,1,0:T(8,128)(2,1)S(1)}, u32[]{:S(2)}) copy-start(bf16[32,400,128]{2,1,0:T(8,128)(2,1)S(1)} %all-to-all-done.qkv_ref) | copy-start | bytes 9830404
  74.4 21.9 %all-to-all-start.1 = ((bf16[4,2,32,2048]{3,2,1,0:T(8,128)(2,1)}), bf16[4,2,32,2048]{3,2,1,0:T(8,128)(2,1)}, u32[]{:S(2)}, u32[]{:S(2)}) async-start(bf16[4,2,32,2048]{3,2,1,0:T(8,128)(2,1)} %broadcast_in_dim.15), calls=%async_computation.1 | async-start | bytes 2097152 | tf_op jit(solution)/shard_map/all_to_all | solution.py:433
  78.6 161.1 %reduce-scatter.2.cloned.1.call-start = ((), (), s32[]{:S(2)}) async-start(), calls=%async_computation.4 | async-start | bytes 8912896 | tf_op jit(solution)/shard_map/reduce_scatter | solution.py:457
  96.3 16.6 %collective-permute-start.2 = (bf16[2,2,2,32,2048]{4,3,2,1,0:T(8,128)(2,1)}, bf16[2,2,2,32,2048]{4,3,2,1,0:T(8,128)(2,1)S(1)}, u32[]{:S(2)}, u32[]{:S(2)}) collective-permute-start(bf16[2,2,2,32,2048]{4,3,2,1,0:T(8,128)(2,1)} %bitcast.7.same_ref), channel_id=1, source_target_pairs={{0,32},{32,0},{1,33},{33,1},{2,34},{34,2},{3,35},{35,3},{4,36},{36... | collective-permute-start | bytes 3145736 | tf_op jit(solution)/shard_map/ppermute | solution.py:454
  97.2 15.6 %collective-permute-start.1 = (bf16[16,128,128]{2,1,0:T(8,128)(2,1)}, bf16[16,128,128]{2,1,0:T(8,128)(2,1)S(1)}, u32[]{:S(2)}, u32[]{:S(2)}) collective-permute-start(bf16[16,128,128]{2,1,0:T(8,128)(2,1)} %get-tuple-element.28), channel_id=1, source_target_pairs={{0,4},{4,0},{1,5},{5,1},{2,6},{6,2},{3,7},{7,3},{8,12},{12,8},{9,1... | collective-permute-start | bytes 1572872 | tf_op jit(solution)/shard_map/ppermute | solution.py:455
  112.8 0.8 copy-start.7
  112.8 1.1 copy-start.6
  123.0 12.5 %copy-start.1 = (bf16[32,400,128]{2,1,0:T(8,128)(2,1)S(1)}, bf16[32,400,128]{2,1,0:T(8,128)(2,1)}, u32[]{:S(2)}) copy-start(bf16[32,400,128]{2,1,0:T(8,128)(2,1)} %copy-done) | copy-start | bytes 9830404
  123.0 12.5 %copy-start.2 = (f32[4,1,1024]{2,1,0:T(1,128)S(1)}, f32[4,1,1024]{2,1,0:T(1,128)}, u32[]{:S(2)}) copy-start(f32[4,1,1024]{2,1,0:T(1,128)} %get-tuple-element.31) | copy-start | bytes 49156
  123.0 12.5 %copy-start.3 = (s32[2]{0:T(128)S(1)}, s32[2]{0:T(128)}, u32[]{:S(2)}) copy-start(s32[2]{0:T(128)} %pad_add_fusion.me_ref) | copy-start | bytes 28
  123.0 12.5 %copy-start.5 = (bf16[32,128,128]{2,1,0:T(8,128)(2,1)S(1)}, bf16[32,128,128]{2,1,0:T(8,128)(2,1)}, u32[]{:S(2)}) copy-start(bf16[32,128,128]{2,1,0:T(8,128)(2,1)} %get-tuple-element.30.out_ref) | copy-start | bytes 3145732
  132.3 18.6 %collective-permute-start.3 = (bf16[16,128,128]{2,1,0:T(8,128)(2,1)}, bf16[16,128,128]{2,1,0:T(8,128)(2,1)S(1)}, u32[]{:S(2)}, u32[]{:S(2)}) collective-permute-start(bf16[16,128,128]{2,1,0:T(8,128)(2,1)} %get-tuple-element.34), channel_id=1, source_target_pairs={{0,4},{4,0},{1,5},{5,1},{2,6},{6,2},{3,7},{7,3},{8,12},{12,8},{9,1... | collective-permute-start | bytes 1572872 | tf_op jit(solution)/shard_map/ppermute | solution.py:460
  135.5 1.1 copy-start.4
Sparse Core Ops, SparseCore 0:
  11.7 104.2 all-gather.2
  123.1 116.6 reduce-scatter.1
